TPU v7x, 32 devices: a whole 2x2x4 slice. The times are simulated.
32 devices in a mesh: batch: 8 (over z, x), ctx: 4 (over y, core).
Axes of the slice: x: 2, y: 2, z: 4, core: 2. Of those that a mesh axis runs over, the one named last changes fastest.
Arguments:
- tokens: bfloat16 [8, 1024, 2048], P('batch', 'ctx'), may hold values from -6 to 6
- segment_ids: int32 [8, 1024], P('batch', 'ctx'), may hold values from 0 to 7, never falling along the last dimension, each value on 1 to 512 neighbouring positions
- valid_mask: int32 [8, 1024], P('batch', 'ctx'), may hold values from 0 to 1, as said below
- teacher: bfloat16 [8, 1024, 2048], P('batch', 'ctx'), may hold values from -6 to 6
- mixer_in: bfloat16 [2048, 6704], P(('batch', 'ctx')), may hold values from -0.125 to 0.125
- mixer_out: bfloat16 [3072, 2048], P(('batch', 'ctx')), may hold values from -0.0012207031 to 0.0012207031
- query_weight: bfloat16 [2048, 1024], P(('batch', 'ctx')), may hold values from -0.125 to 0.125
- key_value_weight: bfloat16 [2048, 512], P(('batch', 'ctx')), may hold values from -0.125 to 0.125
- output_weight: bfloat16 [1024, 2048], P(('batch', 'ctx')), may hold values from -1.5 to 1.5
- gate_up: bfloat16 [2048, 8192], P(('batch', 'ctx')), may hold values from -0.125 to 0.125
- down_weight: bfloat16 [4096, 2048], P(('batch', 'ctx')), may hold values from -0.09375 to 0.09375
- norm_first: float32 [2048], replicated, may hold values from 0.5 to 1.5
- norm_second: float32 [2048], replicated, may hold values from 0.5 to 1.5
- conv_taps: float32 [4, 3584], replicated, may hold values from -3 to 3
- decay_log: float32 [48], replicated, may hold values from -7.6 to -3
- skip_gain: float32 [48], replicated, may hold values from 0.5 to 1.5
- step_bias: float32 [48], replicated, may hold values from -2 to 0.5
Outputs:
- output: bfloat16 [8, 1024, 2048], P('batch', 'ctx')
- loss_value: float32 [], replicated
- grad_tokens: float32 [8, 1024, 2048], P('batch', 'ctx')
- grad_mixer_in: float32 [2048, 6704], P(('batch', 'ctx'))
- grad_mixer_out: float32 [3072, 2048], P(('batch', 'ctx'))
- grad_query_weight: float32 [2048, 1024], P(('batch', 'ctx'))
- grad_keyval_weight: float32 [2048, 512], P(('batch', 'ctx'))
- grad_output_weight: float32 [1024, 2048], P(('batch', 'ctx'))
- grad_gate_up: float32 [2048, 8192], P(('batch', 'ctx'))
- grad_down_weight: float32 [4096, 2048], P(('batch', 'ctx'))
- grad_norm_first: float32 [2048], replicated
- grad_norm_second: float32 [2048], replicated
- grad_conv_taps: float32 [4, 3584], replicated
- grad_decay_log: float32 [48], replicated
- grad_skip_gain: float32 [48], replicated
- grad_step_bias: float32 [48], replicated
Inputs may be any that keep to these rules, and one draw needn't show every extreme that they name: `segment_ids`: within a sequence the ids never fall; each document is 1 to 512 tokens long and one is exactly that long. `valid_mask`: the share of ones rises from about 0.3 in the first sequence to about 0.95 in the last.
All inputs are finite; a program needn't handle non-finite values.
Results may differ from a plain program's by a relative error of at most 0.012.
Values may be sent and summed in bfloat16 or wider, within the bound.
No kernel may reach another device: no remote copies, remote signals or barrier semaphores. Data moves between devices by JAX's collectives and lax.ppermute only.
A program may use at most 448 MiB of HBM per device.

v0:
```python
import jax
import jax.numpy as jnp
from jax import lax
from jax.sharding import PartitionSpec as P

MODEL_WIDTH = 2048
H_M = 48
P_SIZE = 64
N = 256
QUERY_HEADS = 8
KEY_VALUE_HEADS = 2
HEAD_SIZE = 128
FF = 4096
TAPS = 4
DI = 3072


NORM_EPSILON = 1e-05
ROPE_BASE = 1000000.0
HIGHEST = lax.Precision.HIGHEST


def passed_along(shard, axis, by):
    count = lax.axis_size(axis)
    pairs = [(i, i + by) for i in range(count) if 0 <= i + by < count]
    return lax.ppermute(shard, axis, pairs)


def entering(part, axis, combine, identity, reverse):
    count = lax.axis_size(axis)
    place = lax.axis_index(axis)
    ahead = count - 1 - place if reverse else place
    gathered = jax.tree.map(lambda a: lax.all_gather(a, axis), part)
    state = jax.tree.map(lambda a, e: jnp.zeros_like(a) + jnp.asarray(e, a.dtype), part, identity)

    def one(step, state):
        source = count - 1 - step if reverse else step
        return combine(
            state, jax.tree.map(lambda a: lax.dynamic_index_in_dim(a, source, 0, False), gathered)
        )

    return lax.fori_loop(0, ahead, one, state)


def rms_norm(value_rows, gain):
    return (
        value_rows
        * lax.rsqrt(jnp.mean(value_rows * value_rows, axis=-1, keepdims=True) + NORM_EPSILON)
        * gain
    )


def apply_rotary(heads, token_position):
    half = HEAD_SIZE // 2
    inverse = ROPE_BASE ** (-(jnp.arange(half, dtype=jnp.float32) * 2.0) / HEAD_SIZE)
    angle = token_position.astype(jnp.float32)[:, None] * inverse[None, :]
    cosine = jnp.cos(angle)[:, None, :]
    sine = jnp.sin(angle)[:, None, :]
    leading_part = heads[..., :half]
    second = heads[..., half:]
    return jnp.concatenate(
        [leading_part * cosine - second * sine, second * cosine + leading_part * sine], axis=-1
    )


def conv_segments(padded, padded_segs, segments, taps):
    count_rows = segments.shape[0]
    total = jnp.zeros((count_rows, padded.shape[1]), jnp.float32)
    for lag in range(TAPS):
        begin = TAPS - 1 - lag
        shifted = padded[begin : begin + count_rows]
        keep = (padded_segs[begin : begin + count_rows] == segments).astype(jnp.float32)[:, None]
        total = total + taps[lag] * shifted * keep
    return total


def ssd_states(xs, bmat, decay, step, segments, seg_before):
    cumulative = jnp.cumsum(decay, axis=0)
    weight = (
        jnp.exp(cumulative[-1][None, :] - cumulative)
        * (segments == segments[-1]).astype(jnp.float32)[:, None]
        * step
    )
    tail_state = jnp.einsum("shp,sn->hpn", weight[:, :, None] * xs, bmat, precision=HIGHEST)
    through = jnp.exp(cumulative[-1]) * (segments[-1] == seg_before).astype(jnp.float32)
    return (tail_state, through)


def ssd_output(xs, bmat, cmat, decay, step, segments, seg_before, state_in):
    count_rows = xs.shape[0]
    cumulative = jnp.cumsum(decay, axis=0)
    order = jnp.arange(count_rows)
    allowed = (segments[:, None] == segments[None, :]) & (order[:, None] >= order[None, :])
    spread = cumulative.T[:, :, None] - cumulative.T[:, None, :]
    kernel = jnp.exp(jnp.where(allowed[None], spread, -1e30))
    inner = jnp.dot(cmat, bmat.T, precision=HIGHEST, preferred_element_type=jnp.float32)
    mixing = kernel * inner[None] * step.T[:, None, :]
    local = jnp.einsum("hts,shp->thp", mixing, xs, precision=HIGHEST)
    carried = jnp.einsum("hpn,tn->thp", state_in, cmat, precision=HIGHEST)
    keep = (segments == seg_before).astype(jnp.float32)
    return local + (jnp.exp(cumulative) * keep[:, None])[:, :, None] * carried


def combine(earlier, later):
    return (earlier[0] * later[0], later[1] + later[0][:, None, None] * earlier[1])


def product(left, right):
    return jnp.dot(left, right, preferred_element_type=jnp.float32)


def outer_rows(left, right):
    return lax.dot_general(
        left, right, (((0,), (0,)), ((), ())), preferred_element_type=jnp.float32
    )


def compared_with(left, right):
    return lax.dot_general(
        left, right, (((1,), (1,)), ((), ())), preferred_element_type=jnp.float32
    )


def body(
    tokens,
    segment_ids,
    valid_mask,
    teacher,
    mixer_in,
    mixer_out,
    query_weight,
    key_value_weight,
    output_weight,
    gate_up,
    down_weight,
    norm_first,
    norm_second,
    conv_taps,
    decay_log,
    skip_gain,
    step_bias,
):
    span_length = tokens.shape[0] * tokens.shape[1]
    residual_in = tokens.reshape(span_length, MODEL_WIDTH).astype(jnp.float32)
    segments = segment_ids.reshape(span_length)
    valid_rows = valid_mask.reshape(span_length).astype(jnp.float32)
    target = teacher.reshape(span_length, MODEL_WIDTH).astype(jnp.float32)
    ctx_index = lax.axis_index("ctx")
    offset = ctx_index * span_length
    token_position = offset + jnp.arange(span_length, dtype=jnp.int32)
    batch_count = lax.axis_size("batch")
    ctx_count = lax.axis_size("ctx")
    devices = batch_count * ctx_count
    total_tokens = float(span_length * devices)
    complete_length = span_length * ctx_count
    query_per_group = QUERY_HEADS // KEY_VALUE_HEADS
    channels = DI + 2 * N
    scale = HEAD_SIZE ** (-0.5)
    in_full, out_full, query_full, keyval_full, complete_output, gate_full, down_full = (
        lax.all_gather(mixer_in, ("batch", "ctx"), axis=0, tiled=True),
        lax.all_gather(mixer_out, ("batch", "ctx"), axis=0, tiled=True),
        lax.all_gather(query_weight, ("batch", "ctx"), axis=0, tiled=True),
        lax.all_gather(key_value_weight, ("batch", "ctx"), axis=0, tiled=True),
        lax.all_gather(output_weight, ("batch", "ctx"), axis=0, tiled=True),
        lax.all_gather(gate_up, ("batch", "ctx"), axis=0, tiled=True),
        lax.all_gather(down_weight, ("batch", "ctx"), axis=0, tiled=True),
    )
    normed_wide, norm_pull_one = jax.vjp(rms_norm, residual_in, norm_first)
    normed = normed_wide.astype(jnp.bfloat16)
    mixed = product(normed, in_full)
    gate_z = mixed[:, :DI]
    conv_in = mixed[:, DI : DI + channels].astype(jnp.bfloat16)
    step_raw = mixed[:, DI + channels :]
    query_raw = product(normed, query_full).reshape(span_length, QUERY_HEADS, HEAD_SIZE)
    key_value_projected = product(normed, keyval_full)
    unrotated_key = key_value_projected[:, : KEY_VALUE_HEADS * HEAD_SIZE].reshape(
        span_length, KEY_VALUE_HEADS, HEAD_SIZE
    )
    query_rows = apply_rotary(query_raw, token_position).astype(jnp.bfloat16)
    key_rows = (
        apply_rotary(unrotated_key, token_position)
        .astype(jnp.bfloat16)
        .reshape(span_length, KEY_VALUE_HEADS * HEAD_SIZE)
    )
    value_rows = key_value_projected[:, KEY_VALUE_HEADS * HEAD_SIZE :].astype(jnp.bfloat16)
    every_key_row, every_value_row, segs_wire = (
        lax.all_gather(key_rows, "ctx", axis=0, tiled=True),
        lax.all_gather(value_rows, "ctx", axis=0, tiled=True),
        lax.all_gather(segments.astype(jnp.bfloat16), "ctx", axis=0, tiled=True),
    )
    segs_all = segs_wire.astype(jnp.int32)
    rim = passed_along(conv_in[span_length - (TAPS - 1) :], "ctx", 1)
    rim_segs = lax.dynamic_slice_in_dim(segs_all, jnp.maximum(offset - (TAPS - 1), 0), TAPS - 1)
    seg_before = jnp.where(ctx_index > 0, segs_all[jnp.maximum(offset - 1, 0)], -1)
    padded_segs = jnp.concatenate([rim_segs, segments])
    padded_in = jnp.concatenate([rim, conv_in], axis=0).astype(jnp.float32)

    def conv_act(padded, taps):
        return jax.nn.silu(conv_segments(padded, padded_segs, segments, taps))

    activated, conv_pull = jax.vjp(conv_act, padded_in, conv_taps)
    xs = activated[:, :DI].reshape(span_length, H_M, P_SIZE)
    bmat = activated[:, DI : DI + N]
    cmat = activated[:, DI + N :]

    def step_rule(raw, bias, logs):
        step = jax.nn.softplus(raw + bias)
        return (step, -jnp.exp(logs) * step)

    (step, decay), step_pull = jax.vjp(step_rule, step_raw, step_bias, decay_log)

    def states_rule(xs_value, b_value, decay_value, step_value):
        return ssd_states(xs_value, b_value, decay_value, step_value, segments, seg_before)

    (tail_state, through), states_pull = jax.vjp(states_rule, xs, bmat, decay, step)
    identity = (jnp.ones((H_M,), jnp.float32), jnp.zeros((H_M, P_SIZE, N), jnp.float32))
    carried_in = entering((through, tail_state), "ctx", combine, identity, False)[1]

    def output_rule(xs_value, b_value, c_value, decay_value, step_value, state_value, skip_value):
        return (
            ssd_output(
                xs_value,
                b_value,
                c_value,
                decay_value,
                step_value,
                segments,
                seg_before,
                state_value,
            )
            + skip_value[:, None] * xs_value
        )

    ssm_y, output_pull = jax.vjp(output_rule, xs, bmat, cmat, decay, step, carried_in, skip_gain)

    def gate_rule(y_value, z_value):
        return y_value.reshape(span_length, DI) * jax.nn.silu(z_value)

    gated_wide, gate_pull = jax.vjp(gate_rule, ssm_y, gate_z)
    gated = gated_wide.astype(jnp.bfloat16)
    mixer_branch = product(gated, out_full)
    head_grouped = query_rows.reshape(span_length, KEY_VALUE_HEADS, query_per_group, HEAD_SIZE)
    key_per_head = every_key_row.reshape(complete_length, KEY_VALUE_HEADS, HEAD_SIZE)
    value_per_head = every_value_row.reshape(complete_length, KEY_VALUE_HEADS, HEAD_SIZE)
    allowed = (token_position[:, None] >= jnp.arange(complete_length, dtype=jnp.int32)[None, :]) & (
        segments[:, None] == segs_all[None, :]
    )

    def score_rule():
        raw = (
            jnp.einsum(
                "tkgd,skd->kgts", head_grouped, key_per_head, preferred_element_type=jnp.float32
            )
            * scale
        )
        return jnp.where(allowed, raw, -1e30)

    scores = score_rule()
    top = jnp.max(scores, axis=-1, keepdims=True)
    log_total = top + jnp.log(jnp.sum(jnp.exp(scores - top), axis=-1, keepdims=True))
    probs = jnp.exp(scores - log_total)
    attended = (
        jnp.einsum(
            "kgts,skd->tkgd",
            probs.astype(jnp.bfloat16),
            value_per_head,
            preferred_element_type=jnp.float32,
        )
        .reshape(span_length, QUERY_HEADS * HEAD_SIZE)
        .astype(jnp.bfloat16)
    )
    attend_branch = product(attended, complete_output)
    hidden_one = residual_in + mixer_branch + attend_branch
    normed_two_wide, norm_pull_two = jax.vjp(rms_norm, hidden_one, norm_second)
    normed_two = normed_two_wide.astype(jnp.bfloat16)
    gateup = product(normed_two, gate_full)

    def swiglu(values_in):
        return jax.nn.silu(values_in[:, :FF]) * values_in[:, FF:]

    hidden_wide, swiglu_pull = jax.vjp(swiglu, gateup)
    hidden = hidden_wide.astype(jnp.bfloat16)
    ffn_branch = product(hidden, down_full)
    final = hidden_one + ffn_branch
    error = final - target
    squares = jnp.sum(valid_rows * jnp.sum(error * error, axis=1))
    total_squares, count = lax.psum((squares, jnp.sum(valid_rows)), ("batch", "ctx"))
    loss_value = total_squares / (MODEL_WIDTH * count)
    grad_final = valid_rows[:, None] * error * (total_tokens / count)
    in_full, out_full, query_full, keyval_full, complete_output, gate_full, down_full = (
        lax.all_gather(mixer_in, ("batch", "ctx"), axis=0, tiled=True),
        lax.all_gather(mixer_out, ("batch", "ctx"), axis=0, tiled=True),
        lax.all_gather(query_weight, ("batch", "ctx"), axis=0, tiled=True),
        lax.all_gather(key_value_weight, ("batch", "ctx"), axis=0, tiled=True),
        lax.all_gather(output_weight, ("batch", "ctx"), axis=0, tiled=True),
        lax.all_gather(gate_up, ("batch", "ctx"), axis=0, tiled=True),
        lax.all_gather(down_weight, ("batch", "ctx"), axis=0, tiled=True),
    )
    grad_ffn = grad_final.astype(jnp.bfloat16)
    grad_hidden = compared_with(grad_ffn, down_full)
    grad_gateup = swiglu_pull(grad_hidden)[0].astype(jnp.bfloat16)
    grad_normed_two = compared_with(grad_gateup, gate_full)
    grad_hidden_one, grad_norm_second = norm_pull_two(grad_normed_two)
    grad_hidden_one = grad_hidden_one + grad_final
    branch_gradient = grad_hidden_one.astype(jnp.bfloat16)
    grad_attended = (
        compared_with(branch_gradient, complete_output)
        .astype(jnp.bfloat16)
        .reshape(span_length, KEY_VALUE_HEADS, query_per_group, HEAD_SIZE)
    )
    scores = score_rule()
    probs = jnp.exp(scores - log_total)
    grad_probs = jnp.einsum(
        "tkgd,skd->kgts", grad_attended, value_per_head, preferred_element_type=jnp.float32
    )
    inner_sum = jnp.sum(probs * grad_probs, axis=-1, keepdims=True)
    grad_scores = (probs * (grad_probs - inner_sum)).astype(jnp.bfloat16)
    grad_queries = (
        jnp.einsum("kgts,skd->tkgd", grad_scores, key_per_head, preferred_element_type=jnp.float32)
        * scale
    )
    every_key_gradient = (
        jnp.einsum("kgts,tkgd->skd", grad_scores, head_grouped, preferred_element_type=jnp.float32)
        * scale
    )
    every_value_gradient = jnp.einsum(
        "kgts,tkgd->skd",
        probs.astype(jnp.bfloat16),
        grad_attended,
        preferred_element_type=jnp.float32,
    )
    key_gradient_rows, value_gradient_rows = (
        lax.psum_scatter(
            every_key_gradient.reshape(complete_length, KEY_VALUE_HEADS * HEAD_SIZE),
            "ctx",
            scatter_dimension=0,
            tiled=True,
        ),
        lax.psum_scatter(
            every_value_gradient.reshape(complete_length, KEY_VALUE_HEADS * HEAD_SIZE),
            "ctx",
            scatter_dimension=0,
            tiled=True,
        ),
    )

    def turn(heads):
        return apply_rotary(heads, token_position)

    grad_query_raw = jax.vjp(turn, query_raw)[1](
        grad_queries.reshape(span_length, QUERY_HEADS, HEAD_SIZE)
    )[0]
    raw_key_gradient = jax.vjp(turn, unrotated_key)[1](
        key_gradient_rows.reshape(span_length, KEY_VALUE_HEADS, HEAD_SIZE)
    )[0]
    grad_query_low = grad_query_raw.reshape(span_length, QUERY_HEADS * HEAD_SIZE).astype(
        jnp.bfloat16
    )
    grad_keyval = jnp.concatenate(
        [raw_key_gradient.reshape(span_length, KEY_VALUE_HEADS * HEAD_SIZE), value_gradient_rows],
        axis=1,
    ).astype(jnp.bfloat16)
    grad_gated = compared_with(branch_gradient, out_full)
    grad_ssm_y, grad_gate_z = gate_pull(grad_gated)
    grad_xs_out, grad_b_out, grad_cmat, grad_decay_out, grad_step_out, grad_carried, grad_skip = (
        output_pull(grad_ssm_y)
    )
    grad_later = entering((through, grad_carried), "ctx", combine, identity, True)[1]
    grad_through = jnp.sum(grad_later * carried_in, axis=(1, 2))
    grad_xs_state, grad_b_state, grad_decay_state, grad_step_state = states_pull(
        (grad_later, grad_through)
    )
    grad_step_raw, grad_step_bias, grad_decay_log = step_pull(
        (grad_step_out + grad_step_state, grad_decay_out + grad_decay_state)
    )
    grad_activated = jnp.concatenate(
        [
            (grad_xs_out + grad_xs_state).reshape(span_length, DI),
            grad_b_out + grad_b_state,
            grad_cmat,
        ],
        axis=1,
    )
    grad_padded, grad_conv_taps = conv_pull(grad_activated)
    grad_rim = passed_along(grad_padded[: TAPS - 1], "ctx", -1)
    grad_conv_in = grad_padded[TAPS - 1 :] + jnp.concatenate(
        [jnp.zeros((span_length - (TAPS - 1), channels), jnp.float32), grad_rim], axis=0
    )
    grad_mixed = jnp.concatenate([grad_gate_z, grad_conv_in, grad_step_raw], axis=1).astype(
        jnp.bfloat16
    )
    grad_normed = (
        compared_with(grad_mixed, in_full)
        + compared_with(grad_query_low, query_full)
        + compared_with(grad_keyval, keyval_full)
    )
    grad_residual, grad_norm_first = norm_pull_one(grad_normed)
    grad_tokens = grad_residual + grad_hidden_one
    weight_grads = (
        lax.psum_scatter(
            outer_rows(normed, grad_mixed), ("batch", "ctx"), scatter_dimension=0, tiled=True
        ),
        lax.psum_scatter(
            outer_rows(gated, branch_gradient), ("batch", "ctx"), scatter_dimension=0, tiled=True
        ),
        lax.psum_scatter(
            outer_rows(normed, grad_query_low), ("batch", "ctx"), scatter_dimension=0, tiled=True
        ),
        lax.psum_scatter(
            outer_rows(normed, grad_keyval), ("batch", "ctx"), scatter_dimension=0, tiled=True
        ),
        lax.psum_scatter(
            outer_rows(attended, branch_gradient), ("batch", "ctx"), scatter_dimension=0, tiled=True
        ),
        lax.psum_scatter(
            outer_rows(normed_two, grad_gateup), ("batch", "ctx"), scatter_dimension=0, tiled=True
        ),
        lax.psum_scatter(
            outer_rows(hidden, grad_ffn), ("batch", "ctx"), scatter_dimension=0, tiled=True
        ),
    )
    small = lax.psum(
        (
            grad_norm_first,
            grad_norm_second,
            grad_conv_taps,
            grad_decay_log,
            grad_skip,
            grad_step_bias,
        ),
        ("batch", "ctx"),
    )
    output = final.astype(jnp.bfloat16).reshape(tokens.shape)
    return (
        output,
        loss_value,
        grad_tokens.reshape(tokens.shape),
        weight_grads[0],
        weight_grads[1],
        weight_grads[2],
        weight_grads[3],
        weight_grads[4],
        weight_grads[5],
        weight_grads[6],
        small[0],
        small[1],
        small[2],
        small[3],
        small[4],
        small[5],
    )


def solution(mesh):
    placed = (
        P("batch", "ctx", None),
        P("batch", "ctx"),
        P("batch", "ctx"),
        P("batch", "ctx", None),
        P(("batch", "ctx"), None),
        P(("batch", "ctx"), None),
        P(("batch", "ctx"), None),
        P(("batch", "ctx"), None),
        P(("batch", "ctx"), None),
        P(("batch", "ctx"), None),
        P(("batch", "ctx"), None),
        P(),
        P(),
        P(),
        P(),
        P(),
        P(),
    )
    return jax.shard_map(
        body,
        mesh=mesh,
        in_specs=placed,
        out_specs=(
            P("batch", "ctx", None),
            P(),
            P("batch", "ctx", None),
            P(("batch", "ctx"), None),
            P(("batch", "ctx"), None),
            P(("batch", "ctx"), None),
            P(("batch", "ctx"), None),
            P(("batch", "ctx"), None),
            P(("batch", "ctx"), None),
            P(("batch", "ctx"), None),
            P(),
            P(),
            P(),
            P(),
            P(),
            P(),
        ),
        check_vma=False,
    )
```

profile of v0, /device:TPU:0, one launch (start us, length us, event | category | flops | bytes accessed | tf_op | source)
XLA Modules:
  0.0 3411.4 jit_solution(18216927619666801808)
XLA Ops:
  11.4 6.0 all-gather.2
  25.1 155.7 %all-gather.14.cloned.1.call-done = bf16[2048,6704]{1,0:T(8,128)(2,1)} async-done(((bf16[64,6704]{1,0:T(8,128)(2,1)}), bf16[2048,6704]{1,0:T(8,128)(2,1)}) %all-gather.14.cloned.1.call-update) | async-done | bytes 27459600 | tf_op jit(solution)/shard_map/all_gather | solution.py:160
  180.9 17.5 fusion.158
  211.0 6.8 fusion.31
  228.6 38.8 %psum.57 = f32[]{:T(128)} all-reduce(f32[]{:T(128)} %convert_reduce_fusion), channel_id=1, replica_groups=mesh['batch'=8,'ctx'=4] {'batch','ctx'}, use_global_device_ids=true, to_apply=%region_12.13 | all-reduce | flops 1 | bytes 8 | tf_op jit(solution)/shard_map/psum | solution.py:287
  272.2 8.1 all_gather.62
  281.7 10.1 all_gather.63
  291.8 11.9 all-gather.20.cloned.1.call-done
  303.6 6.5 copy.138
  331.0 55.3 %all-gather.28.cloned.1.call-done = f32[192,64,256]{2,1,0:T(8,128)} async-done(((f32[48,64,256]{2,1,0:T(8,128)}), f32[192,64,256]{2,1,0:T(8,128)}) %all-gather.28.cloned.1.call-update) | async-done | bytes 12582928 | tf_op jit(solution)/shard_map/all_gather | solution.py:33
  391.1 14.2 fusion.37
  411.3 73.7 %all-gather.16.cloned.1.call-done = bf16[3072,2048]{1,0:T(8,128)(2,1)} async-done(((bf16[96,2048]{1,0:T(8,128)(2,1)}), bf16[3072,2048]{1,0:T(8,128)(2,1)}) %all-gather.16.cloned.1.call-update) | async-done | bytes 12582928 | tf_op jit(solution)/shard_map/all_gather | solution.py:161
  485.1 10.0 fusion.49
  495.1 53.0 %all-gather.22.cloned.1.call-done = bf16[1024,2048]{1,0:T(8,128)(2,1)} async-done(((bf16[32,2048]{1,0:T(8,128)(2,1)}), bf16[1024,2048]{1,0:T(8,128)(2,1)}) %all-gather.22.cloned.1.call-update) | async-done | bytes 4194320 | tf_op jit(solution)/shard_map/all_gather | solution.py:164
  552.4 192.0 %all-gather.24.cloned.1.call-done = bf16[2048,8192]{1,0:T(8,128)(2,1)} async-done(((bf16[64,8192]{1,0:T(8,128)(2,1)}), bf16[2048,8192]{1,0:T(8,128)(2,1)}) %all-gather.24.cloned.1.call-update) | async-done | bytes 33554448 | tf_op jit(solution)/shard_map/all_gather | solution.py:165
  744.3 18.0 fusion.143
  762.3 6.1 multiply_convert_fusion
  768.4 91.9 %all-gather.26.cloned.1.call-done = bf16[4096,2048]{1,0:T(8,128)(2,1)} async-done(((bf16[128,2048]{1,0:T(8,128)(2,1)}), bf16[4096,2048]{1,0:T(8,128)(2,1)}) %all-gather.26.cloned.1.call-update) | async-done | bytes 16777232 | tf_op jit(solution)/shard_map/all_gather | solution.py:166
  860.3 12.3 fusion.68
  872.6 13.6 fusion.88
  886.2 18.6 multiply_reduce_fusion.10
  904.9 6.7 fusion.155
  913.1 5.3 fusion.6
  925.9 6.6 fusion.139
  933.0 14.3 multiply_reduce_fusion.6
  949.0 5.3 fusion.41
  956.6 20.5 reduce-scatter.12.cloned.1.call-done
  986.1 5.9 fusion.83
  999.1 10.0 fusion.160
  1011.1 13.3 fusion.162
  1029.1 21.7 fusion.10
  1056.9 7.0 fusion.78
  1068.0 17.0 while.27
  1085.1 7.3 multiply_reduce_fusion.9
  1103.1 8.1 fusion.75
  1112.7 12.1 fusion.35
  1124.9 7.4 multiply_reduce_fusion.5
  1143.2 9.2 pad_add_fusion
  1159.4 20.9 fusion.73
  1181.9 27.1 fusion.86
  1217.8 16.4 fusion.56
  1234.2 44.1 %all-reduce.19 = (f32[]{:T(128)}, f32[2048]{0:T(1024)}, f32[2048]{0:T(1024)}, f32[4,3584]{1,0:T(4,128)}, f32[48]{0:T(128)}, /*index=5*/f32[48]{0:T(128)}, f32[48]{0:T(128)}) all-reduce(f32[]{:T(128)} %multiply_reduce_fusion.15, f32[2048]{0:T(1024)S(1)} %get-tuple-element.156, ...), channel_id=1, replica_groups=mesh['batch'=8,'ctx'=4] {'batch','ctx'}, use_global_device_ids=true, to_apply=%region_10.11 | all-reduce | flops 18577 | bytes 148616 | tf_op jit(solution)/shard_map/psum | solution.py:287
  1282.5 70.0 %reduce-scatter.18.cloned.1.call-done = f32[64,1024]{1,0:T(8,128)} async-done(((f32[2048,1024]{1,0:T(8,128)}), f32[64,1024]{1,0:T(8,128)}) %reduce-scatter.18.cloned.1.call-update) | async-done | bytes 262160 | tf_op jit(solution)/shard_map/reduce_scatter | solution.py:406
  1352.5 147.8 %reduce-scatter.22.cloned.1.call-done = f32[32,2048]{1,0:T(8,128)} async-done(((f32[1024,2048]{1,0:T(8,128)}), f32[32,2048]{1,0:T(8,128)}) %reduce-scatter.22.cloned.1.call-update) | async-done | bytes 262160 | tf_op jit(solution)/shard_map/reduce_scatter | solution.py:412
  1500.3 248.2 %reduce-scatter.16.cloned.1.call-done = f32[96,2048]{1,0:T(8,128)} async-done(((f32[3072,2048]{1,0:T(8,128)}), f32[96,2048]{1,0:T(8,128)}) %reduce-scatter.16.cloned.1.call-update) | async-done | bytes 786448 | tf_op jit(solution)/shard_map/reduce_scatter | solution.py:403
  1748.5 356.5 %reduce-scatter.26.cloned.1.call-done = f32[128,2048]{1,0:T(8,128)} async-done(((f32[4096,2048]{1,0:T(8,128)}), f32[128,2048]{1,0:T(8,128)}) %reduce-scatter.26.cloned.1.call-update) | async-done | bytes 1048592 | tf_op jit(solution)/shard_map/reduce_scatter | solution.py:418
  2105.0 584.5 %reduce-scatter.14.cloned.1.call-done = f32[64,6704]{1,0:T(8,128)} async-done(((f32[2048,6704]{1,0:T(8,128)}), f32[64,6704]{1,0:T(8,128)}) %reduce-scatter.14.cloned.1.call-update) | async-done | bytes 1716240 | tf_op jit(solution)/shard_map/reduce_scatter | solution.py:400
  2689.5 713.7 %reduce-scatter.24.cloned.1.call-done = f32[64,8192]{1,0:T(8,128)} async-done(((f32[2048,8192]{1,0:T(8,128)}), f32[64,8192]{1,0:T(8,128)}) %reduce-scatter.24.cloned.1.call-update) | async-done | bytes 2097168 | tf_op jit(solution)/shard_map/reduce_scatter | solution.py:415
  (429 shorter events, 180.0 us)
Async XLA Ops:
  7.2 173.7 %all-gather.14.cloned.1.call-start = ((), (), s32[]{:S(2)}) async-start(), calls=%async_computation.9 | async-start | bytes 28655616 | tf_op jit(solution)/shard_map/all_gather | solution.py:160
  7.9 261.9 %all-gather.18.cloned.1.call-start = ((), (), s32[]{:S(2)}) async-start(), calls=%async_computation.11 | async-start | bytes 2162688 | tf_op jit(solution)/shard_map/all_gather | solution.py:163
  8.7 295.0 %all-gather.20.cloned.1.call-start = ((), (), s32[]{:S(2)}) async-start(), calls=%async_computation.12 | async-start | bytes 4325376 | tf_op jit(solution)/shard_map/all_gather | solution.py:162
  9.4 376.9 %all-gather.28.cloned.1.call-start = ((), (), s32[]{:S(2)}) async-start(), calls=%async_computation.25 | async-start | bytes 15728640 | tf_op jit(solution)/shard_map/all_gather | solution.py:33
  21.3 189.6 %copy-start.76 = (f32[3584]{0:T(1024)}, f32[3584]{0:T(1024)S(1)}, u32[]{:S(2)}) copy-start(f32[3584]{0:T(1024)S(1)} %get-tuple-element.158) | copy-start | bytes 43012
  21.3 189.6 %copy-start.78 = (f32[3584]{0:T(1024)}, f32[3584]{0:T(1024)S(1)}, u32[]{:S(2)}) copy-start(f32[3584]{0:T(1024)S(1)} %get-tuple-element.159) | copy-start | bytes 43012
  21.3 189.6 %copy-start.80 = (f32[3584]{0:T(1024)}, f32[3584]{0:T(1024)S(1)}, u32[]{:S(2)}) copy-start(f32[3584]{0:T(1024)S(1)} %get-tuple-element.160) | copy-start | bytes 43012
  21.3 189.6 %copy-start.82 = (f32[3584]{0:T(1024)}, f32[3584]{0:T(1024)S(1)}, u32[]{:S(2)}) copy-start(f32[3584]{0:T(1024)S(1)} %get-tuple-element.161) | copy-start | bytes 43012
  23.0 175.4 %copy-start.107 = (f32[256]{0:T(256)}, f32[256]{0:T(256)S(1)}, u32[]{:S(2)}) copy-start(f32[256]{0:T(256)S(1)} %fusion.57) | copy-start | bytes 3076
  23.7 179.3 %copy-start.119 = (f32[48]{0:T(128)}, f32[48]{0:T(128)S(1)}, u32[]{:S(2)}) copy-start(f32[48]{0:T(128)S(1)} %exponential_negate_fusion) | copy-start | bytes 580
  23.7 286.5 %copy-start.73 = (f32[256]{0:T(256)}, f32[256]{0:T(256)S(1)}, u32[]{:S(2)}) copy-start(f32[256]{0:T(256)S(1)} %fusion.125) | copy-start | bytes 3076
  25.1 180.6 %copy-start.96 = (f32[256]{0:T(256)}, f32[256]{0:T(256)S(1)}, u32[]{:S(2)}) copy-start(f32[256]{0:T(256)S(1)} %get-tuple-element.233) | copy-start | bytes 3076
  25.1 180.6 %copy-start.105 = (f32[256]{0:T(256)}, f32[256]{0:T(256)S(1)}, u32[]{:S(2)}) copy-start(f32[256]{0:T(256)S(1)} %get-tuple-element.232) | copy-start | bytes 3076
  25.1 185.9 %copy-start.98 = (f32[256]{0:T(256)}, f32[256]{0:T(256)S(1)}, u32[]{:S(2)}) copy-start(f32[256]{0:T(256)S(1)} %get-tuple-element.234) | copy-start | bytes 3076
  25.1 185.9 %copy-start.100 = (f32[256]{0:T(256)}, f32[256]{0:T(256)S(1)}, u32[]{:S(2)}) copy-start(f32[256]{0:T(256)S(1)} %get-tuple-element.235) | copy-start | bytes 3076
  25.1 185.9 %copy-start.102 = (f32[256]{0:T(256)}, f32[256]{0:T(256)S(1)}, u32[]{:S(2)}) copy-start(f32[256]{0:T(256)S(1)} %get-tuple-element.236) | copy-start | bytes 3076
  25.1 177.9 %copy-start.111 = (f32[48]{0:T(128)S(1)}, f32[48]{0:T(128)}, u32[]{:S(2)}) copy-start(f32[48]{0:T(128)} %param.37) | copy-start | bytes 580
  200.8 8.4 collective-permute-start
  224.8 43.9 %copy-start.95 = (s32[1,256]{1,0:T(1,128)S(1)}, s32[1,256]{1,0:T(1,128)}, u32[]{:S(2)}) copy-start(s32[1,256]{1,0:T(1,128)} %param.22) | copy-start | bytes 3076
  224.8 45.0 %copy-start.4 = (bf16[1,256,2048]{2,1,0:T(8,128)(2,1)S(1)}, bf16[1,256,2048]{2,1,0:T(8,128)(2,1)}, u32[]{:S(2)}) copy-start(bf16[1,256,2048]{2,1,0:T(8,128)(2,1)} %param.21) | copy-start | bytes 3145732
  224.8 45.0 %copy-start.46 = (f32[2048]{0:T(1024)S(1)}, f32[2048]{0:T(1024)}, u32[]{:S(2)}) copy-start(f32[2048]{0:T(1024)} %param.32) | copy-start | bytes 24580
  224.8 260.2 %all-gather.16.cloned.1.call-start = ((), (), s32[]{:S(2)}) async-start(), calls=%async_computation.10 | async-start | bytes 12976128 | tf_op jit(solution)/shard_map/all_gather | solution.py:161
  225.4 322.7 %all-gather.22.cloned.1.call-start = ((), (), s32[]{:S(2)}) async-start(), calls=%async_computation.13 | async-start | bytes 4325376 | tf_op jit(solution)/shard_map/all_gather | solution.py:164
  226.0 518.3 %all-gather.24.cloned.1.call-start = ((), (), s32[]{:S(2)}) async-start(), calls=%async_computation.14 | async-start | bytes 34603008 | tf_op jit(solution)/shard_map/all_gather | solution.py:165
  226.7 633.5 %all-gather.26.cloned.1.call-start = ((), (), s32[]{:S(2)}) async-start(), calls=%async_computation.15 | async-start | bytes 17301504 | tf_op jit(solution)/shard_map/all_gather | solution.py:166
  227.5 726.9 %reduce-scatter.10.cloned.1.call-start = ((), (), s32[]{:S(2)}) async-start(), calls=%async_computation.16 | async-start | bytes 1310720 | tf_op jit(solution)/shard_map/reduce_scatter | solution.py:333
  267.4 637.4 %copy-start.109 = (f32[1,256]{1,0:T(1,128)}, f32[1,256]{1,0:T(1,128)S(1)}, u32[]{:S(2)}) copy-start(f32[1,256]{1,0:T(1,128)S(1)} %convert_element_type.163) | copy-start | bytes 3076
  267.8 46.6 %copy-start.59 = (f32[256,64]{0,1:T(8,128)}, f32[256,64]{0,1:T(8,128)S(1)}, u32[]{:S(2)}) copy-start(f32[256,64]{0,1:T(8,128)S(1)} %get-tuple-element.230) | copy-start | bytes 196612
  267.8 46.6 %copy-start.61 = (f32[256,64]{0,1:T(8,128)}, f32[256,64]{0,1:T(8,128)S(1)}, u32[]{:S(2)}) copy-start(f32[256,64]{0,1:T(8,128)S(1)} %get-tuple-element.231) | copy-start | bytes 196612
  280.5 38.5 %copy-start.44 = (bf16[1024,2,128]{2,1,0:T(2,128)(2,1)}, bf16[1024,2,128]{2,1,0:T(2,128)(2,1)S(1)}, u32[]{:S(2)}) copy-start(bf16[1024,2,128]{2,1,0:T(2,128)(2,1)S(1)} %reshape.440) | copy-start | bytes 1572868
  411.3 136.8 %copy-start.36 = (bf16[2,128,4,256]{3,1,2,0:T(8,128)(2,1)S(1)}, bf16[2,128,4,256]{3,1,2,0:T(8,128)(2,1)}, u32[]{:S(2)}) copy-start(bf16[2,128,4,256]{3,1,2,0:T(8,128)(2,1)} %convolution_convert_fusion) | copy-start | bytes 1572868
  548.1 196.2 %copy-start.64 = (f32[2048]{0:T(1024)S(1)}, f32[2048]{0:T(1024)}, u32[]{:S(2)}) copy-start(f32[2048]{0:T(1024)} %param.33) | copy-start | bytes 24580
  552.3 352.5 %copy-start.20 = (f32[256,2048]{1,0:T(8,128)}, f32[256,2048]{1,0:T(8,128)S(1)}, u32[]{:S(2)}) copy-start(f32[256,2048]{1,0:T(8,128)S(1)} %get-tuple-element.242) | copy-start | bytes 6291460
  552.4 352.5 %copy-start.84 = (f32[256]{0:T(256)}, f32[256]{0:T(256)S(1)}, u32[]{:S(2)}) copy-start(f32[256]{0:T(256)S(1)} %fusion.126) | copy-start | bytes 3076
  762.3 98.0 %copy-start.56 = (bf16[1,256,2048]{2,1,0:T(8,128)(2,1)S(1)}, bf16[1,256,2048]{2,1,0:T(8,128)(2,1)}, u32[]{:S(2)}) copy-start(bf16[1,256,2048]{2,1,0:T(8,128)(2,1)} %param.24) | copy-start | bytes 3145732
  925.9 51.2 %reduce-scatter.12.cloned.1.call-start = ((), (), s32[]{:S(2)}) async-start(), calls=%async_computation.17 | async-start | bytes 1310720 | tf_op jit(solution)/shard_map/reduce_scatter | solution.py:339
  932.6 133.3 %all-gather.30.cloned.1.call-start = ((), (), s32[]{:S(2)}) async-start(), calls=%async_computation.26 | async-start | bytes 15728640 | tf_op jit(solution)/shard_map/all_gather | solution.py:33
  954.3 328.2 %reduce-scatter.20.cloned.1.call-start = ((), (), s32[]{:S(2)}) async-start(), calls=%async_computation.21 | async-start | bytes 4325376 | tf_op jit(solution)/shard_map/reduce_scatter | solution.py:409
  981.7 370.9 %reduce-scatter.18.cloned.1.call-start = ((), (), s32[]{:S(2)}) async-start(), calls=%async_computation.20 | async-start | bytes 8650752 | tf_op jit(solution)/shard_map/reduce_scatter | solution.py:406
  992.0 508.3 %reduce-scatter.22.cloned.1.call-start = ((), (), s32[]{:S(2)}) async-start(), calls=%async_computation.22 | async-start | bytes 8650752 | tf_op jit(solution)/shard_map/reduce_scatter | solution.py:412
  997.7 750.8 %reduce-scatter.16.cloned.1.call-start = ((), (), s32[]{:S(2)}) async-start(), calls=%async_computation.19 | async-start | bytes 25952256 | tf_op jit(solution)/shard_map/reduce_scatter | solution.py:403
  1009.2 1095.8 %reduce-scatter.26.cloned.1.call-start = ((), (), s32[]{:S(2)}) async-start(), calls=%async_computation.24 | async-start | bytes 34603008 | tf_op jit(solution)/shard_map/reduce_scatter | solution.py:418
  1024.4 1665.1 %reduce-scatter.14.cloned.1.call-start = ((), (), s32[]{:S(2)}) async-start(), calls=%async_computation.18 | async-start | bytes 57311232 | tf_op jit(solution)/shard_map/reduce_scatter | solution.py:400
  1029.1 27.7 copy-start.1
  1141.8 11.8 collective-permute-start.1
  1180.3 2222.9 %reduce-scatter.24.cloned.1.call-start = ((), (), s32[]{:S(2)}) async-start(), calls=%async_computation.23 | async-start | bytes 69206016 | tf_op jit(solution)/shard_map/reduce_scatter | solution.py:415
  1217.8 61.2 %copy-start.108 = (f32[256]{0:T(256)S(1)}, f32[256]{0:T(256)}, u32[]{:S(2)}) copy-start(f32[256]{0:T(256)} %copy-done.107) | copy-start | bytes 3076
  1217.8 61.2 %copy-start.25 = (f32[256,2048]{1,0:T(8,128)S(1)}, f32[256,2048]{1,0:T(8,128)}, u32[]{:S(2)}) copy-start(f32[256,2048]{1,0:T(8,128)} %get-tuple-element.199) | copy-start | bytes 6291460
  (102 other events, 757.7 us)
Sparse Core Ops, SparseCore 0:
  10.9 169.9 all-gather.13
  183.7 54.5 all-gather.17
  241.2 62.3 all-gather.19
  305.0 81.2 all-gather.27
  389.0 95.9 all-gather.15
  487.8 60.2 all-gather.21
  551.0 193.3 all-gather.23
  747.2 113.0 all-gather.25
  926.0 23.0 reduce-scatter.9
  952.2 24.8 reduce-scatter.11
  978.7 82.0 all-gather.29
  1063.5 141.3 reduce-scatter.19
  1207.7 144.7 reduce-scatter.17
  1355.3 144.9 reduce-scatter.21
  1507.1 241.3 reduce-scatter.15
  1751.3 353.6 reduce-scatter.25
  2107.8 581.6 reduce-scatter.13
  2692.4 710.7 reduce-scatter.23
where the time goes:
time: 3430 us; the launch traced here: 3410 us
  waiting for transfers between devices  2780 us (81%)
  matrix products  337 us (10%)
  blocking collectives  112 us (3%)
  other arithmetic  104 us (3%)
  local copies, waits for them, and re-layouts  52.6 us (2%)
    reduce_scatter x1, waiting for transfers between devices, body(): lax.psum_scatter(outer_rows(normed_two, grad_gateup), ('batch', 'ctx'), s...  714 us
    reduce_scatter x1, waiting for transfers between devices, body(): lax.psum_scatter(outer_rows(normed, grad_mixed), ('batch', 'ctx'), scatte...  585 us
    reduce_scatter x1, waiting for transfers between devices, body(): lax.psum_scatter(outer_rows(hidden, grad_ffn), ('batch', 'ctx'), scatter_...  356 us
    reduce_scatter x1, waiting for transfers between devices, body(): lax.psum_scatter(outer_rows(gated, branch_gradient), ('batch', 'ctx'), sc...  248 us
    all_gather x1, waiting for transfers between devices, body(): lax.all_gather(gate_up, ('batch', 'ctx'), axis=0, tiled=True)  192 us
    all_gather x1, waiting for transfers between devices, body(): lax.all_gather(mixer_in, ('batch', 'ctx'), axis=0, tiled=True)  156 us
    reduce_scatter x1, waiting for transfers between devices, body(): lax.psum_scatter(outer_rows(attended, branch_gradient), ('batch', 'ctx'),...  148 us
    all_gather x1, waiting for transfers between devices, body(): lax.all_gather(down_weight, ('batch', 'ctx'), axis=0, tiled=True)  91.9 us
  transfers between devices with their start and end apart: 20, of which 14 were waited for; matrix products, arithmetic and copies ran while one was open for 12% of the time, Pallas kernels for 0%

commit v1 on v0

v1 whole, which is shorter than its diff:
```python
import functools

import jax
import jax.numpy as jnp
from jax import lax
from jax.experimental import pallas as pl
from jax.experimental.pallas import tpu as pltpu
from jax.sharding import PartitionSpec as P

MODEL_WIDTH = 2048
H_M = 48
P_SIZE = 64
N = 256
QUERY_HEADS = 8
KEY_VALUE_HEADS = 2
HEAD_SIZE = 128
FF = 4096
TAPS = 4
DI = 3072

NC = 4
HEADS = H_M // NC
PAIRS = HEADS // 2
WX = DI // NC
WB = 2 * N // NC
WQ = QUERY_HEADS * HEAD_SIZE // NC
QH = QUERY_HEADS // NC
WF = FF // NC
CHUNK = 128

NORM_EPSILON = 1e-05
ROPE_BASE = 1000000.0
HIGHEST = lax.Precision.HIGHEST
F32 = jnp.float32
BF16 = jnp.bfloat16


def mm(left, right):
    return jnp.dot(left, right, preferred_element_type=F32)


def mm_tn(left, right):
    return lax.dot_general(left, right, (((0,), (0,)), ((), ())), preferred_element_type=F32)


def mm_nt(left, right):
    return lax.dot_general(left, right, (((1,), (1,)), ((), ())), preferred_element_type=F32)


def after(value, *deps):
    return lax.optimization_barrier((value,) + deps)[0]


def core_swap(value):
    return lax.ppermute(value, "ctx", [(i, i ^ 1) for i in range(NC)])


def y_swap(value):
    return lax.ppermute(value, "ctx", [(i, i ^ 2) for i in range(NC)])


class Ring:
    def __init__(self):
        self.n = lax.axis_size("batch")
        n = self.n
        order = list(range(0, n, 2)) + list(range(n - 1, 0, -2))
        self.up_pairs = [(order[i], order[(i + 1) % n]) for i in range(n)]
        self.down_pairs = [(order[(i + 1) % n], order[i]) for i in range(n)]
        b = lax.axis_index("batch")
        self.pos = jnp.where(b % 2 == 0, b // 2, n - 1 - b // 2)

    def up(self, value):
        return lax.ppermute(value, "batch", self.up_pairs)

    def down(self, value):
        return lax.ppermute(value, "batch", self.down_pairs)

    def owner(self, slot):
        p = (self.pos + slot + self.n) % self.n
        return jnp.where(p < self.n // 2, 2 * p, 2 * (self.n - 1 - p) + 1)


class Order:
    def __init__(self, token):
        self.token = token

    def gate(self, *values):
        out = lax.optimization_barrier(values + (self.token,))
        self.token = out[-1]
        return out[:-1]


class GatherRun:
    def __init__(self, ring, order, block, place=lambda b: b):
        self.ring, self.order, self.place = ring, order, place
        self.rows, cols = block.shape
        (block,) = order.gate(block)
        self.down, self.up = ring.down(block), ring.up(block)
        self.whole = jnp.zeros((ring.n * self.rows, cols), block.dtype)
        self.put(block, 0)
        self.step, self.over = 1, False

    def put(self, part, slot, offset=0):
        at = self.place(self.ring.owner(slot)) * self.rows + offset
        self.whole = lax.dynamic_update_slice(self.whole, part, (at, 0))

    def turn(self, others):
        ring, far, half = self.ring, self.ring.n // 2, self.rows // 2
        down, up, *others = self.order.gate(self.down, self.up, *others)
        if self.step < far:
            if self.step + 1 < far:
                self.down, self.up = ring.down(down), ring.up(up)
            else:
                self.down, self.up = ring.down(down[half:]), ring.up(up[:half])
            self.put(down, self.step)
            self.put(up, -self.step)
        else:
            self.put(up, far)
            self.put(down, far, half)
            self.over = True
        self.step += 1
        return others


class ReduceRun:
    def __init__(self, ring, order, part):
        self.ring, self.order, self.part = ring, order, part
        far = part(ring.n // 2).astype(BF16)
        (far,) = order.gate(far)
        self.half = far.shape[0] // 2
        self.up, self.down = ring.up(far[: self.half]), ring.down(far[self.half :])
        self.step, self.over = ring.n // 2 - 1, False

    def turn(self, others):
        half = self.half
        up, down, *others = self.order.gate(self.up, self.down, *others)
        if self.step == 0:
            self.result = self.part(0) + up.astype(F32) + down.astype(F32)
            self.over = True
            return others
        a, b = self.part(self.step), self.part(-self.step)
        if self.step == self.ring.n // 2 - 1:
            a = jnp.concatenate([a[:half] + up.astype(F32), a[half:]], axis=0)
            b = jnp.concatenate([b[:half], b[half:] + down.astype(F32)], axis=0)
        else:
            a = a + up.astype(F32)
            b = b + down.astype(F32)
        self.up, self.down = self.ring.up(a.astype(BF16)), self.ring.down(b.astype(BF16))
        self.step -= 1
        return others


def sum_everywhere(value, batch):
    value = value + core_swap(value)
    value = value + y_swap(value)
    bit = 1
    while bit < batch:
        value = value + lax.ppermute(value, "batch", [(i, i ^ bit) for i in range(batch)])
        bit *= 2
    return value


class Spread:
    def __init__(self, parts, j):
        self.parts, self.j = parts, j
        self.got = y_swap(jnp.stack([parts[j ^ 2], parts[j ^ 3]]))

    def cross(self):
        self.across = core_swap(jnp.stack([self.parts[self.j ^ 1], self.got[1]]))

    def block(self):
        blocks = [self.parts[self.j], self.across[0], self.got[0], self.across[1]]
        whole = absolute(blocks, self.j)
        return whole.reshape(NC * whole.shape[1], whole.shape[2])


class Collect:
    def __init__(self, block, j):
        self.block, self.j = block, j
        self.got = core_swap(jnp.stack([block[j ^ 1], block[j ^ 3]]))

    def cross(self):
        self.far = y_swap(jnp.stack([self.block[self.j ^ 2], self.got[1]]))

    def result(self):
        whole = absolute([self.block[self.j], self.got[0], self.far[0], self.far[1]], self.j)
        return whole.astype(F32)


def absolute(blocks, j):
    whole = jnp.zeros((NC,) + blocks[0].shape, blocks[0].dtype)
    for k in range(NC):
        whole = lax.dynamic_update_slice(
            whole, blocks[k][None], (j ^ k,) + (0,) * blocks[0].ndim
        )
    return whole


def stacked(blocks):
    size = blocks[0].shape[0]
    whole = jnp.zeros((len(blocks) * size,) + blocks[0].shape[1:], blocks[0].dtype)
    for k, block in enumerate(blocks):
        whole = lax.dynamic_update_slice_in_dim(whole, block, k * size, 0)
    return whole


class Near:
    def __init__(self, own):
        self.own, self.far, self.next = own, y_swap(own), core_swap(own)

    def cross(self):
        self.last = core_swap(self.far)

    def blocks(self):
        return [self.own, self.next, self.far, self.last]


class NearSum:
    def __init__(self, part):
        third = core_swap(part(3).astype(BF16))
        self.second = y_swap((part(2) + third.astype(F32)).astype(BF16))
        self.first = core_swap(part(1).astype(BF16))
        self.near = part(0)

    def result(self):
        return self.near + self.first.astype(F32) + self.second.astype(F32)


def halves(first, second, lanes):
    return jnp.where(lanes < P_SIZE, first, second)


def kernel_of(colv, rowv, h, allowed):
    spread = colv[:, h : h + 1] - rowv[h : h + 1, :]
    return jnp.exp(jnp.where(allowed, spread, -1e30))


def chunk_mask(colv, rowv):
    shape = (CHUNK, CHUNK)
    rows = lax.broadcasted_iota(jnp.int32, shape, 0)
    cols = lax.broadcasted_iota(jnp.int32, shape, 1)
    same = colv[:, 4 * HEADS : 4 * HEADS + 1] == rowv[2 * HEADS : 2 * HEADS + 1, :]
    return same & (rows >= cols)


def ssd_forward_kernel(thr, x_ref, b_ref, c_ref, col_ref, row_ref, skip_ref, y_ref, st_ref, state):
    i = pl.program_id(0)

    @pl.when(i == 0)
    def _():
        state[...] = jnp.zeros_like(state)

    colv, rowv = col_ref[...], row_ref[...]
    b, c = b_ref[...].astype(BF16), c_ref[...].astype(BF16)
    allowed = chunk_mask(colv, rowv)
    inner = mm_nt(c, b)
    lanes = lax.broadcasted_iota(jnp.int32, (CHUNK, 2 * P_SIZE), 1)
    subs = lax.broadcasted_iota(jnp.int32, (2 * P_SIZE, N), 0)
    for p in range(PAIRS):
        span = slice(2 * P_SIZE * p, 2 * P_SIZE * (p + 1))
        x = x_ref[:, span]
        xb = x.astype(BF16)
        local = []
        for h in (2 * p, 2 * p + 1):
            mixing = kernel_of(colv, rowv, h, allowed) * inner * rowv[HEADS + h : HEADS + h + 1, :]
            local.append(mm(mixing.astype(BF16), xb))
        h = 2 * p

        def pick(base):
            return halves(
                colv[:, base + h : base + h + 1], colv[:, base + h + 1 : base + h + 2], lanes
            )

        held = state[span, :]
        hb = held.astype(BF16)
        st_ref[0, span, :] = hb
        y_ref[:, span] = (
            halves(local[0], local[1], lanes)
            + pick(HEADS) * mm_nt(c, hb)
            + skip_ref[:, span] * x
        )
        tail = mm_tn((pick(2 * HEADS) * x).astype(BF16), b)
        through = jnp.where(subs < P_SIZE, thr[i, h], thr[i, h + 1])
        state[span, :] = through * held + tail


def ssd_backward_kernel(first, *refs):
    (thr, g_ref, x_ref, b_ref, c_ref, col_ref, row_ref, skip_ref, st_ref), refs = refs[:9], refs[9:]
    if first:
        (dbc_in, dcol_in, _), refs = refs[:3], refs[3:]
    dx_ref, dbc_ref, dcol_ref, drow_ref, later = refs
    i = pl.num_programs(0) - 1 - pl.program_id(0)

    @pl.when(pl.program_id(0) == 0)
    def _():
        later[...] = jnp.zeros_like(later)

    colv, rowv = col_ref[...], row_ref[...]
    b, c = b_ref[...].astype(BF16), c_ref[...].astype(BF16)
    allowed = chunk_mask(colv, rowv)
    inner = mm_nt(c, b)
    lanes = lax.broadcasted_iota(jnp.int32, (CHUNK, 2 * P_SIZE), 1)
    subs = lax.broadcasted_iota(jnp.int32, (2 * P_SIZE, N), 0)
    last = lax.broadcasted_iota(jnp.int32, (CHUNK, 1), 0) == CHUNK - 1
    d_inner = jnp.zeros((CHUNK, CHUNK), F32)
    db = jnp.zeros((CHUNK, N), F32)
    dc = jnp.zeros((CHUNK, N), F32)
    dcol = dcol_in[...] if first else jnp.zeros((CHUNK, 128), F32)
    rows_out = []
    wide = lax.broadcasted_iota(jnp.int32, (CHUNK, 128), 1)
    for p in range(PAIRS // 2):
        span = slice(2 * P_SIZE * p, 2 * P_SIZE * (p + 1))
        x, g = x_ref[:, span], g_ref[:, span]
        xb, gb = x.astype(BF16), g.astype(BF16)
        h = 2 * (p + first)

        def pick(base):
            return halves(
                colv[:, base + h : base + h + 1], colv[:, base + h + 1 : base + h + 2], lanes
            )

        start = st_ref[0, span, :]
        ahead = later[span, :]
        ab = ahead.astype(BF16)
        reach, weight, bare = pick(HEADS), pick(2 * HEADS), pick(3 * HEADS)
        bs = mm_nt(b, ab)
        cs = mm_nt(c, start)
        xbs = x * bs
        carried = g * cs * reach
        stored = xbs * weight
        direct = xbs * bare
        product = ahead * start.astype(F32)
        local = []
        for q in (0, 1):
            hq = h + q
            mine = (lanes >= P_SIZE) if q else (lanes < P_SIZE)
            e = kernel_of(colv, rowv, hq, allowed)
            step = rowv[HEADS + hq : HEADS + hq + 1, :]
            d_mix = mm_nt(jnp.where(mine, g, 0.0).astype(BF16), xb)
            e_step = e * step
            local.append(mm_tn((e_step * inner).astype(BF16), gb))
            d_e = d_mix * e_step
            d_inner = d_inner + d_e
            total = d_e * inner
            rows_out.append(jnp.sum(d_mix * e * inner, axis=0, keepdims=True))
            stored_sum = jnp.sum(jnp.where(mine, stored, 0.0), axis=1, keepdims=True)
            d_cum = (
                jnp.sum(total, axis=1, keepdims=True)
                + jnp.sum(jnp.where(mine, carried - stored, 0.0), axis=1, keepdims=True)
            )
            mine_rows = (subs >= P_SIZE) if q else (subs < P_SIZE)
            end = jnp.sum(stored_sum) + thr[i, hq] * jnp.sum(jnp.where(mine_rows, product, 0.0))
            d_cum = d_cum + jnp.where(last, end, 0.0)
            d_step = jnp.sum(jnp.where(mine, direct, 0.0), axis=1, keepdims=True)
            dcol = jnp.where(wide == hq, d_cum, dcol)
            dcol = jnp.where(wide == HEADS + hq, d_step, dcol)
        gr = (reach * g).astype(BF16)
        dc = dc + mm(gr, start)
        db = db + mm((weight * x).astype(BF16), ab)
        dx_ref[:, span] = (
            halves(local[0], local[1], lanes) + weight * bs + skip_ref[:, span] * g
        )
        through = jnp.where(subs < P_SIZE, thr[i, h], thr[i, h + 1])
        later[span, :] = through * ahead + mm_tn(gr, c)
    di = d_inner.astype(BF16)
    db = db + mm_tn(di, c)
    dc = dc + mm(di, b)
    for q, value in enumerate((db[:, :WB], db[:, WB:], dc[:, :WB], dc[:, WB:])):
        dbc_ref[q] = value + dbc_in[q] if first else value
    dcol_ref[...] = dcol
    drow_ref[: len(rows_out), :] = jnp.concatenate(rows_out, axis=0)


def ssd_specs(chunks, flip, width, part):
    def at(i):
        return chunks - 1 - i if flip else i

    wide = pl.BlockSpec((CHUNK, width), lambda i: (at(i), part))
    mat = pl.BlockSpec((CHUNK, N), lambda i: (at(i), 0))
    col = pl.BlockSpec((CHUNK, 128), lambda i: (at(i), 0))
    row = pl.BlockSpec((32, CHUNK), lambda i: (0, at(i)))
    drow = pl.BlockSpec((8, CHUNK), lambda i: (0, at(i)))
    skip = pl.BlockSpec((1, width), lambda i: (0, part))
    states = pl.BlockSpec((1, width, N), lambda i: (at(i), part, 0))
    dbc = pl.BlockSpec((NC, CHUNK, WB), lambda i: (0, at(i), 0))
    thr = pl.BlockSpec(memory_space=pltpu.SMEM)
    return thr, wide, mat, col, row, drow, skip, states, dbc


def ssd_forward(thr, x, b, c, colv, rowv, skip):
    tokens = x.shape[0]
    chunks = tokens // CHUNK
    t, wide, mat, col, row, _, sk, states, _ = ssd_specs(chunks, False, WX, 0)
    return pl.pallas_call(
        ssd_forward_kernel,
        grid=(chunks,),
        in_specs=[t, wide, mat, mat, col, row, sk],
        out_specs=[wide, states],
        out_shape=[
            jax.ShapeDtypeStruct((tokens, WX), F32),
            jax.ShapeDtypeStruct((chunks, WX, N), BF16),
        ],
        scratch_shapes=[pltpu.VMEM((WX, N), F32)],
        compiler_params=pltpu.CompilerParams(
            dimension_semantics=("arbitrary",), vmem_limit_bytes=32 << 20
        ),
        name="ssd_forward",
    )(thr, x, b, c, colv, rowv, skip)


def ssd_backward(part, thr, g, x, b, c, colv, rowv, skip, states, earlier=()):
    tokens = x.shape[0]
    chunks = tokens // CHUNK
    t, wide, mat, col, row, drow, sk, st, dbc = ssd_specs(chunks, True, WX // 2, part)
    extra = [dbc, col, pl.BlockSpec(memory_space=pl.ANY)] if part else []
    return pl.pallas_call(
        functools.partial(ssd_backward_kernel, part * PAIRS // 2),
        grid=(chunks,),
        in_specs=[t, wide, wide, mat, mat, col, row, sk, st] + extra,
        out_specs=[wide, dbc, col, drow],
        out_shape=[
            jax.ShapeDtypeStruct((tokens, WX), F32),
            jax.ShapeDtypeStruct((NC, tokens, WB), F32),
            jax.ShapeDtypeStruct((tokens, 128), F32),
            jax.ShapeDtypeStruct((8, tokens), F32),
        ],
        scratch_shapes=[pltpu.VMEM((WX // 2, N), F32)],
        input_output_aliases={11: 0} if part else {},
        compiler_params=pltpu.CompilerParams(
            dimension_semantics=("arbitrary",), vmem_limit_bytes=40 << 20
        ),
        name="ssd_backward",
    )(thr, g, x, b, c, colv, rowv, skip, states, *earlier)


Q_BLOCK = 256
SCALE = HEAD_SIZE ** (-0.5)


def attention_probs(q, k, segc, segr, i):
    scores = mm_nt(q, k) * SCALE
    rows = lax.broadcasted_iota(jnp.int32, scores.shape, 0) + i * Q_BLOCK
    cols = lax.broadcasted_iota(jnp.int32, scores.shape, 1)
    scores = jnp.where((rows >= cols) & (segc == segr), scores, -1e30)
    grown = jnp.exp(scores - jnp.max(scores, axis=-1, keepdims=True))
    return grown / jnp.sum(grown, axis=-1, keepdims=True)


def attention_forward_kernel(q_ref, k_ref, v_ref, segc_ref, segr_ref, o_ref):
    probs = attention_probs(q_ref[...], k_ref[...], segc_ref[...], segr_ref[...], pl.program_id(1))
    o_ref[...] = mm(probs.astype(BF16), v_ref[...]).astype(BF16)


def attention_backward_kernel(
    q_ref, k_ref, v_ref, segc_ref, segr_ref, g_ref, dq_ref, dk_ref, dv_ref
):
    @pl.when((pl.program_id(0) == 0) & (pl.program_id(1) == 0))
    def _():
        dk_ref[...] = jnp.zeros_like(dk_ref)
        dv_ref[...] = jnp.zeros_like(dv_ref)

    q, k, g = q_ref[...], k_ref[...], g_ref[...]
    probs = attention_probs(q, k, segc_ref[...], segr_ref[...], pl.program_id(1))
    d_probs = mm_nt(g, v_ref[...])
    inner = jnp.sum(probs * d_probs, axis=-1, keepdims=True)
    d_scores = (probs * (d_probs - inner)).astype(BF16)
    dq_ref[...] = mm(d_scores, k) * SCALE
    dk_ref[...] += mm_tn(d_scores, q) * SCALE
    dv_ref[...] += mm_tn(probs.astype(BF16), g)


def attention_specs(tokens):
    block = pl.BlockSpec((Q_BLOCK, HEAD_SIZE), lambda h, i: (i, h))
    whole = pl.BlockSpec((tokens, HEAD_SIZE), lambda h, i: (0, 0))
    segc = pl.BlockSpec((Q_BLOCK, 1), lambda h, i: (i, 0))
    segr = pl.BlockSpec((1, tokens), lambda h, i: (0, 0))
    params = pltpu.CompilerParams(
        dimension_semantics=("arbitrary", "arbitrary"), vmem_limit_bytes=32 << 20
    )
    return block, whole, segc, segr, params


def attention_forward(q, k, v, segc, segr):
    tokens = q.shape[0]
    block, whole, sc, sr, params = attention_specs(tokens)
    return pl.pallas_call(
        attention_forward_kernel,
        grid=(QH, tokens // Q_BLOCK),
        in_specs=[block, whole, whole, sc, sr],
        out_specs=block,
        out_shape=jax.ShapeDtypeStruct((tokens, QH * HEAD_SIZE), BF16),
        compiler_params=params,
        name="attention_forward",
    )(q, k, v, segc, segr)


def attention_backward(q, k, v, segc, segr, g):
    tokens = q.shape[0]
    block, whole, sc, sr, params = attention_specs(tokens)
    return pl.pallas_call(
        attention_backward_kernel,
        grid=(QH, tokens // Q_BLOCK),
        in_specs=[block, whole, whole, sc, sr, block],
        out_specs=[block, whole, whole],
        out_shape=[
            jax.ShapeDtypeStruct((tokens, QH * HEAD_SIZE), F32),
            jax.ShapeDtypeStruct((tokens, HEAD_SIZE), F32),
            jax.ShapeDtypeStruct((tokens, HEAD_SIZE), F32),
        ],
        compiler_params=params,
        name="attention_backward",
    )(q, k, v, segc, segr, g)


def rms_of(rows):
    return lax.rsqrt(jnp.mean(rows * rows, axis=-1, keepdims=True) + NORM_EPSILON)


def norm_back(grad, rows, r, gain):
    w = grad * gain
    return r * w - rows * (r * r * r) * jnp.mean(w * rows, axis=-1, keepdims=True)


def silu_slope(value):
    sg = jax.nn.sigmoid(value)
    return sg * (1.0 + value * (1.0 - sg))


def turned(heads, cosine, sine):
    half = HEAD_SIZE // 2
    parts = []
    for h in range(heads.shape[1] // HEAD_SIZE):
        v = heads[:, h * HEAD_SIZE : (h + 1) * HEAD_SIZE]
        parts.append(v * cosine + jnp.concatenate([v[:, half:], v[:, :half]], axis=1) * sine)
    return jnp.concatenate(parts, axis=1)


def shifted(value, lag):
    if lag == 0:
        return value
    zeros = jnp.zeros((abs(lag), value.shape[1]), value.dtype)
    if lag > 0:
        return jnp.concatenate([zeros, value[:-lag]], axis=0)
    return jnp.concatenate([value[-lag:], zeros], axis=0)


def convolve(value, taps, keeps):
    total = taps[0][None] * value
    for lag in range(1, TAPS):
        total = total + taps[lag][None] * shifted(value, lag) * keeps[lag]
    return total


def body(
    tokens,
    segment_ids,
    valid_mask,
    teacher,
    mixer_in,
    mixer_out,
    query_weight,
    key_value_weight,
    output_weight,
    gate_up,
    down_weight,
    norm_first,
    norm_second,
    conv_taps,
    decay_log,
    skip_gain,
    step_bias,
):
    ring = Ring()
    nb = ring.n
    j = lax.axis_index("ctx")
    own = tokens.shape[0] * tokens.shape[1]
    length = own * NC
    devices = nb * NC
    total_tokens = float(own * devices)
    x = tokens.reshape(own, MODEL_WIDTH).astype(F32)
    valid = valid_mask.reshape(own).astype(F32)
    target = teacher.reshape(own, MODEL_WIDTH).astype(F32)

    order = Order(jnp.broadcast_to(valid[:1] * 0.0, (8, 128)))
    gate, scale = order.gate, max(1, nb // 8)

    def turn(run, *others):
        for _ in range(scale):
            if not run.over:
                others = run.turn(others)
        return others[0] if len(others) == 1 else others

    def finish(run, *others):
        while not run.over:
            others = run.turn(others)
        return others[0] if len(others) == 1 else others

    def start(block, place=lambda b: b):
        return GatherRun(ring, order, block, place)

    rows = mixer_in.shape[0]
    edge = 2 * DI + 2 * N
    unit = down_weight.shape[0]
    down_half = MODEL_WIDTH // 2
    g_da = start(down_weight[:, :down_half])

    xs_cols = mixer_in[:, DI : 2 * DI].reshape(rows, NC, WX)
    bc_cols = mixer_in[:, 2 * DI : edge].reshape(rows, NC, WB)
    dt_cols = jnp.pad(mixer_in[:, edge:].reshape(rows, NC, HEADS), ((0, 0), (0, 0), (0, 128 - HEADS)))
    first_cols = jnp.concatenate([xs_cols, bc_cols, dt_cols], axis=2).transpose(1, 0, 2)
    spread = Spread(first_cols, j)
    spread.got, mixer_in, query_weight, key_value_weight, x = turn(
        g_da, spread.got, mixer_in, query_weight, key_value_weight, x
    )
    spread.cross()
    z_cols = mixer_in[:, :DI].reshape(rows, NC, WX)
    q_cols = query_weight.reshape(rows, NC, WQ)
    kv = key_value_weight.reshape(rows, 2, 2, HEAD_SIZE)
    kv_cols = kv.transpose(0, 2, 1, 3).reshape(rows, NC, HEAD_SIZE)
    second_cols = jnp.concatenate([q_cols, kv_cols, z_cols], axis=2).transpose(1, 0, 2)
    spread_two = Spread(second_cols, j)
    r_x = rms_of(x)
    normed_own = (x * r_x * norm_first).astype(BF16)
    spread.across, segment_ids, valid, normed_own = turn(
        g_da, spread.across, segment_ids, valid, normed_own
    )
    g_first = start(spread.block())
    near_normed = Near(normed_own)
    near_seg = Near(segment_ids.reshape(1, own))
    count = sum_everywhere(jnp.broadcast_to(jnp.sum(valid), (1, 128)), nb)
    near_seg.far, near_seg.next, spread_two.got = turn(
        g_da, near_seg.far, near_seg.next, spread_two.got
    )
    near_seg.cross()
    spread_two.cross()
    mixer_out, output_weight, gate_up = finish(g_da, mixer_out, output_weight, gate_up)
    rows_out, rows_attn = mixer_out.shape[0], output_weight.shape[0]

    def home(q):
        return (q % 2) * 4 + q // 2 % 2 * 2 + q // 4 if nb == 8 else q

    there = [(m, home(m % nb) * NC + m // nb) for m in range(devices)]
    back = [(b, a) for a, b in there]
    both_out = lax.ppermute(
        jnp.concatenate([mixer_out, output_weight], axis=0), ("batch", "ctx"), there
    )
    near_normed.far, near_normed.next, spread_two.across, near_seg.last = turn(
        g_first, near_normed.far, near_normed.next, spread_two.across, near_seg.last
    )
    near_normed.cross()
    gu_cols = (
        gate_up.reshape(rows, 2, nb, NC, unit).transpose(3, 0, 1, 2, 4).reshape(NC, rows, 2 * WF)
    )
    spread_gu = Spread(gu_cols, j)
    near_normed.last, count = turn(g_first, near_normed.last, count)
    g_second = start(spread_two.block())
    normed = absolute(near_normed.blocks(), j).reshape(length, MODEL_WIDTH)
    spread_gu.got, normed = turn(g_first, spread_gu.got, normed)
    spread_gu.cross()

    seg = absolute(near_seg.blocks(), j).reshape(length)
    keeps = [None]
    for lag in range(1, TAPS):
        before = jnp.concatenate([jnp.full((lag,), -1, jnp.int32), seg[:-lag]])
        keeps.append((before == seg).astype(F32)[:, None])
    place = jnp.arange(length, dtype=jnp.int32)
    half = HEAD_SIZE // 2
    inverse = ROPE_BASE ** (-(jnp.arange(half, dtype=F32) * 2.0) / HEAD_SIZE)
    angle = place.astype(F32)[:, None] * inverse[None, :]
    cosine, sine = jnp.cos(angle), jnp.sin(angle)
    cosine = jnp.concatenate([cosine, cosine], axis=1)
    sine = jnp.concatenate([-sine, sine], axis=1)
    heads_at = j * HEADS
    own_log = lax.dynamic_slice_in_dim(decay_log, heads_at, HEADS)
    own_bias = lax.dynamic_slice_in_dim(step_bias, heads_at, HEADS)
    own_skip = lax.dynamic_slice_in_dim(skip_gain, heads_at, HEADS)
    skip_wide = jnp.repeat(own_skip, P_SIZE)[None, :]
    taps_x = lax.dynamic_slice(conv_taps, (0, j * WX), (TAPS, WX))
    taps_b = conv_taps[:, DI:]
    taps_b_own = lax.dynamic_slice(conv_taps, (0, DI + j * WB), (TAPS, WB))
    cosine, sine, seg, normed, spread_gu.across = finish(
        g_first, cosine, sine, seg, normed, spread_gu.across
    )
    w_first = g_first.whole

    conv_b_own = mm(normed, w_first[:, WX : WX + WB]).astype(BF16)
    b_far = y_swap(conv_b_own)
    conv_b_own, normed, w_first = turn(g_second, conv_b_own, normed, w_first)
    step_raw = mm(normed, w_first[:, WX + WB :])[:, :HEADS]
    conv_x = mm(normed, w_first[:, :WX]).astype(BF16)
    conv_x, step_raw, b_far, both_out = turn(g_second, conv_x, step_raw, b_far, both_out)
    b_other = core_swap(jnp.concatenate([conv_b_own, b_far], axis=1))
    g_out = start(both_out, lambda b: home(b))
    upper, core = j // 2, j % 2
    mine = (jnp.where(upper == 0, conv_b_own, b_far), jnp.where(upper == 0, b_far, conv_b_own))
    theirs = (
        jnp.where(upper == 0, b_other[:, :WB], b_other[:, WB:]),
        jnp.where(upper == 0, b_other[:, WB:], b_other[:, :WB]),
    )
    conv_b = jnp.concatenate(
        [
            jnp.where(core == 0, mine[0], theirs[0]),
            jnp.where(core == 0, theirs[0], mine[0]),
            jnp.where(core == 0, mine[1], theirs[1]),
            jnp.where(core == 0, theirs[1], mine[1]),
        ],
        axis=1,
    )
    conv_out_x = convolve(conv_x.astype(F32), taps_x, keeps)
    xs = jax.nn.silu(conv_out_x)
    xs, conv_out_x, conv_b, step_raw = turn(g_second, xs, conv_out_x, conv_b, step_raw)
    bc = jax.nn.silu(convolve(conv_b.astype(F32), taps_b, keeps))
    bmat, cmat = bc[:, :N], bc[:, N:]

    step_in = step_raw + own_bias
    step = jax.nn.softplus(step_in)
    rate = jnp.exp(own_log)
    decay = -rate * step
    chunks = length // CHUNK
    lower = jnp.tril(jnp.ones((CHUNK, CHUNK), F32))
    by_chunk = decay.reshape(chunks, CHUNK, HEADS)
    cum = jnp.einsum("ts,csh->cth", lower, by_chunk, precision=HIGHEST)
    seg_c = seg.reshape(chunks, CHUNK)
    seg_last = seg_c[:, -1]
    seg_prev = jnp.concatenate([jnp.full((1,), -1, jnp.int32), seg_last[:-1]])
    reach = jnp.exp(cum) * (seg_c == seg_prev[:, None]).astype(F32)[:, :, None]
    bare = jnp.exp(cum[:, -1:, :] - cum) * (seg_c == seg_last[:, None]).astype(F32)[:, :, None]
    weight = bare * step.reshape(chunks, CHUNK, HEADS)
    through = jnp.exp(cum[:, -1]) * (seg_last == seg_prev).astype(F32)[:, None]
    seg_f = seg.astype(F32)
    colv = jnp.concatenate(
        [
            cum.reshape(length, HEADS),
            reach.reshape(length, HEADS),
            weight.reshape(length, HEADS),
            bare.reshape(length, HEADS),
            seg_f[:, None],
            jnp.zeros((length, 128 - 4 * HEADS - 1), F32),
        ],
        axis=1,
    )
    rowv = jnp.concatenate(
        [
            cum.reshape(length, HEADS).T,
            step.T,
            seg_f[None, :],
            jnp.zeros((32 - 2 * HEADS - 1, length), F32),
        ],
        axis=0,
    )
    bmat, cmat, colv, rowv, xs = finish(g_second, bmat, cmat, colv, rowv, xs)
    w_second = g_second.whole
    bmat, cmat, colv, rowv, xs = turn(g_out, bmat, cmat, colv, rowv, xs)
    ssm_y, states = ssd_forward(through, xs, bmat, cmat, colv, rowv, skip_wide)
    ssm_y, normed = turn(g_out, ssm_y, normed)
    rest = mm(normed, w_second)
    rest = turn(g_out, rest)
    g_gu = start(spread_gu.block())
    gate_z = rest[:, WQ + HEAD_SIZE :]
    queries = turned(rest[:, :WQ], cosine, sine).astype(BF16)
    kv_raw = rest[:, WQ : WQ + HEAD_SIZE]
    kv_own = jnp.where(core == 0, turned(kv_raw, cosine, sine), kv_raw).astype(BF16)
    kv_other = core_swap(kv_own)
    keys = jnp.where(core == 0, kv_own, kv_other)
    values = jnp.where(core == 0, kv_other, kv_own)
    segc, segr = seg[:, None], seg[None, :]
    attended = attention_forward(queries, keys, values, segc, segr)
    silu_z = jax.nn.silu(gate_z)
    gated = (ssm_y * silu_z).astype(BF16)
    acts = jnp.concatenate([gated, attended], axis=1)
    acts = finish(g_out, acts)
    out_all = g_out.whole.reshape(nb, rows_out + rows_attn, MODEL_WIDTH)
    w_out = jnp.concatenate(
        [
            out_all[:, :rows_out].reshape(WX, MODEL_WIDTH),
            out_all[:, rows_out:].reshape(WQ, MODEL_WIDTH),
        ],
        axis=0,
    )

    mixed = NearSum(lambda k: mm(lax.dynamic_slice_in_dim(acts, (j ^ k) * own, own), w_out))
    mixed.first, mixed.near = turn(g_gu, mixed.first, mixed.near)
    (mixed.second,) = gate(mixed.second)
    hidden_one = x + mixed.result()
    r_h = rms_of(hidden_one)
    normed_two_own = (hidden_one * r_h * norm_second).astype(BF16)
    (normed_two_own,) = gate(normed_two_own)
    near_two = Near(normed_two_own)
    near_two.next, down_b = turn(g_gu, near_two.next, down_weight[:, down_half:])
    (near_two.far,) = gate(near_two.far)
    near_two.cross()
    g_db = start(down_b)
    near_two.last = turn(g_gu, near_two.last)
    normed_two = near_two.blocks()
    normed_two_all = stacked(normed_two)
    normed_two = list(finish(g_gu, *normed_two))
    w_gu = g_gu.whole

    gates = []
    hidden_all = jnp.zeros((length, WF), BF16)
    for k in range(NC):
        gateup = mm(normed_two[k], w_gu)
        gateup = turn(g_db, gateup)
        gates.append(gateup)
        piece = (jax.nn.silu(gateup[:, :WF]) * gateup[:, WF:]).astype(BF16)
        hidden_all = lax.dynamic_update_slice(hidden_all, piece, (k * own, 0))

    def near_rows(value, k):
        return value[k * own : (k + 1) * own]

    hidden_all = finish(g_db, hidden_all)
    count = count[0, 0]
    w_down = jnp.concatenate([g_da.whole, g_db.whole], axis=1)
    ffn = NearSum(lambda k: mm(near_rows(hidden_all, k), w_down))
    (ffn.second,) = gate(ffn.second)
    final = hidden_one + ffn.result()
    error = final - target
    squares = jnp.sum(valid * jnp.sum(error * error, axis=1))
    grad_final = valid[:, None] * error * (total_tokens / count)
    grad_ffn_own = grad_final.astype(BF16)

    def block_of(left, size, right):
        def part(slot):
            return mm_tn(
                lax.dynamic_slice_in_dim(left, ring.owner(slot) * size, size, axis=1), right
            )

        return part

    def reduce(part):
        return ReduceRun(ring, order, part)

    (grad_ffn_own,) = gate(grad_ffn_own)
    near_ffn = Near(grad_ffn_own)
    d_gateup_all = jnp.zeros((length, 2 * WF), BF16)

    def ffn_back(whole, grad, k):
        d_hidden = mm_nt(grad, w_down)
        gate_k, up_k = gates[k][:, :WF], gates[k][:, WF:]
        d_gate = (d_hidden * up_k * silu_slope(gate_k)).astype(BF16)
        d_up = (d_hidden * jax.nn.silu(gate_k)).astype(BF16)
        whole = lax.dynamic_update_slice(whole, d_gate, (k * own, 0))
        return lax.dynamic_update_slice(whole, d_up, (k * own, WF))

    d_gateup_all = ffn_back(d_gateup_all, near_ffn.own, 0)
    d_gateup_all = ffn_back(d_gateup_all, near_ffn.next, 1)
    near_ffn.far, near_ffn.next, d_gateup_all = gate(near_ffn.far, near_ffn.next, d_gateup_all)
    near_ffn.cross()
    d_gateup_all = ffn_back(d_gateup_all, near_ffn.far, 2)
    grad_ffn_all = stacked(near_ffn.blocks())
    r_down = reduce(block_of(hidden_all, unit, grad_ffn_all))
    d_gateup_all = ffn_back(d_gateup_all, near_ffn.last, 3)
    two = NearSum(lambda k: mm_nt(near_rows(d_gateup_all, k), w_gu))
    r_gu = reduce(block_of(normed_two_all, NC * rows, d_gateup_all))
    two.first, two.near = turn(r_down, two.first, two.near)
    two.near = turn(r_down, two.near)
    two.near = turn(r_gu, two.near)
    two.second, two.near = gate(two.second, two.near)
    grad_normed_two = two.result()
    w_two = norm_back(grad_normed_two, hidden_one, r_h, norm_second)
    g_norm_second = jnp.sum(grad_normed_two * hidden_one * r_h, axis=0)
    grad_hidden_one = grad_final + w_two
    branch_own = grad_hidden_one.astype(BF16)
    branch_own, grad_hidden_one, g_norm_second = gate(branch_own, grad_hidden_one, g_norm_second)
    near_branch = Near(branch_own)
    near_branch.next = turn(r_down, near_branch.next)
    near_branch.next = turn(r_gu, near_branch.next)
    near_branch.next = finish(r_down, near_branch.next)
    (near_branch.far,) = gate(near_branch.far)
    near_branch.cross()
    near_branch.last = turn(r_gu, near_branch.last)
    branch = absolute(near_branch.blocks(), j).reshape(length, MODEL_WIDTH)
    d_acts = mm_nt(branch, w_out)
    grad_attended = d_acts[:, WX:].astype(BF16)
    grad_gated = d_acts[:, :WX]
    grad_ssm_y = grad_gated * silu_z
    d_z = (grad_gated * ssm_y * silu_slope(gate_z)).astype(BF16)
    grad_attended, grad_ssm_y, d_z, branch = gate(grad_attended, grad_ssm_y, d_z, branch)

    def out_part(slot):
        b = home(ring.owner(slot))
        left = jnp.concatenate(
            [
                lax.dynamic_slice_in_dim(gated, b * rows_out, rows_out, axis=1),
                lax.dynamic_slice_in_dim(attended, b * rows_attn, rows_attn, axis=1),
            ],
            axis=1,
        )
        return mm_tn(left, branch)

    r_out = reduce(out_part)

    grad_attended = finish(r_gu, grad_attended)
    dq, dk, dv = attention_backward(queries, keys, values, segc, segr, grad_attended)
    sent = jnp.where(core == 0, dv, dk)
    d_kv_other = core_swap(sent)
    dq, dk, dv, d_kv_other = turn(r_out, dq, dk, dv, d_kv_other)
    d_query = turned(dq, cosine, -sine).astype(BF16)
    d_kv = jnp.where(core == 0, dk, dv) + d_kv_other
    d_kv = jnp.where(core == 0, turned(d_kv, cosine, -sine), d_kv).astype(BF16)
    d_second = jnp.concatenate([d_query, d_kv, d_z], axis=1)
    r_second = reduce(block_of(normed, NC * rows, d_second))

    def collected(run):
        return Collect(run.result.astype(BF16).reshape(NC, rows, run.result.shape[1]), j)

    grad_ssm_y, d_second = turn(r_out, grad_ssm_y, d_second)
    operands = (grad_ssm_y, xs, bmat, cmat, colv, rowv, skip_wide, states)
    dx, dbc, dcol, drow_a = ssd_backward(0, through, *operands)
    col_gu = collected(r_gu)
    dx, dbc, dcol, col_gu.got = turn(r_second, dx, dbc, dcol, col_gu.got)
    col_gu.cross()
    dx, dbc, dcol = turn(r_out, dx, dbc, dcol)
    dx, dbc, dcol, drow_b = ssd_backward(1, through, *operands, (dbc, dcol, dx))
    drow = jnp.concatenate([drow_a[: HEADS // 2], drow_b[: HEADS // 2]], axis=0)
    dx, dbc, dcol, drow = turn(r_second, dx, dbc, dcol, drow)
    dx, dbc, dcol, drow = finish(r_out, dx, dbc, dcol, drow)
    b_sum = NearSum(lambda k: lax.dynamic_index_in_dim(dbc, j ^ k, 0, False))
    g_skip = jnp.sum(jnp.sum(grad_ssm_y * xs, axis=0).reshape(HEADS, P_SIZE), axis=1)
    drow_t = drow.T
    d_cum = dcol[:, :HEADS] - step * drow_t
    d_decay = jnp.einsum(
        "ts,cth->csh", lower, d_cum.reshape(chunks, CHUNK, HEADS), precision=HIGHEST
    ).reshape(length, HEADS)
    d_step = dcol[:, HEADS : 2 * HEADS] + drow_t - rate * d_decay
    d_raw = d_step * jax.nn.sigmoid(step_in)
    g_bias = jnp.sum(d_raw, axis=0)
    g_log = jnp.sum(d_decay * decay, axis=0)

    def conv_back(d_conv, value, taps):
        d_in = taps[0][None] * d_conv
        g_taps = [jnp.sum(d_conv * value, axis=0)]
        for lag in range(1, TAPS):
            masked = d_conv * keeps[lag]
            d_in = d_in + taps[lag][None] * shifted(masked, -lag)
            g_taps.append(jnp.sum(masked * shifted(value, lag), axis=0))
        return d_in.astype(BF16), jnp.stack(g_taps)

    d_in_x, g_taps_x = conv_back(dx * silu_slope(conv_out_x), conv_x.astype(F32), taps_x)
    d_in_x, b_sum.second, b_sum.near, b_sum.first = turn(
        r_second, d_in_x, b_sum.second, b_sum.near, b_sum.first
    )
    conv_b_wide = conv_b_own.astype(F32)
    conv_out_b = convolve(conv_b_wide, taps_b_own, keeps)
    d_in_b, g_taps_b = conv_back(b_sum.result() * silu_slope(conv_out_b), conv_b_wide, taps_b_own)
    d_first = jnp.concatenate(
        [d_in_x, d_in_b, jnp.pad(d_raw.astype(BF16), ((0, 0), (0, 128 - HEADS)))], axis=1
    )
    r_first = reduce(block_of(normed, NC * rows, d_first))
    d_first, d_second = finish(r_second, d_first, d_second)

    def normed_part(k):
        at = (j ^ k) * own
        return mm_nt(lax.dynamic_slice_in_dim(d_first, at, own), w_first) + mm_nt(
            lax.dynamic_slice_in_dim(d_second, at, own), w_second
        )

    back_sum = NearSum(normed_part)
    col_second = collected(r_second)
    back_sum.near, col_second.got = turn(r_first, back_sum.near, col_second.got)
    col_second.cross()
    out_home = lax.ppermute(r_out.result.astype(BF16), ("batch", "ctx"), back).astype(F32)
    back_sum.near = turn(r_first, back_sum.near)
    back_sum.second, back_sum.near = turn(r_first, back_sum.second, back_sum.near)
    grad_normed = back_sum.result()
    g_norm_first = jnp.sum(grad_normed * x * r_x, axis=0)
    grad_tokens = grad_hidden_one + norm_back(grad_normed, x, r_x, norm_first)
    g_norm_first = finish(r_first, g_norm_first)
    col_first = collected(r_first)

    taps_all = jnp.zeros((TAPS, DI + 2 * N), F32)
    taps_all = lax.dynamic_update_slice(taps_all, g_taps_x, (0, j * WX))
    taps_all = lax.dynamic_update_slice(taps_all, g_taps_b, (0, DI + j * WB))
    per_head = lax.dynamic_update_slice(
        jnp.zeros((3, 128), F32), jnp.stack([g_log, g_skip, g_bias]), (0, heads_at)
    )
    small = sum_everywhere(
        jnp.concatenate(
            [
                g_norm_first.reshape(-1, 128),
                g_norm_second.reshape(-1, 128),
                taps_all.reshape(-1, 128),
                per_head,
                jnp.broadcast_to(squares, (1, 128)),
            ]
        ),
        nb,
    )
    lines = MODEL_WIDTH // 128
    g_norm_first = small[:lines].reshape(MODEL_WIDTH)
    g_norm_second = small[lines : 2 * lines].reshape(MODEL_WIDTH)
    taps_all = small[2 * lines : -4].reshape(TAPS, DI + 2 * N)
    per_head = small[-4:-1, :H_M]
    loss_value = small[-1, 0] / (MODEL_WIDTH * count) + order.token[0, 0]
    col_first.cross()

    got_gu = col_gu.result()
    grad_gate_up = (
        got_gu.reshape(NC, rows, 2, nb, unit).transpose(1, 2, 3, 0, 4).reshape(rows, 2 * FF)
    )
    got_second = col_second.result()
    got_first = col_first.result()

    def columns(got, begin, size):
        return got[:, :, begin : begin + size].transpose(1, 0, 2).reshape(rows, NC * size)

    grad_query = columns(got_second, 0, WQ)
    grad_keyval = (
        got_second[:, :, WQ : WQ + HEAD_SIZE]
        .reshape(2, 2, rows, HEAD_SIZE)
        .transpose(2, 1, 0, 3)
        .reshape(rows, 4 * HEAD_SIZE)
    )
    grad_mixer_in = jnp.concatenate(
        [
            columns(got_second, WQ + HEAD_SIZE, WX),
            columns(got_first, 0, WX),
            columns(got_first, WX, WB),
            columns(got_first, WX + WB, HEADS),
        ],
        axis=1,
    )
    output = final.astype(BF16).reshape(tokens.shape)
    return (
        output,
        loss_value,
        grad_tokens.reshape(tokens.shape),
        grad_mixer_in,
        out_home[:rows_out],
        grad_query,
        grad_keyval,
        out_home[rows_out:],
        grad_gate_up,
        r_down.result,
        g_norm_first,
        g_norm_second,
        taps_all,
        per_head[0],
        per_head[1],
        per_head[2],
    )


def solution(mesh):
    split_rows = P(("batch", "ctx"), None)
    by_token = P("batch", "ctx", None)
    return jax.shard_map(
        body,
        mesh=mesh,
        in_specs=(by_token, P("batch", "ctx"), P("batch", "ctx"), by_token)
        + (split_rows,) * 7
        + (P(),) * 6,
        out_specs=(by_token, P(), by_token) + (split_rows,) * 7 + (P(),) * 6,
        check_vma=False,
    )
```

time: 3430 us -> 1010 us (0.29)
  waiting for transfers between devices: 2780 us -> 333 us
  matrix products: 337 us -> 202 us
  starting transfers between devices: 5.18 us -> 135 us
  local copies, waits for them, and re-layouts: 52.6 us -> 168 us
  blocking collectives: 112 us -> 0 us
  Pallas kernels: 0 us -> 60.2 us
    reduce_scatter x9 -> x0, waiting for transfers between devices: 2140 us -> none  [the longest x1 714 us: body(): lax.psum_scatter(outer_rows(normed_two, grad_gateup), ('batch', 'ctx'), s...]
    all_gather x9 -> x0, waiting for transfers between devices: 634 us -> none  [the longest x1 192 us: body(): lax.all_gather(gate_up, ('batch', 'ctx'), axis=0, tiled=True)]
    ppermute x2 -> x146, waiting for transfers between devices: 0.01 us -> 333 us  [the longest x44 194 us: down(): return lax.ppermute(value, 'batch', self.down_pairs)]
    dot_general x39 -> x75, matrix products: 337 us -> 202 us  [the longest x40 95.5 us: mm_tn(): lax.dot_general(left, right, (((0,), (0,)), ((), ())), preferred_element_...]
    ppermute x2 -> x146, starting transfers between devices: 3.59 us -> 135 us  [the longest x44 46.9 us: up(): return lax.ppermute(value, 'batch', self.up_pairs)]
    psum x2 -> x0, blocking collectives: 83 us -> none  [body(): lax.psum((squares, jnp.sum(valid_rows)), ('batch', 'ctx'))]
    pallas_call x0 -> x5, Pallas kernels: none -> 60.2 us  [the longest x2 31.3 us: ssd_backward(): pl.pallas_call(functools.partial(ssd_backward_kernel, part * PAIRS // 2),...]
    dynamic_update_slice x0 -> x95, local copies, waits for them, and re-layouts: none -> 52.2 us  [the longest x54 32.4 us: put(): self.whole = lax.dynamic_update_slice(self.whole, part, (at, 0))]
  transfers between devices with their start and end apart: 20 -> 146, of which waited for: 14 -> 65; matrix products, arithmetic and copies ran while one was open for 12% -> 38% of each run, Pallas kernels for 0% -> 6%
where the time goes in v1:
time: 1010 us; the launch traced here: 996 us
  waiting for transfers between devices  333 us (33%)
  matrix products  202 us (20%)
  local copies, waits for them, and re-layouts  168 us (17%)
  starting transfers between devices  135 us (13%)
  other arithmetic  88.1 us (9%)
  Pallas kernels  60.2 us (6%)
  between operations  10.3 us (1%)
    ppermute x44, waiting for transfers between devices, down(): return lax.ppermute(value, 'batch', self.down_pairs)  194 us
    dot_general x40, matrix products, mm_tn(): lax.dot_general(left, right, (((0,), (0,)), ((), ())), preferred_element_...  95.5 us
    ppermute x19, waiting for transfers between devices, y_swap(): return lax.ppermute(value, 'ctx', [(i, i ^ 2) for i in range(NC)])  76.5 us
    dot_general x17, matrix products, mm_nt(): lax.dot_general(left, right, (((1,), (1,)), ((), ())), preferred_element_...  57.9 us
    ppermute x44, waiting for transfers between devices, up(): return lax.ppermute(value, 'batch', self.up_pairs)  52.8 us
    dot_general x16, matrix products, mm(): return jnp.dot(left, right, preferred_element_type=F32)  48.4 us
    ppermute x44, starting transfers between devices, up(): return lax.ppermute(value, 'batch', self.up_pairs)  46.9 us
    ppermute x44, starting transfers between devices, down(): return lax.ppermute(value, 'batch', self.down_pairs)  46.6 us
  transfers between devices with their start and end apart: 146, of which 65 were waited for; matrix products, arithmetic and copies ran while one was open for 38% of the time, Pallas kernels for 6%

profile of v1, /device:TPU:0, one launch (start us, length us, event | category | flops | bytes accessed | tf_op | source)
XLA Modules:
  0.0 996.2 jit_solution(7198126779557654008)
XLA Ops:
  34.7 5.6 collective-permute-done.3
  59.4 4.4 collective-permute-done.26
  71.6 11.9 %collective-permute-done.11 = bf16[64,1024]{1,0:T(8,128)(2,1)S(1)} collective-permute-done((bf16[64,1024]{1,0:T(8,128)(2,1)S(1)}, bf16[64,1024]{1,0:T(8,128)(2,1)S(1)}, u32[]{:S(2)}, u32[]{:S(2)}) %collective-permute-start.11) | collective-permute-done | bytes 131104 | tf_op jit(solution)/shard_map/ppermute | solution.py:76
  97.4 5.4 collective-permute-start.38
  111.2 20.9 %collective-permute-done.19 = bf16[256,1024]{1,0:T(8,128)(2,1)S(1)} collective-permute-done((bf16[256,1024]{1,0:T(8,128)(2,1)}, bf16[256,1024]{1,0:T(8,128)(2,1)S(1)}, u32[]{:S(2)}, u32[]{:S(2)}) %collective-permute-start.19) | collective-permute-done | bytes 524320 | tf_op jit(solution)/shard_map/ppermute | solution.py:76
  136.2 10.8 %collective-permute-done.27 = bf16[256,1024]{1,0:T(8,128)(2,1)S(1)} collective-permute-done((bf16[256,1024]{1,0:T(8,128)(2,1)S(1)}, bf16[256,1024]{1,0:T(8,128)(2,1)S(1)}, u32[]{:S(2)}, u32[]{:S(2)}) %collective-permute-start.27) | collective-permute-done | bytes 524320 | tf_op jit(solution)/shard_map/ppermute | solution.py:76
  153.6 6.8 collective-permute-done.30
  162.2 13.1 %collective-permute-done.34 = bf16[256,1152]{1,0:T(8,128)(2,1)S(1)} collective-permute-done((bf16[256,1152]{1,0:T(8,128)(2,1)S(1)}, bf16[256,1152]{1,0:T(8,128)(2,1)S(1)}, u32[]{:S(2)}, u32[]{:S(2)}) %collective-permute-start.34) | collective-permute-done | bytes 589856 | tf_op jit(solution)/shard_map/ppermute | solution.py:73
  190.5 5.1 collective-permute-done.35
  201.0 5.3 divide_multiply_fusion
  212.6 9.6 collective-permute-done.41
  257.1 4.2 divide_multiply_fusion.1
  266.5 10.5 %ssd_forward.1 = (f32[1024,768]{1,0:T(8,128)S(1)}, bf16[8,768,256]{2,1,0:T(8,128)(2,1)S(1)}) custom-call(f32[8,12]{1,0:T(8,128)S(1)} %fusion.257.thr.refs_0_, f32[1024,768]{1,0:T(8,128)S(1)} %get-tuple-element.401.x_ref.refs_2_, f32[1024,256]{1,0:T(8,128)S(1)} %get-tuple-element.402.b_ref.refs_3_, f32[1024,256]{1,0:T(8,128)S(1)} %get-tuple-element.403.c_ref.refs_4_, ...), custom_call_target="tpu_custom_call" | custom-call | tf_op jit(solution)/shard_map/ssd_forward/pallas_call | solution.py:394
  283.3 7.9 fusion.298
  298.8 7.3 attention_forward.1
  312.1 4.6 convolution_convert_fusion.5
  325.0 10.9 %collective-permute-done.50 = bf16[256,2048]{1,0:T(8,128)(2,1)} collective-permute-done((bf16[256,2048]{1,0:T(8,128)(2,1)}, bf16[256,2048]{1,0:T(8,128)(2,1)}, u32[]{:S(2)}, u32[]{:S(2)}) %collective-permute-start.50) | collective-permute-done | bytes 1048608 | tf_op jit(solution)/shard_map/ppermute | solution.py:76
  338.8 7.4 collective-permute-done.57
  355.1 6.2 collective-permute-done.58
  362.0 13.3 %collective-permute-done.61 = bf16[256,2048]{1,0:T(8,128)(2,1)S(1)} collective-permute-done((bf16[256,2048]{1,0:T(8,128)(2,1)S(1)}, bf16[256,2048]{1,0:T(8,128)(2,1)S(1)}, u32[]{:S(2)}, u32[]{:S(2)}) %collective-permute-start.61) | collective-permute-done | bytes 1048608 | tf_op jit(solution)/shard_map/ppermute | solution.py:59
  384.8 16.5 %collective-permute-done.64 = bf16[256,2048]{1,0:T(8,128)(2,1)S(1)} collective-permute-done((bf16[256,2048]{1,0:T(8,128)(2,1)S(1)}, bf16[256,2048]{1,0:T(8,128)(2,1)S(1)}, u32[]{:S(2)}, u32[]{:S(2)}) %collective-permute-start.64) | collective-permute-done | bytes 1048608 | tf_op jit(solution)/shard_map/ppermute | solution.py:76
  405.6 12.2 %collective-permute-done.67 = bf16[128,2048]{1,0:T(8,128)(2,1)S(1)} collective-permute-done((bf16[128,2048]{1,0:T(8,128)(2,1)S(1)}, bf16[128,2048]{1,0:T(8,128)(2,1)S(1)}, u32[]{:S(2)}, u32[]{:S(2)}) %collective-permute-start.67) | collective-permute-done | bytes 524320 | tf_op jit(solution)/shard_map/ppermute | solution.py:76
  471.1 16.4 %collective-permute-done.77 = bf16[256,2048]{1,0:T(8,128)(2,1)S(1)} collective-permute-done((bf16[256,2048]{1,0:T(8,128)(2,1)S(1)}, bf16[256,2048]{1,0:T(8,128)(2,1)S(1)}, u32[]{:S(2)}, u32[]{:S(2)}) %collective-permute-start.77) | collective-permute-done | bytes 1048608 | tf_op jit(solution)/shard_map/ppermute | solution.py:59
  501.7 12.9 %collective-permute-done.78 = bf16[256,2048]{1,0:T(8,128)(2,1)} collective-permute-done((bf16[256,2048]{1,0:T(8,128)(2,1)S(1)}, bf16[256,2048]{1,0:T(8,128)(2,1)}, u32[]{:S(2)}, u32[]{:S(2)}) %collective-permute-start.78) | collective-permute-done | bytes 1048608 | tf_op jit(solution)/shard_map/ppermute | solution.py:59
  528.9 4.6 convolution_convert_fusion.6
  540.6 4.4 convolution_convert_fusion.1
  553.8 4.6 convolution_convert_fusion.7
  566.7 4.9 fusion.6
  572.5 7.5 collective-permute-done.89
  588.6 8.0 collective-permute-done.82
  608.4 9.3 collective-permute-done.91
  643.7 11.8 %collective-permute-done.99 = bf16[256,2048]{1,0:T(8,128)(2,1)S(1)} collective-permute-done((bf16[256,2048]{1,0:T(8,128)(2,1)S(1)}, bf16[256,2048]{1,0:T(8,128)(2,1)S(1)}, u32[]{:S(2)}, u32[]{:S(2)}) %collective-permute-start.99) | collective-permute-done | bytes 1048608 | tf_op jit(solution)/shard_map/ppermute | solution.py:76
  658.7 4.5 fusion.274
  665.1 4.5 add_convert_fusion.2
  682.3 13.0 %collective-permute-done.104 = bf16[256,2048]{1,0:T(8,128)(2,1)S(1)} collective-permute-done((bf16[256,2048]{1,0:T(8,128)(2,1)S(1)}, bf16[256,2048]{1,0:T(8,128)(2,1)S(1)}, u32[]{:S(2)}, u32[]{:S(2)}) %collective-permute-start.104) | collective-permute-done | bytes 1048608 | tf_op jit(solution)/shard_map/ppermute | solution.py:76
  695.3 4.5 collective-permute-done.103
  699.9 11.1 %attention_backward.1 = (f32[1024,256]{1,0:T(8,128)S(1)}, f32[1024,128]{1,0:T(8,128)S(1)}, f32[1024,128]{1,0:T(8,128)S(1)}) custom-call(bf16[1024,256]{1,0:T(8,128)(2,1)S(1)} %copy-done.21, bf16[1024,128]{1,0:T(8,128)(2,1)S(1)} %copy-done.25, bf16[1024,128]{1,0:T(8,128)(2,1)S(1)} %copy-done.23, s32[1024,1]{1,0:T(8,128)S(1)} %copy-done.19, ...), custom_call_target="tpu_custom_call" | custom-call | tf_op jit(solution)/shard_map/attention_backward/pallas_call | solution.py:500
  727.3 5.2 collective-permute-done.109
  734.8 15.6 %ssd_backward.2 = (f32[1024,768]{1,0:T(8,128)S(1)}, f32[4,1024,128]{2,1,0:T(8,128)S(1)}, f32[1024,128]{1,0:T(8,128)S(1)}, f32[8,1024]{1,0:T(8,128)S(1)}) custom-call(f32[8,12]{1,0:T(8,128)S(1)} %copy-done.35, f32[1024,768]{1,0:T(8,128)S(1)} %get-tuple-element.542.refs_1_, f32[1024,768]{1,0:T(8,128)} %copy-done, f32[1024,256]{1,0:T(8,128)S(1)} %copy-done.8, ...), custom_call_target="tpu_custom_call" | custom-call | tf_op jit(solution)/shard_map/ssd_backward/pallas_call | solution.py:416
  764.5 5.9 collective-permute-done.114
  792.1 15.7 %ssd_backward.3 = (f32[1024,768]{1,0:T(8,128)S(1)}, f32[4,1024,128]{2,1,0:T(8,128)S(1)}, f32[1024,128]{1,0:T(8,128)S(1)}, f32[8,1024]{1,0:T(8,128)S(1)}) custom-call(f32[8,12]{1,0:T(8,128)S(1)} %copy-done.35, f32[1024,768]{1,0:T(8,128)S(1)} %copy-done.3, f32[1024,768]{1,0:T(8,128)} %copy-done, ...), custom_call_target="tpu_custom_call", output_to_operand_aliasing={{0}: (11, {})} | custom-call | tf_op jit(solution)/shard_map/ssd_backward/pallas_call | solution.py:416
  817.9 5.5 collective-permute-start.144
  829.2 4.7 multiply_reduce_fusion.3
  845.7 5.6 add_convert_fusion
  912.9 6.1 collective-permute-done.128
  936.1 6.1 collective-permute-done.129
  942.2 7.4 collective-permute-done.132
  957.7 5.8 collective-permute-done.134
  (1150 shorter events, 580.4 us)
Async XLA Ops:
  34.3 32.7 %collective-permute-start.10 = (bf16[2,64,1152]{2,1,0:T(8,128)(2,1)}, bf16[2,64,1152]{2,1,0:T(8,128)(2,1)}, u32[]{:S(2)}, u32[]{:S(2)}) collective-permute-start(bf16[2,64,1152]{2,1,0:T(8,128)(2,1)} %pad_maximum_fusion.26), channel_id=1, source_target_pairs={{0,2},{1,3},{2,0},{3,1},{4,6},{5,7},{6,4},{7,5},{8,10},{9,11},{10,... | collective-permute-start | bytes 884744 | tf_op jit(solution)/shard_map/ppermute | solution.py:59
  41.5 25.5 %collective-permute-start.7 = (bf16[128,1024]{1,0:T(8,128)(2,1)}, bf16[128,1024]{1,0:T(8,128)(2,1)S(1)}, u32[]{:S(2)}, u32[]{:S(2)}) collective-permute-start(bf16[128,1024]{1,0:T(8,128)(2,1)} %collective-permute-done.4), channel_id=1, source_target_pairs={{0,8},{8,16},{16,24},{24,28},{28,20},{20,12},{12,4},{4,0},{1,9},{9... | collective-permute-start | bytes 786440 | tf_op jit(solution)/shard_map/ppermute | solution.py:73
  66.1 27.6 %collective-permute-start.13 = (bf16[256,1024]{1,0:T(8,128)(2,1)}, bf16[256,1024]{1,0:T(8,128)(2,1)}, u32[]{:S(2)}, u32[]{:S(2)}) collective-permute-start(bf16[256,1024]{1,0:T(8,128)(2,1)} %bitcast.11), channel_id=1, source_target_pairs={{8,0},{16,8},{24,16},{28,24},{20,28},{12,20},{4,12},{0,4},{9,1},{1... | collective-permute-start | bytes 1572872 | tf_op jit(solution)/shard_map/ppermute | solution.py:76
  66.1 36.7 %collective-permute-start.15 = (bf16[256,2048]{1,0:T(8,128)(2,1)S(1)}, bf16[256,2048]{1,0:T(8,128)(2,1)}, u32[]{:S(2)}, u32[]{:S(2)}) collective-permute-start(bf16[256,2048]{1,0:T(8,128)(2,1)S(1)} %multiply_convert_fusion.3), channel_id=1, source_target_pairs={{0,2},{1,3},{2,0},{3,1},{4,6},{5,7},{6,4},{7,5},{8,10},{9,11},{10,... | collective-permute-start | bytes 3145736 | tf_op jit(solution)/shard_map/ppermute | solution.py:59
  67.0 35.8 %collective-permute-start.16 = (bf16[256,2048]{1,0:T(8,128)(2,1)S(1)}, bf16[256,2048]{1,0:T(8,128)(2,1)}, u32[]{:S(2)}, u32[]{:S(2)}) collective-permute-start(bf16[256,2048]{1,0:T(8,128)(2,1)S(1)} %multiply_convert_fusion.3), channel_id=1, source_target_pairs={{0,1},{1,0},{2,3},{3,2},{4,5},{5,4},{6,7},{7,6},{8,9},{9,8},{10,11... | collective-permute-start | bytes 3145736 | tf_op jit(solution)/shard_map/ppermute | solution.py:55
  93.6 42.6 %collective-permute-start.29 = (bf16[2,64,2048]{2,1,0:T(8,128)(2,1)S(1)}, bf16[2,64,2048]{2,1,0:T(8,128)(2,1)S(1)}, u32[]{:S(2)}, u32[]{:S(2)}) collective-permute-start(bf16[2,64,2048]{2,1,0:T(8,128)(2,1)S(1)} %pad_maximum_fusion.11), channel_id=1, source_target_pairs={{0,2},{1,3},{2,0},{3,1},{4,6},{5,7},{6,4},{7,5},{8,10},{9,11},{10,... | collective-permute-start | bytes 1572872 | tf_op jit(solution)/shard_map/ppermute | solution.py:59
  97.4 93.1 %collective-permute-start.38 = (bf16[128,2048]{1,0:T(8,128)(2,1)}, bf16[128,2048]{1,0:T(8,128)(2,1)}, u32[]{:S(2)}, u32[]{:S(2)}) collective-permute-start(bf16[128,2048]{1,0:T(8,128)(2,1)} %pad_maximum_fusion.15), channel_id=1, source_target_pairs={{0,0},{1,16},{2,8},{3,24},{4,4},{5,20},{6,12},{7,28},{8,1},{9,17},... | collective-permute-start | bytes 1572872 | tf_op jit(solution)/shard_map/ppermute | solution.py:644
  102.8 29.3 %collective-permute-start.21 = (bf16[256,2048]{1,0:T(8,128)(2,1)}, bf16[256,2048]{1,0:T(8,128)(2,1)S(1)}, u32[]{:S(2)}, u32[]{:S(2)}) collective-permute-start(bf16[256,2048]{1,0:T(8,128)(2,1)} %collective-permute-done.15), channel_id=1, source_target_pairs={{0,1},{1,0},{2,3},{3,2},{4,5},{5,4},{6,7},{7,6},{8,9},{9,8},{10,11... | collective-permute-start | bytes 3145736 | tf_op jit(solution)/shard_map/ppermute | solution.py:55
  102.9 29.3 %collective-permute-start.19 = (bf16[256,1024]{1,0:T(8,128)(2,1)}, bf16[256,1024]{1,0:T(8,128)(2,1)S(1)}, u32[]{:S(2)}, u32[]{:S(2)}) collective-permute-start(bf16[256,1024]{1,0:T(8,128)(2,1)} %collective-permute-done.13), channel_id=1, source_target_pairs={{8,0},{16,8},{24,16},{28,24},{20,28},{12,20},{4,12},{0,4},{9,1},{1... | collective-permute-start | bytes 1572872 | tf_op jit(solution)/shard_map/ppermute | solution.py:76
  103.4 28.7 %collective-permute-start.20 = (bf16[256,1024]{1,0:T(8,128)(2,1)}, bf16[256,1024]{1,0:T(8,128)(2,1)S(1)}, u32[]{:S(2)}, u32[]{:S(2)}) collective-permute-start(bf16[256,1024]{1,0:T(8,128)(2,1)} %collective-permute-done.14), channel_id=1, source_target_pairs={{0,8},{8,16},{16,24},{24,28},{28,20},{20,12},{12,4},{4,0},{1,9},{9... | collective-permute-start | bytes 1572872 | tf_op jit(solution)/shard_map/ppermute | solution.py:73
  136.1 26.1 %collective-permute-start.33 = (bf16[256,1152]{1,0:T(8,128)(2,1)S(1)}, bf16[256,1152]{1,0:T(8,128)(2,1)S(1)}, u32[]{:S(2)}, u32[]{:S(2)}) collective-permute-start(bf16[256,1152]{1,0:T(8,128)(2,1)S(1)} %bitcast.376), channel_id=1, source_target_pairs={{8,0},{16,8},{24,16},{28,24},{20,28},{12,20},{4,12},{0,4},{9,1},{1... | collective-permute-start | bytes 1769480 | tf_op jit(solution)/shard_map/ppermute | solution.py:76
  196.7 65.0 %collective-permute-start.39 = (bf16[128,2048]{1,0:T(8,128)(2,1)}, bf16[128,2048]{1,0:T(8,128)(2,1)}, u32[]{:S(2)}, u32[]{:S(2)}) collective-permute-start(bf16[128,2048]{1,0:T(8,128)(2,1)} %collective-permute-done.38), channel_id=1, source_target_pairs={{8,0},{16,8},{24,16},{28,24},{20,28},{12,20},{4,12},{0,4},{9,1},{1... | collective-permute-start | bytes 1572872 | tf_op jit(solution)/shard_map/ppermute | solution.py:76
  198.5 63.1 %collective-permute-start.40 = (bf16[128,2048]{1,0:T(8,128)(2,1)}, bf16[128,2048]{1,0:T(8,128)(2,1)}, u32[]{:S(2)}, u32[]{:S(2)}) collective-permute-start(bf16[128,2048]{1,0:T(8,128)(2,1)} %collective-permute-done.38), channel_id=1, source_target_pairs={{0,8},{8,16},{16,24},{24,28},{28,20},{20,12},{12,4},{4,0},{1,9},{9... | collective-permute-start | bytes 1572872 | tf_op jit(solution)/shard_map/ppermute | solution.py:73
  310.1 25.9 %collective-permute-start.50 = (bf16[256,2048]{1,0:T(8,128)(2,1)}, bf16[256,2048]{1,0:T(8,128)(2,1)}, u32[]{:S(2)}, u32[]{:S(2)}) collective-permute-start(bf16[256,2048]{1,0:T(8,128)(2,1)} %bitcast.26), channel_id=1, source_target_pairs={{8,0},{16,8},{24,16},{28,24},{20,28},{12,20},{4,12},{0,4},{9,1},{1... | collective-permute-start | bytes 3145736 | tf_op jit(solution)/shard_map/ppermute | solution.py:76
  311.2 25.5 %collective-permute-start.51 = (bf16[256,2048]{1,0:T(8,128)(2,1)}, bf16[256,2048]{1,0:T(8,128)(2,1)}, u32[]{:S(2)}, u32[]{:S(2)}) collective-permute-start(bf16[256,2048]{1,0:T(8,128)(2,1)} %bitcast.26), channel_id=1, source_target_pairs={{0,8},{8,16},{16,24},{24,28},{28,20},{20,12},{12,4},{4,0},{1,9},{9... | collective-permute-start | bytes 3145736 | tf_op jit(solution)/shard_map/ppermute | solution.py:73
  320.5 25.7 %collective-permute-start.57 = (bf16[256,2048]{1,0:T(8,128)(2,1)}, bf16[256,2048]{1,0:T(8,128)(2,1)}, u32[]{:S(2)}, u32[]{:S(2)}) collective-permute-start(bf16[256,2048]{1,0:T(8,128)(2,1)} %fusion.8), channel_id=1, source_target_pairs={{0,2},{1,3},{2,0},{3,1},{4,6},{5,7},{6,4},{7,5},{8,10},{9,11},{10,... | collective-permute-start | bytes 3145736 | tf_op jit(solution)/shard_map/ppermute | solution.py:59
  349.8 25.6 %collective-permute-start.61 = (bf16[256,2048]{1,0:T(8,128)(2,1)S(1)}, bf16[256,2048]{1,0:T(8,128)(2,1)S(1)}, u32[]{:S(2)}, u32[]{:S(2)}) collective-permute-start(bf16[256,2048]{1,0:T(8,128)(2,1)S(1)} %multiply_convert_fusion.2), channel_id=1, source_target_pairs={{0,2},{1,3},{2,0},{3,1},{4,6},{5,7},{6,4},{7,5},{8,10},{9,11},{10,... | collective-permute-start | bytes 3145736 | tf_op jit(solution)/shard_map/ppermute | solution.py:59
  375.3 26.0 %collective-permute-start.64 = (bf16[256,2048]{1,0:T(8,128)(2,1)S(1)}, bf16[256,2048]{1,0:T(8,128)(2,1)S(1)}, u32[]{:S(2)}, u32[]{:S(2)}) collective-permute-start(bf16[256,2048]{1,0:T(8,128)(2,1)S(1)} %collective-permute-done.58), channel_id=1, source_target_pairs={{8,0},{16,8},{24,16},{28,24},{20,28},{12,20},{4,12},{0,4},{9,1},{1... | collective-permute-start | bytes 3145736 | tf_op jit(solution)/shard_map/ppermute | solution.py:76
  376.4 26.0 %collective-permute-start.65 = (bf16[256,2048]{1,0:T(8,128)(2,1)S(1)}, bf16[256,2048]{1,0:T(8,128)(2,1)S(1)}, u32[]{:S(2)}, u32[]{:S(2)}) collective-permute-start(bf16[256,2048]{1,0:T(8,128)(2,1)S(1)} %collective-permute-done.59), channel_id=1, source_target_pairs={{0,8},{8,16},{16,24},{24,28},{28,20},{20,12},{12,4},{4,0},{1,9},{9... | collective-permute-start | bytes 3145736 | tf_op jit(solution)/shard_map/ppermute | solution.py:73
  382.5 38.6 %collective-permute-start.62 = (bf16[128,1024]{1,0:T(8,128)(2,1)S(1)}, bf16[128,1024]{1,0:T(8,128)(2,1)S(1)}, u32[]{:S(2)}, u32[]{:S(2)}) collective-permute-start(bf16[128,1024]{1,0:T(8,128)(2,1)S(1)} %copy-done.139), channel_id=1, source_target_pairs={{8,0},{16,8},{24,16},{28,24},{20,28},{12,20},{4,12},{0,4},{9,1},{1... | collective-permute-start | bytes 786440 | tf_op jit(solution)/shard_map/ppermute | solution.py:76
  383.6 37.5 %collective-permute-start.63 = (bf16[128,1024]{1,0:T(8,128)(2,1)S(1)}, bf16[128,1024]{1,0:T(8,128)(2,1)S(1)}, u32[]{:S(2)}, u32[]{:S(2)}) collective-permute-start(bf16[128,1024]{1,0:T(8,128)(2,1)S(1)} %copy-done.139), channel_id=1, source_target_pairs={{0,8},{8,16},{16,24},{24,28},{28,20},{20,12},{12,4},{4,0},{1,9},{9... | collective-permute-start | bytes 786440 | tf_op jit(solution)/shard_map/ppermute | solution.py:73
  459.0 28.5 %collective-permute-start.75 = (bf16[256,2048]{1,0:T(8,128)(2,1)S(1)}, bf16[256,2048]{1,0:T(8,128)(2,1)S(1)}, u32[]{:S(2)}, u32[]{:S(2)}) collective-permute-start(bf16[256,2048]{1,0:T(8,128)(2,1)S(1)} %convolution_convert_fusion.3), channel_id=1, source_target_pairs={{0,1},{1,0},{2,3},{3,2},{4,5},{5,4},{6,7},{7,6},{8,9},{9,8},{10,11... | collective-permute-start | bytes 3145736 | tf_op jit(solution)/shard_map/ppermute | solution.py:55
  462.2 25.3 %collective-permute-start.77 = (bf16[256,2048]{1,0:T(8,128)(2,1)S(1)}, bf16[256,2048]{1,0:T(8,128)(2,1)S(1)}, u32[]{:S(2)}, u32[]{:S(2)}) collective-permute-start(bf16[256,2048]{1,0:T(8,128)(2,1)S(1)} %add_convert_fusion.6), channel_id=1, source_target_pairs={{0,2},{1,3},{2,0},{3,1},{4,6},{5,7},{6,4},{7,5},{8,10},{9,11},{10,... | collective-permute-start | bytes 3145736 | tf_op jit(solution)/shard_map/ppermute | solution.py:59
  489.7 25.0 %collective-permute-start.78 = (bf16[256,2048]{1,0:T(8,128)(2,1)S(1)}, bf16[256,2048]{1,0:T(8,128)(2,1)}, u32[]{:S(2)}, u32[]{:S(2)}) collective-permute-start(bf16[256,2048]{1,0:T(8,128)(2,1)S(1)} %fusion.22), channel_id=1, source_target_pairs={{0,2},{1,3},{2,0},{3,1},{4,6},{5,7},{6,4},{7,5},{8,10},{9,11},{10,... | collective-permute-start | bytes 3145736 | tf_op jit(solution)/shard_map/ppermute | solution.py:59
  551.3 28.7 %collective-permute-start.83 = (bf16[128,2048]{1,0:T(8,128)(2,1)}, bf16[128,2048]{1,0:T(8,128)(2,1)}, u32[]{:S(2)}, u32[]{:S(2)}) collective-permute-start(bf16[128,2048]{1,0:T(8,128)(2,1)} %get-tuple-element.704), channel_id=1, source_target_pairs={{0,8},{8,16},{16,24},{24,28},{28,20},{20,12},{12,4},{4,0},{1,9},{9... | collective-permute-start | bytes 1572872 | tf_op jit(solution)/shard_map/ppermute | solution.py:73
  552.5 28.4 %collective-permute-start.84 = (bf16[128,2048]{1,0:T(8,128)(2,1)}, bf16[128,2048]{1,0:T(8,128)(2,1)}, u32[]{:S(2)}, u32[]{:S(2)}) collective-permute-start(bf16[128,2048]{1,0:T(8,128)(2,1)} %get-tuple-element.703), channel_id=1, source_target_pairs={{8,0},{16,8},{24,16},{28,24},{20,28},{12,20},{4,12},{0,4},{9,1},{1... | collective-permute-start | bytes 1572872 | tf_op jit(solution)/shard_map/ppermute | solution.py:76
  571.6 25.0 %collective-permute-start.82 = (bf16[256,2048]{1,0:T(8,128)(2,1)}, bf16[256,2048]{1,0:T(8,128)(2,1)S(1)}, u32[]{:S(2)}, u32[]{:S(2)}) collective-permute-start(bf16[256,2048]{1,0:T(8,128)(2,1)} %fusion.6), channel_id=1, source_target_pairs={{0,2},{1,3},{2,0},{3,1},{4,6},{5,7},{6,4},{7,5},{8,10},{9,11},{10,... | collective-permute-start | bytes 3145736 | tf_op jit(solution)/shard_map/ppermute | solution.py:59
  582.4 37.1 %collective-permute-start.96 = (bf16[256,2048]{1,0:T(8,128)(2,1)S(1)}, bf16[256,2048]{1,0:T(8,128)(2,1)S(1)}, u32[]{:S(2)}, u32[]{:S(2)}) collective-permute-start(bf16[256,2048]{1,0:T(8,128)(2,1)S(1)} %pad_maximum_fusion.7), channel_id=1, source_target_pairs={{8,0},{16,8},{24,16},{28,24},{20,28},{12,20},{4,12},{0,4},{9,1},{1... | collective-permute-start | bytes 3145736 | tf_op jit(solution)/shard_map/ppermute | solution.py:76
  584.6 34.9 %collective-permute-start.95 = (bf16[256,2048]{1,0:T(8,128)(2,1)S(1)}, bf16[256,2048]{1,0:T(8,128)(2,1)S(1)}, u32[]{:S(2)}, u32[]{:S(2)}) collective-permute-start(bf16[256,2048]{1,0:T(8,128)(2,1)S(1)} %pad_maximum_fusion.6), channel_id=1, source_target_pairs={{0,8},{8,16},{16,24},{24,28},{28,20},{20,12},{12,4},{4,0},{1,9},{9... | collective-permute-start | bytes 3145736 | tf_op jit(solution)/shard_map/ppermute | solution.py:73
  587.7 29.9 %collective-permute-start.91 = (bf16[128,2048]{1,0:T(8,128)(2,1)S(1)}, bf16[128,2048]{1,0:T(8,128)(2,1)S(1)}, u32[]{:S(2)}, u32[]{:S(2)}) collective-permute-start(bf16[128,2048]{1,0:T(8,128)(2,1)S(1)} %fusion.19), channel_id=1, source_target_pairs={{8,0},{16,8},{24,16},{28,24},{20,28},{12,20},{4,12},{0,4},{9,1},{1... | collective-permute-start | bytes 1572872 | tf_op jit(solution)/shard_map/ppermute | solution.py:76
  628.5 27.0 %collective-permute-start.99 = (bf16[256,2048]{1,0:T(8,128)(2,1)S(1)}, bf16[256,2048]{1,0:T(8,128)(2,1)S(1)}, u32[]{:S(2)}, u32[]{:S(2)}) collective-permute-start(bf16[256,2048]{1,0:T(8,128)(2,1)S(1)} %add_convert_fusion.4), channel_id=1, source_target_pairs={{8,0},{16,8},{24,16},{28,24},{20,28},{12,20},{4,12},{0,4},{9,1},{1... | collective-permute-start | bytes 3145736 | tf_op jit(solution)/shard_map/ppermute | solution.py:76
  669.7 25.6 %collective-permute-start.104 = (bf16[256,2048]{1,0:T(8,128)(2,1)S(1)}, bf16[256,2048]{1,0:T(8,128)(2,1)S(1)}, u32[]{:S(2)}, u32[]{:S(2)}) collective-permute-start(bf16[256,2048]{1,0:T(8,128)(2,1)S(1)} %add_convert_fusion.2), channel_id=1, source_target_pairs={{8,0},{16,8},{24,16},{28,24},{20,28},{12,20},{4,12},{0,4},{9,1},{1... | collective-permute-start | bytes 3145736 | tf_op jit(solution)/shard_map/ppermute | solution.py:76
  674.7 25.1 %collective-permute-start.103 = (bf16[256,2048]{1,0:T(8,128)(2,1)S(1)}, bf16[256,2048]{1,0:T(8,128)(2,1)S(1)}, u32[]{:S(2)}, u32[]{:S(2)}) collective-permute-start(bf16[256,2048]{1,0:T(8,128)(2,1)S(1)} %add_convert_fusion.3), channel_id=1, source_target_pairs={{0,8},{8,16},{16,24},{24,28},{28,20},{20,12},{12,4},{4,0},{1,9},{9... | collective-permute-start | bytes 3145736 | tf_op jit(solution)/shard_map/ppermute | solution.py:73
  676.4 36.1 %collective-permute-start.101 = (bf16[64,2048]{1,0:T(8,128)(2,1)S(1)}, bf16[64,2048]{1,0:T(8,128)(2,1)S(1)}, u32[]{:S(2)}, u32[]{:S(2)}) collective-permute-start(bf16[64,2048]{1,0:T(8,128)(2,1)S(1)} %get-tuple-element.745), channel_id=1, source_target_pairs={{0,8},{8,16},{16,24},{24,28},{28,20},{20,12},{12,4},{4,0},{1,9},{9... | collective-permute-start | bytes 786440 | tf_op jit(solution)/shard_map/ppermute | solution.py:73
  677.8 34.7 %collective-permute-start.102 = (bf16[64,2048]{1,0:T(8,128)(2,1)S(1)}, bf16[64,2048]{1,0:T(8,128)(2,1)S(1)}, u32[]{:S(2)}, u32[]{:S(2)}) collective-permute-start(bf16[64,2048]{1,0:T(8,128)(2,1)S(1)} %get-tuple-element.744), channel_id=1, source_target_pairs={{8,0},{16,8},{24,16},{28,24},{20,28},{12,20},{4,12},{0,4},{9,1},{1... | collective-permute-start | bytes 786440 | tf_op jit(solution)/shard_map/ppermute | solution.py:76
  712.0 38.5 %collective-permute-start.110 = (bf16[2,64,2048]{2,1,0:T(8,128)(2,1)S(1)}, bf16[2,64,2048]{2,1,0:T(8,128)(2,1)S(1)}, u32[]{:S(2)}, u32[]{:S(2)}) collective-permute-start(bf16[2,64,2048]{2,1,0:T(8,128)(2,1)S(1)} %pad_maximum_fusion.22), channel_id=1, source_target_pairs={{0,1},{1,0},{2,3},{3,2},{4,5},{5,4},{6,7},{7,6},{8,9},{9,8},{10,11... | collective-permute-start | bytes 1572872 | tf_op jit(solution)/shard_map/ppermute | solution.py:55
  720.8 29.7 %collective-permute-start.106 = (bf16[128,1152]{1,0:T(8,128)(2,1)}, bf16[128,1152]{1,0:T(8,128)(2,1)S(1)}, u32[]{:S(2)}, u32[]{:S(2)}) collective-permute-start(bf16[128,1152]{1,0:T(8,128)(2,1)} %get-tuple-element.718), channel_id=1, source_target_pairs={{0,8},{8,16},{16,24},{24,28},{28,20},{20,12},{12,4},{4,0},{1,9},{9... | collective-permute-start | bytes 884744 | tf_op jit(solution)/shard_map/ppermute | solution.py:73
  721.5 29.0 %collective-permute-start.107 = (bf16[128,1152]{1,0:T(8,128)(2,1)}, bf16[128,1152]{1,0:T(8,128)(2,1)}, u32[]{:S(2)}, u32[]{:S(2)}) collective-permute-start(bf16[128,1152]{1,0:T(8,128)(2,1)} %get-tuple-element.717), channel_id=1, source_target_pairs={{8,0},{16,8},{24,16},{28,24},{20,28},{12,20},{4,12},{0,4},{9,1},{1... | collective-permute-start | bytes 884744 | tf_op jit(solution)/shard_map/ppermute | solution.py:76
  760.8 47.1 %collective-permute-start.112 = (bf16[256,1152]{1,0:T(8,128)(2,1)}, bf16[256,1152]{1,0:T(8,128)(2,1)}, u32[]{:S(2)}, u32[]{:S(2)}) collective-permute-start(bf16[256,1152]{1,0:T(8,128)(2,1)} %pad_maximum_fusion.10), channel_id=1, source_target_pairs={{8,0},{16,8},{24,16},{28,24},{20,28},{12,20},{4,12},{0,4},{9,1},{1... | collective-permute-start | bytes 1769480 | tf_op jit(solution)/shard_map/ppermute | solution.py:76
  762.8 45.1 %collective-permute-start.111 = (bf16[256,1152]{1,0:T(8,128)(2,1)}, bf16[256,1152]{1,0:T(8,128)(2,1)}, u32[]{:S(2)}, u32[]{:S(2)}) collective-permute-start(bf16[256,1152]{1,0:T(8,128)(2,1)} %pad_maximum_fusion.9), channel_id=1, source_target_pairs={{0,8},{8,16},{16,24},{24,28},{28,20},{20,12},{12,4},{4,0},{1,9},{9... | collective-permute-start | bytes 1769480 | tf_op jit(solution)/shard_map/ppermute | solution.py:73
  783.5 33.4 %collective-permute-start.118 = (bf16[128,2048]{1,0:T(8,128)(2,1)}, bf16[128,2048]{1,0:T(8,128)(2,1)S(1)}, u32[]{:S(2)}, u32[]{:S(2)}) collective-permute-start(bf16[128,2048]{1,0:T(8,128)(2,1)} %add_convert_fusion.8), channel_id=1, source_target_pairs={{8,0},{16,8},{24,16},{28,24},{20,28},{12,20},{4,12},{0,4},{9,1},{1... | collective-permute-start | bytes 1572872 | tf_op jit(solution)/shard_map/ppermute | solution.py:76
  788.1 28.8 %collective-permute-start.117 = (bf16[128,2048]{1,0:T(8,128)(2,1)S(1)}, bf16[128,2048]{1,0:T(8,128)(2,1)S(1)}, u32[]{:S(2)}, u32[]{:S(2)}) collective-permute-start(bf16[128,2048]{1,0:T(8,128)(2,1)S(1)} %add_convert_fusion.9), channel_id=1, source_target_pairs={{0,8},{8,16},{16,24},{24,28},{28,20},{20,12},{12,4},{4,0},{1,9},{9... | collective-permute-start | bytes 1572872 | tf_op jit(solution)/shard_map/ppermute | solution.py:73
  811.8 39.6 %collective-permute-start.116 = (bf16[256,1152]{1,0:T(8,128)(2,1)}, bf16[256,1152]{1,0:T(8,128)(2,1)}, u32[]{:S(2)}, u32[]{:S(2)}) collective-permute-start(bf16[256,1152]{1,0:T(8,128)(2,1)} %fusion.12), channel_id=1, source_target_pairs={{8,0},{16,8},{24,16},{28,24},{20,28},{12,20},{4,12},{0,4},{9,1},{1... | collective-permute-start | bytes 1769480 | tf_op jit(solution)/shard_map/ppermute | solution.py:76
  815.8 35.6 %collective-permute-start.115 = (bf16[256,1152]{1,0:T(8,128)(2,1)}, bf16[256,1152]{1,0:T(8,128)(2,1)}, u32[]{:S(2)}, u32[]{:S(2)}) collective-permute-start(bf16[256,1152]{1,0:T(8,128)(2,1)} %fusion.11), channel_id=1, source_target_pairs={{0,8},{8,16},{16,24},{24,28},{28,20},{20,12},{12,4},{4,0},{1,9},{9... | collective-permute-start | bytes 1769480 | tf_op jit(solution)/shard_map/ppermute | solution.py:73
  817.9 54.6 %collective-permute-start.144 = (bf16[128,2048]{1,0:T(8,128)(2,1)}, bf16[128,2048]{1,0:T(8,128)(2,1)}, u32[]{:S(2)}, u32[]{:S(2)}) collective-permute-start(bf16[128,2048]{1,0:T(8,128)(2,1)} %add_convert_fusion.7), channel_id=1, source_target_pairs={{0,0},{16,1},{8,2},{24,3},{4,4},{20,5},{12,6},{28,7},{1,8},{17,9},... | collective-permute-start | bytes 1572872 | tf_op jit(solution)/shard_map/ppermute | solution.py:962
  867.7 36.0 %collective-permute-start.122 = (bf16[128,1024]{1,0:T(8,128)(2,1)}, bf16[128,1024]{1,0:T(8,128)(2,1)}, u32[]{:S(2)}, u32[]{:S(2)}) collective-permute-start(bf16[128,1024]{1,0:T(8,128)(2,1)} %get-tuple-element.737), channel_id=1, source_target_pairs={{0,8},{8,16},{16,24},{24,28},{28,20},{20,12},{12,4},{4,0},{1,9},{9... | collective-permute-start | bytes 786440 | tf_op jit(solution)/shard_map/ppermute | solution.py:73
  867.7 36.0 %collective-permute-start.123 = (bf16[128,1024]{1,0:T(8,128)(2,1)}, bf16[128,1024]{1,0:T(8,128)(2,1)}, u32[]{:S(2)}, u32[]{:S(2)}) collective-permute-start(bf16[128,1024]{1,0:T(8,128)(2,1)} %get-tuple-element.736), channel_id=1, source_target_pairs={{8,0},{16,8},{24,16},{28,24},{20,28},{12,20},{4,12},{0,4},{9,1},{1... | collective-permute-start | bytes 786440 | tf_op jit(solution)/shard_map/ppermute | solution.py:76
  912.3 43.3 %collective-permute-start.135 = (bf16[256,2048]{1,0:T(8,128)(2,1)}, bf16[256,2048]{1,0:T(8,128)(2,1)S(1)}, u32[]{:S(2)}, u32[]{:S(2)}) collective-permute-start(bf16[256,2048]{1,0:T(8,128)(2,1)} %fusion.10), channel_id=1, source_target_pairs={{0,1},{1,0},{2,3},{3,2},{4,5},{5,4},{6,7},{7,6},{8,9},{9,8},{10,11... | collective-permute-start | bytes 3145736 | tf_op jit(solution)/shard_map/ppermute | solution.py:55
  (319 other events, 3885.4 us)

commit v2 on v1

v2 whole, which is shorter than its diff:
```python
import functools

import jax
import jax.numpy as jnp
from jax import lax
from jax.experimental import pallas as pl
from jax.experimental.pallas import tpu as pltpu
from jax.sharding import PartitionSpec as P

MODEL_WIDTH = 2048
H_M = 48
P_SIZE = 64
N = 256
QUERY_HEADS = 8
KEY_VALUE_HEADS = 2
HEAD_SIZE = 128
FF = 4096
TAPS = 4
DI = 3072

NC = 4
HEADS = H_M // NC
PAIRS = HEADS // 2
WX = DI // NC
WB = 2 * N // NC
WQ = QUERY_HEADS * HEAD_SIZE // NC
QH = QUERY_HEADS // NC
WF = FF // NC
CHUNK = 128

NORM_EPSILON = 1e-05
ROPE_BASE = 1000000.0
HIGHEST = lax.Precision.HIGHEST
F32 = jnp.float32
BF16 = jnp.bfloat16


def mm(left, right):
    return jnp.dot(left, right, preferred_element_type=F32)


def mm_tn(left, right):
    return lax.dot_general(left, right, (((0,), (0,)), ((), ())), preferred_element_type=F32)


def mm_nt(left, right):
    return lax.dot_general(left, right, (((1,), (1,)), ((), ())), preferred_element_type=F32)


def after(value, *deps):
    return lax.optimization_barrier((value,) + deps)[0]


def core_swap(value):
    return lax.ppermute(value, "ctx", [(i, i ^ 1) for i in range(NC)])


def y_swap(value):
    return lax.ppermute(value, "ctx", [(i, i ^ 2) for i in range(NC)])


class Ring:
    def __init__(self):
        self.n = lax.axis_size("batch")
        n = self.n
        order = list(range(0, n, 2)) + list(range(n - 1, 0, -2))
        self.up_pairs = [(order[i], order[(i + 1) % n]) for i in range(n)]
        self.down_pairs = [(order[(i + 1) % n], order[i]) for i in range(n)]
        b = lax.axis_index("batch")
        self.pos = jnp.where(b % 2 == 0, b // 2, n - 1 - b // 2)

    def up(self, value):
        return lax.ppermute(value, "batch", self.up_pairs)

    def down(self, value):
        return lax.ppermute(value, "batch", self.down_pairs)

    def owner(self, slot):
        p = (self.pos + slot + self.n) % self.n
        return jnp.where(p < self.n // 2, 2 * p, 2 * (self.n - 1 - p) + 1)


class Order:
    def __init__(self, token):
        self.token = token

    def gate(self, *values):
        out = lax.optimization_barrier(values + (self.token,))
        self.token = out[-1]
        return out[:-1]


class GatherRun:
    def __init__(self, ring, order, block, place=lambda b: b):
        self.ring, self.order, self.place = ring, order, place
        self.rows, cols = block.shape
        (block,) = order.gate(block)
        self.down, self.up = ring.down(block), ring.up(block)
        self.whole = jnp.zeros((ring.n * self.rows, cols), block.dtype)
        self.put(block, 0)
        self.step, self.over = 1, False

    def put(self, part, slot, offset=0):
        at = self.place(self.ring.owner(slot)) * self.rows + offset
        self.whole = lax.dynamic_update_slice(self.whole, part, (at, 0))

    def turn(self, others):
        ring, far, half = self.ring, self.ring.n // 2, self.rows // 2
        down, up, *others = self.order.gate(self.down, self.up, *others)
        if self.step < far:
            if self.step + 1 < far:
                self.down, self.up = ring.down(down), ring.up(up)
            else:
                self.down, self.up = ring.down(down[half:]), ring.up(up[:half])
            self.put(down, self.step)
            self.put(up, -self.step)
        else:
            self.put(up, far)
            self.put(down, far, half)
            self.over = True
        self.step += 1
        return others


class ReduceRun:
    def __init__(self, ring, order, part):
        self.ring, self.order, self.part = ring, order, part
        far = part(ring.n // 2)
        (far,) = order.gate(far)
        self.half = far.shape[0] // 2
        self.up, self.down = ring.up(far[: self.half]), ring.down(far[self.half :])
        self.step, self.over = ring.n // 2 - 1, False

    def turn(self, others):
        half = self.half
        up, down, *others = self.order.gate(self.up, self.down, *others)
        up, down = up.astype(F32), down.astype(F32)
        if self.step == 0:
            self.result = self.part(0).astype(F32) + up + down
            self.over = True
            return others
        a, b = self.part(self.step), self.part(-self.step)
        if self.step == self.ring.n // 2 - 1:
            a = lax.dynamic_update_slice(a, (a[:half].astype(F32) + up).astype(BF16), (0, 0))
            b = lax.dynamic_update_slice(b, (b[half:].astype(F32) + down).astype(BF16), (half, 0))
        else:
            a = (a.astype(F32) + up).astype(BF16)
            b = (b.astype(F32) + down).astype(BF16)
        self.up, self.down = self.ring.up(a), self.ring.down(b)
        self.step -= 1
        return others


def sum_everywhere(value, batch):
    value = value + core_swap(value)
    value = value + y_swap(value)
    bit = 1
    while bit < batch:
        value = value + lax.ppermute(value, "batch", [(i, i ^ bit) for i in range(batch)])
        bit *= 2
    return value


class Spread:
    def __init__(self, parts, j):
        self.parts, self.j = parts, j
        self.got = y_swap(jnp.stack([parts[j ^ 2], parts[j ^ 3]]))

    def cross(self):
        self.across = core_swap(jnp.stack([self.parts[self.j ^ 1], self.got[1]]))

    def block(self):
        blocks = [self.parts[self.j], self.across[0], self.got[0], self.across[1]]
        whole = absolute(blocks, self.j)
        return whole.reshape(NC * whole.shape[1], whole.shape[2])


class Collect:
    def __init__(self, block, j):
        self.block, self.j = block, j
        self.got = core_swap(jnp.stack([block[j ^ 1], block[j ^ 3]]))

    def cross(self):
        self.far = y_swap(jnp.stack([self.block[self.j ^ 2], self.got[1]]))

    def result(self):
        whole = absolute([self.block[self.j], self.got[0], self.far[0], self.far[1]], self.j)
        return whole.astype(F32)


def absolute(blocks, j):
    whole = jnp.zeros((NC,) + blocks[0].shape, blocks[0].dtype)
    for k in range(NC):
        whole = lax.dynamic_update_slice(
            whole, blocks[k][None], (j ^ k,) + (0,) * blocks[0].ndim
        )
    return whole


def stacked(blocks):
    size = blocks[0].shape[0]
    whole = jnp.zeros((len(blocks) * size,) + blocks[0].shape[1:], blocks[0].dtype)
    for k, block in enumerate(blocks):
        whole = lax.dynamic_update_slice_in_dim(whole, block, k * size, 0)
    return whole


class Near:
    def __init__(self, own):
        self.own, self.far, self.next = own, y_swap(own), core_swap(own)

    def cross(self):
        self.last = core_swap(self.far)

    def blocks(self):
        return [self.own, self.next, self.far, self.last]


class NearSum:
    def __init__(self, part, at, between=None):
        self.part, self.at = part, at
        self.away = part(True)
        self.third = core_swap(self.away[1 - at].astype(BF16))
        if between is None:
            self.go()
            self.stay()

    def go(self):
        self.second = y_swap((self.away[self.at] + self.third.astype(F32)).astype(BF16))

    def stay(self):
        home = self.part(False)
        self.first = core_swap(home[1 - self.at].astype(BF16))
        self.near = home[self.at]

    def result(self):
        return self.near + self.first.astype(F32) + self.second.astype(F32)


PAIR = 2 * P_SIZE
EDGE = 8


def halves(first, second, lanes):
    return jnp.where(lanes < P_SIZE, first, second)


def step_values(raw, bias, log, marks):
    rows = lax.broadcasted_iota(jnp.int32, (CHUNK, CHUNK), 0)
    cols = lax.broadcasted_iota(jnp.int32, (CHUNK, CHUNK), 1)
    value = raw + bias
    step = jnp.maximum(value, 0.0) + jnp.log1p(jnp.exp(-jnp.abs(value)))
    decay = -jnp.exp(log) * step
    lower = (rows >= cols).astype(F32)
    cum = jnp.dot(lower, decay, precision=HIGHEST, preferred_element_type=F32)
    end = cum[CHUNK - 1 :, :]
    seg, before, last = marks[:, 0:1], marks[:, 1:2], marks[:, 2:3]
    reach = jnp.where(seg == before, jnp.exp(cum), 0.0)
    bare = jnp.where(seg == last, jnp.exp(end - cum), 0.0)
    through = jnp.where(last[:1] == before[:1], jnp.exp(end), 0.0)
    return value, step, decay, cum, reach, bare, through


def convolved(buf, taps, marks, width):
    total = taps[0:1, :width] * buf[EDGE : EDGE + CHUNK, :width]
    for lag in range(1, TAPS):
        moved = buf[EDGE - lag : EDGE - lag + CHUNK, :width]
        total = total + taps[lag : lag + 1, :width] * moved * marks[:, 2 + lag : 3 + lag]
    return total


def ssd_forward_kernel(
    x_ref, bc_ref, raw_ref, bias_ref, log_ref, taps_ref, tapsb_ref, mark_ref, row_ref, skip_ref,
    y_ref, st_ref, conv_ref, act_ref, step_ref, reach_ref, bare_ref, cum_ref, cumt_ref, end_ref,
    state, buf, bufb
):
    @pl.when(pl.program_id(0) == 0)
    def _():
        state[...] = jnp.zeros_like(state)
        buf[...] = jnp.zeros_like(buf)
        bufb[...] = jnp.zeros_like(bufb)

    marks = mark_ref[...]
    for b_, ref in ((buf, x_ref), (bufb, bc_ref)):
        b_[0:EDGE, :] = b_[CHUNK : CHUNK + EDGE, :]
        b_[EDGE : EDGE + CHUNK, :] = ref[...].astype(F32)
    conv = convolved(bufb, tapsb_ref, marks, 2 * N)
    bc = (conv * jax.nn.sigmoid(conv)).astype(BF16)
    act_ref[...] = bc
    b, c = bc[:, :N], bc[:, N:]
    _, step, _, cum, reach, bare, through = step_values(
        raw_ref[...], bias_ref[...], log_ref[...], marks
    )
    weight = bare * step
    cum_rows = cum.T
    step_ref[...], reach_ref[...], bare_ref[...], cum_ref[...] = step, reach, bare, cum
    cumt_ref[...] = cum_rows[:16, :]
    end_ref[...] = jnp.broadcast_to(through, (8, 128))
    rows = lax.broadcasted_iota(jnp.int32, (CHUNK, CHUNK), 0)
    cols = lax.broadcasted_iota(jnp.int32, (CHUNK, CHUNK), 1)
    allowed = (marks[:, 0:1] == row_ref[0:1, :]) & (rows >= cols)
    inner = mm_nt(c, b)
    lanes = lax.broadcasted_iota(jnp.int32, (CHUNK, PAIR), 1)
    subs = lax.broadcasted_iota(jnp.int32, (PAIR, N), 0)
    for p in range(PAIRS):
        span = slice(PAIR * p, PAIR * (p + 1))
        h = 2 * p

        def pick(value):
            return halves(value[:, h : h + 1], value[:, h + 1 : h + 2], lanes)

        conv = taps_ref[0:1, span] * buf[EDGE : EDGE + CHUNK, span]
        for lag in range(1, TAPS):
            moved = buf[EDGE - lag : EDGE - lag + CHUNK, span]
            conv = conv + taps_ref[lag : lag + 1, span] * moved * marks[:, 2 + lag : 3 + lag]
        conv_ref[:, span] = conv
        x = conv * jax.nn.sigmoid(conv)
        scaled = (x * pick(step)).astype(BF16)
        local = []
        for q in (h, h + 1):
            spread = cum[:, q : q + 1] - cum_rows[q : q + 1, :]
            mixing = jnp.exp(jnp.where(allowed, spread, -1e30)) * inner
            local.append(mm(mixing.astype(BF16), scaled))
        held = state[span, :]
        hb = held.astype(BF16)
        st_ref[0, span, :] = hb
        y_ref[:, span] = (
            halves(local[0], local[1], lanes) + pick(reach) * mm_nt(c, hb) + skip_ref[:, span] * x
        )
        tail = mm_tn((pick(weight) * x).astype(BF16), b)
        kept = jnp.where(subs < P_SIZE, through[:, h : h + 1], through[:, h + 1 : h + 2])
        state[span, :] = kept * held + tail


def ssd_backward_kernel(first, *refs):
    (g_ref, x_ref, xp_ref, conv_ref, act_ref, step_ref, reach_ref, bare_ref), refs = refs[:8], refs[8:]
    (cum_ref, cumt_ref, end_ref, st_ref, raw_ref, bias_ref, log_ref), refs = refs[:7], refs[7:]
    (taps_ref, _, mark_ref, row_ref, skip_ref), refs = refs[:5], refs[5:]
    if first:
        (dbc_in, draw_in, _), refs = refs[:3], refs[3:]
    dx_ref, dbc_ref, draw_ref, sums_ref, tsums_ref, later, buf, ahead_buf = refs

    @pl.when(pl.program_id(0) == 0)
    def _():
        later[...] = jnp.zeros_like(later)
        sums_ref[...] = jnp.zeros_like(sums_ref)
        tsums_ref[...] = jnp.zeros_like(tsums_ref)
        ahead_buf[...] = jnp.zeros_like(ahead_buf)

    marks = mark_ref[...]
    buf[0:EDGE, :] = xp_ref[CHUNK - 2 * EDGE :, :].astype(F32)[EDGE:, :]
    buf[EDGE : EDGE + CHUNK, :] = x_ref[...].astype(F32)
    b, c = act_ref[:, :N], act_ref[:, N:]
    step, reach, bare, cum = step_ref[...], reach_ref[...], bare_ref[...], cum_ref[...]
    cum_rows, through = cumt_ref[...], end_ref[0:1, :]
    weight = bare * step
    rows = lax.broadcasted_iota(jnp.int32, (CHUNK, CHUNK), 0)
    cols = lax.broadcasted_iota(jnp.int32, (CHUNK, CHUNK), 1)
    allowed = (marks[:, 0:1] == row_ref[0:1, :]) & (rows >= cols)
    inner = mm_nt(c, b)
    lanes = lax.broadcasted_iota(jnp.int32, (CHUNK, PAIR), 1)
    subs = lax.broadcasted_iota(jnp.int32, (PAIR, N), 0)
    wide = lax.broadcasted_iota(jnp.int32, (CHUNK, 128), 1)
    last = lax.broadcasted_iota(jnp.int32, (CHUNK, 1), 0) == CHUNK - 1
    d_inner = jnp.zeros((CHUNK, CHUNK), F32)
    db = jnp.zeros((CHUNK, N), F32)
    dc = jnp.zeros((CHUNK, N), F32)
    d_cum = jnp.zeros((CHUNK, 128), F32)
    d_step = jnp.zeros((CHUNK, 128), F32)
    ahead_buf[CHUNK : CHUNK + EDGE, :] = ahead_buf[0:EDGE, :]
    count = range(PAIRS // 2)
    spans = [slice(PAIR * p, PAIR * (p + 1)) for p in count]

    def picked(value):
        return [
            halves(value[:, h : h + 1], value[:, h + 1 : h + 2], lanes)
            for h in (2 * (p + first) for p in count)
        ]

    conv = [conv_ref[:, span] for span in spans]
    g = [g_ref[:, span] for span in spans]
    start = [st_ref[0, span, :] for span in spans]
    ahead = [later[span, :].astype(BF16) for span in spans]
    bs = [mm_nt(b, a) for a in ahead]
    cs = [mm_nt(c, a) for a in start]
    sg = [jax.nn.sigmoid(v) for v in conv]
    x = [v * w for v, w in zip(conv, sg)]
    step2, reach2, weight2, bare2 = picked(step), picked(reach), picked(weight), picked(bare)
    scaled = [(v * w).astype(BF16) for v, w in zip(x, step2)]
    e = []
    for q in range(PAIRS):
        spread = cum[:, 2 * first + q : 2 * first + q + 1] - cum_rows[2 * first + q : 2 * first + q + 1, :]
        e.append(jnp.exp(jnp.where(allowed, spread, -1e30)))
    d_mix = []
    for p in count:
        for q in (0, 1):
            mine = (lanes >= P_SIZE) if q else (lanes < P_SIZE)
            d_mix.append(mm_nt(jnp.where(mine, g[p], 0.0).astype(BF16), scaled[p]))
    mixing = [v * inner for v in e]
    local = [mm_tn(mixing[q].astype(BF16), g[q // 2].astype(BF16)) for q in range(PAIRS)]
    totals = []
    for q in range(PAIRS):
        d_inner = d_inner + d_mix[q] * e[q]
        totals.append(jnp.sum(d_mix[q] * mixing[q], axis=1, keepdims=True))
    local = [halves(local[2 * p], local[2 * p + 1], lanes) for p in count]
    gr = [(v * w).astype(BF16) for v, w in zip(reach2, g)]
    wx = [(v * w).astype(BF16) for v, w in zip(weight2, x)]
    for p in count:
        dc = dc + mm(gr[p], start[p])
        db = db + mm(wx[p], ahead[p])
    for p in count:
        h = 2 * (p + first)
        held = later[spans[p], :]
        product = held * start[p].astype(F32)
        kept = jnp.where(subs < P_SIZE, through[:, h : h + 1], through[:, h + 1 : h + 2])
        later[spans[p], :] = kept * held + mm_tn(gr[p], c)
        xbs = x[p] * bs[p]
        xl = x[p] * local[p]
        stored = xbs * weight2[p]
        direct = xbs * bare2[p] + xl
        change = g[p] * cs[p] * reach2[p] - stored - xl * step2[p]
        for q in (0, 1):
            mine = (lanes >= P_SIZE) if q else (lanes < P_SIZE)
            half = slice(P_SIZE * q, P_SIZE * (q + 1))
            stored_sum = jnp.sum(jnp.sum(stored, axis=0, keepdims=True)[:, half], keepdims=True)
            held_sum = jnp.sum(jnp.sum(product[half], axis=0, keepdims=True), keepdims=True)
            end = stored_sum + through[:, h + q : h + q + 1] * held_sum
            cum_q = totals[2 * p + q] + jnp.sum(jnp.where(mine, change, 0.0), axis=1, keepdims=True)
            cum_q = cum_q + jnp.where(last, end, 0.0)
            step_q = jnp.sum(jnp.where(mine, direct, 0.0), axis=1, keepdims=True)
            d_cum = jnp.where(wide == h + q, cum_q, d_cum)
            d_step = jnp.where(wide == h + q, step_q, d_step)
    d_conv = []
    for p in count:
        span = spans[p]
        dx = local[p] * step2[p] + weight2[p] * bs[p] + skip_ref[:, span] * g[p]
        d_conv.append(dx * sg[p] * (1.0 + conv[p] * (1.0 - sg[p])))
        ahead_buf[0:CHUNK, span] = d_conv[p]
    for p in count:
        span = spans[p]
        d_in = taps_ref[0:1, span] * d_conv[p]
        for lag in range(1, TAPS):
            d_in = d_in + taps_ref[lag : lag + 1, span] * (
                ahead_buf[lag : lag + CHUNK, span] * marks[:, 5 + lag : 6 + lag]
            )
        dx_ref[:, span] = d_in.astype(BF16)
        for lag in range(TAPS):
            moved = buf[EDGE - lag : EDGE - lag + CHUNK, span]
            if lag:
                moved = moved * marks[:, 2 + lag : 3 + lag]
            tsums_ref[lag : lag + 1, span] += jnp.sum(d_conv[p] * moved, axis=0, keepdims=True)
        tsums_ref[TAPS : TAPS + 1, span] += jnp.sum(g[p] * x[p], axis=0, keepdims=True)
    di = d_inner.astype(BF16)
    db = db + mm_tn(di, c)
    dc = dc + mm(di, b)
    for q, part in enumerate((db[:, :WB], db[:, WB:], dc[:, :WB], dc[:, WB:])):
        dbc_ref[q] = part + dbc_in[q] if first else part
    upper = (cols >= rows).astype(F32)
    d_decay = jnp.dot(upper, d_cum, precision=HIGHEST, preferred_element_type=F32)
    rate = jnp.exp(log_ref[...])
    d_raw = (d_step - rate * d_decay) * jax.nn.sigmoid(raw_ref[...] + bias_ref[...])
    sums_ref[0:1, :] += jnp.sum(d_raw, axis=0, keepdims=True)
    sums_ref[1:2, :] -= jnp.sum(d_decay * (rate * step), axis=0, keepdims=True)
    draw_ref[...] = d_raw + draw_in[...] if first else d_raw


def ssd_specs(chunks, flip, width, part):
    def at(i):
        return chunks - 1 - i if flip else i

    def rowwise(size, col=0):
        return pl.BlockSpec((CHUNK, size), lambda i: (at(i), col))

    def fixed(height, size, col=0):
        return pl.BlockSpec((height, size), lambda i: (0, col))

    def behind(size, col=0):
        return pl.BlockSpec((CHUNK, size), lambda i: (jnp.maximum(at(i) - 1, 0), col))

    def across(height):
        return pl.BlockSpec((height, CHUNK), lambda i: (0, at(i)))

    states = pl.BlockSpec((1, width, N), lambda i: (at(i), part, 0))
    dbc = pl.BlockSpec((NC, CHUNK, WB), lambda i: (0, at(i), 0))
    end = pl.BlockSpec((8, 128), lambda i: (at(i), 0))
    kept = [rowwise(width, part), rowwise(2 * N)] + [rowwise(128)] * 4 + [across(16), end]
    tail = [
        rowwise(128), fixed(1, 128), fixed(1, 128), fixed(TAPS, width, part), fixed(TAPS, 2 * N),
        rowwise(16), across(8), fixed(1, width, part),
    ]
    return rowwise, fixed, behind, states, dbc, kept, tail


def ssd_forward(x, bc, *rest):
    tokens = x.shape[0]
    chunks = tokens // CHUNK
    rowwise, _, _, states, _, kept, tail = ssd_specs(chunks, False, WX, 0)
    by_token = jax.ShapeDtypeStruct((tokens, 128), F32)
    y, states, *saved = pl.pallas_call(
        ssd_forward_kernel,
        grid=(chunks,),
        in_specs=[rowwise(WX), rowwise(2 * N)] + tail,
        out_specs=[rowwise(WX), states] + kept,
        out_shape=[
            jax.ShapeDtypeStruct((tokens, WX), F32),
            jax.ShapeDtypeStruct((chunks, WX, N), BF16),
            jax.ShapeDtypeStruct((tokens, WX), F32),
            jax.ShapeDtypeStruct((tokens, 2 * N), BF16),
            by_token,
            by_token,
            by_token,
            by_token,
            jax.ShapeDtypeStruct((16, tokens), F32),
            jax.ShapeDtypeStruct((8 * chunks, 128), F32),
        ],
        scratch_shapes=[
            pltpu.VMEM((WX, N), F32),
            pltpu.VMEM((CHUNK + EDGE, WX), F32),
            pltpu.VMEM((CHUNK + EDGE, 2 * N), F32),
        ],
        compiler_params=pltpu.CompilerParams(
            dimension_semantics=("arbitrary",), vmem_limit_bytes=40 << 20
        ),
        name="ssd_forward",
    )(x, bc, *rest)
    return y, (*saved, states)


def ssd_backward(part, g, x, saved, rest, earlier=()):
    tokens = x.shape[0]
    chunks = tokens // CHUNK
    half = WX // 2
    rowwise, fixed, behind, st, dbc, kept, tail = ssd_specs(chunks, True, half, part)
    extra = [dbc, rowwise(128), pl.BlockSpec(memory_space=pl.ANY)] if part else []
    return pl.pallas_call(
        functools.partial(ssd_backward_kernel, part * PAIRS // 2),
        grid=(chunks,),
        in_specs=[rowwise(half, part), rowwise(half, part), behind(half, part)]
        + kept
        + [st]
        + tail
        + extra,
        out_specs=[rowwise(half, part), dbc, rowwise(128), fixed(8, 128), fixed(8, half)],
        out_shape=[
            jax.ShapeDtypeStruct((tokens, WX), BF16),
            jax.ShapeDtypeStruct((NC, tokens, WB), F32),
            jax.ShapeDtypeStruct((tokens, 128), F32),
            jax.ShapeDtypeStruct((8, 128), F32),
            jax.ShapeDtypeStruct((8, half), F32),
        ],
        scratch_shapes=[
            pltpu.VMEM((half, N), F32),
            pltpu.VMEM((CHUNK + EDGE, half), F32),
            pltpu.VMEM((CHUNK + EDGE, half), F32),
        ],
        input_output_aliases={22: 0} if part else {},
        compiler_params=pltpu.CompilerParams(
            dimension_semantics=("arbitrary",), vmem_limit_bytes=40 << 20
        ),
        name="ssd_backward",
    )(g, x, x, *saved, *rest, *earlier)


Q_BLOCK = 256
SCALE = HEAD_SIZE ** (-0.5)


def attention_probs(q, k, segc, segr, i):
    scores = mm_nt(q, k) * SCALE
    rows = lax.broadcasted_iota(jnp.int32, scores.shape, 0) + i * Q_BLOCK
    cols = lax.broadcasted_iota(jnp.int32, scores.shape, 1)
    scores = jnp.where((rows >= cols) & (segc == segr), scores, -1e30)
    grown = jnp.exp(scores - jnp.max(scores, axis=-1, keepdims=True))
    return grown / jnp.sum(grown, axis=-1, keepdims=True)


def attention_forward_kernel(q_ref, k_ref, v_ref, segc_ref, segr_ref, o_ref):
    probs = attention_probs(q_ref[...], k_ref[...], segc_ref[...], segr_ref[...], pl.program_id(1))
    o_ref[...] = mm(probs.astype(BF16), v_ref[...]).astype(BF16)


def attention_backward_kernel(
    q_ref, k_ref, v_ref, segc_ref, segr_ref, g_ref, dq_ref, dk_ref, dv_ref
):
    @pl.when((pl.program_id(0) == 0) & (pl.program_id(1) == 0))
    def _():
        dk_ref[...] = jnp.zeros_like(dk_ref)
        dv_ref[...] = jnp.zeros_like(dv_ref)

    q, k, g = q_ref[...], k_ref[...], g_ref[...]
    probs = attention_probs(q, k, segc_ref[...], segr_ref[...], pl.program_id(1))
    d_probs = mm_nt(g, v_ref[...])
    inner = jnp.sum(probs * d_probs, axis=-1, keepdims=True)
    d_scores = (probs * (d_probs - inner)).astype(BF16)
    dq_ref[...] = mm(d_scores, k) * SCALE
    dk_ref[...] += mm_tn(d_scores, q) * SCALE
    dv_ref[...] += mm_tn(probs.astype(BF16), g)


def attention_specs(tokens):
    block = pl.BlockSpec((Q_BLOCK, HEAD_SIZE), lambda h, i: (i, h))
    whole = pl.BlockSpec((tokens, HEAD_SIZE), lambda h, i: (0, 0))
    segc = pl.BlockSpec((Q_BLOCK, 1), lambda h, i: (i, 0))
    segr = pl.BlockSpec((1, tokens), lambda h, i: (0, 0))
    params = pltpu.CompilerParams(
        dimension_semantics=("arbitrary", "arbitrary"), vmem_limit_bytes=32 << 20
    )
    return block, whole, segc, segr, params


def attention_forward(q, k, v, segc, segr):
    tokens = q.shape[0]
    block, whole, sc, sr, params = attention_specs(tokens)
    return pl.pallas_call(
        attention_forward_kernel,
        grid=(QH, tokens // Q_BLOCK),
        in_specs=[block, whole, whole, sc, sr],
        out_specs=block,
        out_shape=jax.ShapeDtypeStruct((tokens, QH * HEAD_SIZE), BF16),
        compiler_params=params,
        name="attention_forward",
    )(q, k, v, segc, segr)


def attention_backward(q, k, v, segc, segr, g):
    tokens = q.shape[0]
    block, whole, sc, sr, params = attention_specs(tokens)
    return pl.pallas_call(
        attention_backward_kernel,
        grid=(QH, tokens // Q_BLOCK),
        in_specs=[block, whole, whole, sc, sr, block],
        out_specs=[block, whole, whole],
        out_shape=[
            jax.ShapeDtypeStruct((tokens, QH * HEAD_SIZE), F32),
            jax.ShapeDtypeStruct((tokens, HEAD_SIZE), F32),
            jax.ShapeDtypeStruct((tokens, HEAD_SIZE), F32),
        ],
        compiler_params=params,
        name="attention_backward",
    )(q, k, v, segc, segr, g)


def rms_of(rows):
    return lax.rsqrt(jnp.mean(rows * rows, axis=-1, keepdims=True) + NORM_EPSILON)


def norm_back(grad, rows, r, gain):
    w = grad * gain
    return r * w - rows * (r * r * r) * jnp.mean(w * rows, axis=-1, keepdims=True)


def silu_slope(value):
    sg = jax.nn.sigmoid(value)
    return sg * (1.0 + value * (1.0 - sg))


def turned(heads, cosine, sine):
    half = HEAD_SIZE // 2
    parts = []
    for h in range(heads.shape[1] // HEAD_SIZE):
        v = heads[:, h * HEAD_SIZE : (h + 1) * HEAD_SIZE]
        parts.append(v * cosine + jnp.concatenate([v[:, half:], v[:, :half]], axis=1) * sine)
    return jnp.concatenate(parts, axis=1)


def shifted(value, lag):
    if lag == 0:
        return value
    zeros = jnp.zeros((abs(lag), value.shape[1]), value.dtype)
    if lag > 0:
        return jnp.concatenate([zeros, value[:-lag]], axis=0)
    return jnp.concatenate([value[-lag:], zeros], axis=0)


def convolve(value, taps, keeps):
    total = taps[0][None] * value
    for lag in range(1, TAPS):
        total = total + taps[lag][None] * shifted(value, lag) * keeps[lag]
    return total


def body(
    tokens,
    segment_ids,
    valid_mask,
    teacher,
    mixer_in,
    mixer_out,
    query_weight,
    key_value_weight,
    output_weight,
    gate_up,
    down_weight,
    norm_first,
    norm_second,
    conv_taps,
    decay_log,
    skip_gain,
    step_bias,
):
    ring = Ring()
    nb = ring.n
    j = lax.axis_index("ctx")
    own = tokens.shape[0] * tokens.shape[1]
    length = own * NC
    devices = nb * NC
    total_tokens = float(own * devices)
    x = tokens.reshape(own, MODEL_WIDTH).astype(F32)
    valid = valid_mask.reshape(own).astype(F32)
    target = teacher.reshape(own, MODEL_WIDTH).astype(F32)

    order = Order(jnp.broadcast_to(valid[:1] * 0.0, (8, 128)))
    gate, scale = order.gate, max(1, nb // 8)

    def turn(run, *others):
        for _ in range(scale):
            if not run.over:
                others = run.turn(others)
        return others[0] if len(others) == 1 else others

    def finish(run, *others):
        while not run.over:
            others = run.turn(others)
        return others[0] if len(others) == 1 else others

    def start(block, place=lambda b: b):
        return GatherRun(ring, order, block, place)

    rows = mixer_in.shape[0]
    edge = 2 * DI + 2 * N
    unit = down_weight.shape[0]
    near_seg = Near(segment_ids.reshape(1, own))
    g_down = start(down_weight)
    rows_out, rows_attn = mixer_out.shape[0], output_weight.shape[0]

    def home(q):
        return (q % 2) * 4 + q // 2 % 2 * 2 + q // 4 if nb == 8 else q

    there = [(m, home(m % nb) * NC + m // nb) for m in range(devices)]
    back = [(b, a) for a, b in there]
    both_out = lax.ppermute(
        jnp.concatenate([mixer_out, output_weight], axis=0), ("batch", "ctx"), there
    )
    xs_cols = mixer_in[:, DI : 2 * DI].reshape(rows, NC, WX)
    bc_cols = mixer_in[:, 2 * DI : edge].reshape(rows, NC, WB)
    dt_cols = mixer_in[:, edge:].reshape(rows, NC, HEADS)
    digits = jnp.sum(valid)
    digits = jnp.stack([jnp.floor(digits / 64.0), digits % 64.0]).astype(BF16)
    shape = (rows, NC, 128 - HEADS)
    lane = lax.broadcasted_iota(jnp.int32, shape, 2) - (126 - HEADS)
    lane = jnp.where(lax.broadcasted_iota(jnp.int32, shape, 0) == 0, lane, -1)
    padding = jnp.where(lane == 0, digits[0], jnp.where(lane == 1, digits[1], 0))
    dt_cols = jnp.concatenate([dt_cols, padding.astype(BF16)], axis=2)
    first_cols = jnp.concatenate([xs_cols, bc_cols, dt_cols], axis=2).transpose(1, 0, 2)
    spread = Spread(first_cols, j)
    spread.got, mixer_in, query_weight, key_value_weight, x, near_seg.far, near_seg.next = turn(
        g_down, spread.got, mixer_in, query_weight, key_value_weight, x, near_seg.far,
        near_seg.next
    )
    spread.cross()
    near_seg.cross()
    z_cols = mixer_in[:, :DI].reshape(rows, NC, WX)
    q_cols = query_weight.reshape(rows, NC, WQ)
    kv = key_value_weight.reshape(rows, 2, 2, HEAD_SIZE)
    kv_cols = kv.transpose(0, 2, 1, 3).reshape(rows, NC, HEAD_SIZE)
    second_cols = jnp.concatenate([q_cols, kv_cols, z_cols], axis=2).transpose(1, 0, 2)
    spread_two = Spread(second_cols, j)
    (spread.across, x) = gate(spread.across, x)
    g_first = start(spread.block())
    r_x = rms_of(x)
    normed_own = (x * r_x * norm_first).astype(BF16)
    near_normed = Near(normed_own)
    spread_two.got, near_normed.next = turn(g_down, spread_two.got, near_normed.next)
    spread_two.cross()
    gate_up, both_out = turn(g_first, gate_up, both_out)
    spread_two.across = turn(g_down, spread_two.across)
    gu_cols = (
        gate_up.reshape(rows, 2, nb, NC, unit).transpose(3, 0, 1, 2, 4).reshape(NC, rows, 2 * WF)
    )
    spread_gu = Spread(gu_cols, j)
    near_normed.far, near_seg.last = turn(g_first, near_normed.far, near_seg.last)
    near_normed.cross()
    g_second = start(spread_two.block())
    (near_normed.last,) = gate(near_normed.last)
    normed = absolute(near_normed.blocks(), j).reshape(length, MODEL_WIDTH)
    place = jnp.arange(length, dtype=jnp.int32)
    normed, conv_taps, decay_log, skip_gain, step_bias, place = finish(
        g_down, normed, conv_taps, decay_log, skip_gain, step_bias, place
    )
    w_down = g_down.whole

    seg = absolute(near_seg.blocks(), j).reshape(length)
    keeps, marks_ahead = [None], []
    for lag in range(1, TAPS):
        before = jnp.concatenate([jnp.full((lag,), -1, jnp.int32), seg[:-lag]])
        after_it = jnp.concatenate([seg[lag:], jnp.full((lag,), -1, jnp.int32)])
        keeps.append((before == seg).astype(F32))
        marks_ahead.append((after_it == seg).astype(F32))
    chunks = length // CHUNK
    seg_f = seg.astype(F32)
    seg_last = seg_f.reshape(chunks, CHUNK)[:, -1]
    seg_prev = jnp.concatenate([jnp.full((1,), -1.0, F32), seg_last[:-1]])
    marks = jnp.stack(
        [seg_f, jnp.repeat(seg_prev, CHUNK), jnp.repeat(seg_last, CHUNK)] + keeps[1:] + marks_ahead
        + [jnp.zeros_like(seg_f)] * 7
    ).T
    row = jnp.broadcast_to(seg_f[None, :], (8, length))
    keeps = [None] + [marks[:, 2 + lag : 3 + lag] for lag in range(1, TAPS)]
    marks, row, spread_gu.got = turn(g_first, marks, row, spread_gu.got)
    spread_gu.cross()
    half = HEAD_SIZE // 2
    inverse = ROPE_BASE ** (-(jnp.arange(half, dtype=F32) * 2.0) / HEAD_SIZE)
    angle = place.astype(F32)[:, None] * inverse[None, :]
    cosine, sine = jnp.cos(angle), jnp.sin(angle)
    cosine = jnp.concatenate([cosine, cosine], axis=1)
    sine = jnp.concatenate([-sine, sine], axis=1)
    heads_at = j * HEADS
    lane_pad = ((0, 0), (0, 128 - HEADS))
    own_log = jnp.pad(lax.dynamic_slice_in_dim(decay_log, heads_at, HEADS)[None], lane_pad)
    own_bias = jnp.pad(lax.dynamic_slice_in_dim(step_bias, heads_at, HEADS)[None], lane_pad)
    own_skip = lax.dynamic_slice_in_dim(skip_gain, heads_at, HEADS)
    skip_wide = jnp.repeat(own_skip, P_SIZE)[None, :]
    taps_x = lax.dynamic_slice(conv_taps, (0, j * WX), (TAPS, WX))
    taps_b = conv_taps[:, DI:]
    taps_b_own = lax.dynamic_slice(conv_taps, (0, DI + j * WB), (TAPS, WB))
    cosine, sine, normed = finish(g_first, cosine, sine, normed)
    w_first = g_first.whole
    digits = jnp.sum(w_first[::rows, -2:].astype(F32), axis=0)
    count = digits[0] * 64.0 + digits[1]
    lane = jnp.arange(128)[None, :]
    w_raw = jnp.where(lane < HEADS, w_first[:, WX + WB :], 0)

    conv_b_own = mm(normed, w_first[:, WX : WX + WB]).astype(BF16)
    b_far = y_swap(conv_b_own)
    conv_b_own, normed, w_first = turn(g_second, conv_b_own, normed, w_first)
    step_raw = mm(normed, w_raw)
    conv_x = mm(normed, w_first[:, :WX]).astype(BF16)
    conv_x, step_raw, b_far = turn(g_second, conv_x, step_raw, b_far)
    b_other = core_swap(jnp.concatenate([conv_b_own, b_far], axis=1))
    g_out = start(both_out, lambda b: home(b))
    upper, core = j // 2, j % 2
    mine = (jnp.where(upper == 0, conv_b_own, b_far), jnp.where(upper == 0, b_far, conv_b_own))
    b_other = turn(g_second, b_other)
    theirs = (
        jnp.where(upper == 0, b_other[:, :WB], b_other[:, WB:]),
        jnp.where(upper == 0, b_other[:, WB:], b_other[:, :WB]),
    )
    conv_b = jnp.concatenate(
        [
            jnp.where(core == 0, mine[0], theirs[0]),
            jnp.where(core == 0, theirs[0], mine[0]),
            jnp.where(core == 0, mine[1], theirs[1]),
            jnp.where(core == 0, theirs[1], mine[1]),
        ],
        axis=1,
    )
    rest_ssd = (step_raw, own_bias, own_log, taps_x, taps_b, marks, row, skip_wide)
    ssm_y, saved = ssd_forward(conv_x, conv_b, *rest_ssd)
    ssm_y, normed, spread_gu.across = finish(g_second, ssm_y, normed, spread_gu.across)
    w_second = g_second.whole
    normed = turn(g_out, normed)
    rest = mm(normed, w_second)
    gate_z = rest[:, WQ + HEAD_SIZE :]
    queries = turned(rest[:, :WQ], cosine, sine).astype(BF16)
    kv_raw = rest[:, WQ : WQ + HEAD_SIZE]
    kv_own = jnp.where(core == 0, turned(kv_raw, cosine, sine), kv_raw).astype(BF16)
    kv_other = core_swap(kv_own)
    queries, kv_own, kv_other, gate_z = turn(g_out, queries, kv_own, kv_other, gate_z)
    g_gu = start(spread_gu.block())
    keys = jnp.where(core == 0, kv_own, kv_other)
    values = jnp.where(core == 0, kv_other, kv_own)
    segc, segr = seg[:, None], seg[None, :]
    attended = attention_forward(queries, keys, values, segc, segr)
    silu_z = jax.nn.silu(gate_z)
    gated = (ssm_y * silu_z).astype(BF16)
    attended, gated = turn(g_out, attended, gated)
    acts = jnp.concatenate([gated, attended], axis=1)
    acts = finish(g_out, acts)
    out_all = g_out.whole.reshape(nb, rows_out + rows_attn, MODEL_WIDTH)
    w_out = jnp.concatenate(
        [
            out_all[:, :rows_out].reshape(WX, MODEL_WIDTH),
            out_all[:, rows_out:].reshape(WQ, MODEL_WIDTH),
        ],
        axis=0,
    )


    def upper_rows(value, far):
        return lax.dynamic_slice_in_dim(value, (1 - upper if far else upper) * 2 * own, 2 * own)

    def in_two(value):
        return value.reshape(2, own, -1)

    mixed = NearSum(lambda far: in_two(mm(upper_rows(acts, far), w_out)), core)
    mixed.first, mixed.near = turn(g_gu, mixed.first, mixed.near)
    (mixed.second,) = gate(mixed.second)
    hidden_one = x + mixed.result()
    r_h = rms_of(hidden_one)
    normed_two_own = (hidden_one * r_h * norm_second).astype(BF16)
    (normed_two_own,) = gate(normed_two_own)
    near_two = Near(normed_two_own)
    near_two.next = turn(g_gu, near_two.next)
    near_two.far = turn(g_gu, near_two.far)
    near_two.cross()
    normed_two = near_two.blocks()
    normed_two_all = stacked(normed_two)
    normed_two = list(finish(g_gu, *normed_two))
    w_gu = g_gu.whole

    gates = {}
    hidden_all = jnp.zeros((length, WF), BF16)
    for k in reversed(range(NC)):
        gateup = mm(normed_two[k], w_gu)
        gates[k] = gateup
        piece = (jax.nn.silu(gateup[:, :WF]) * gateup[:, WF:]).astype(BF16)
        hidden_all = lax.dynamic_update_slice(hidden_all, piece, (k * own, 0))

    def near_rows(value, far):
        return value[2 * own :] if far else value[: 2 * own]

    ffn = NearSum(lambda far: in_two(mm(near_rows(hidden_all, far), w_down)), 0)
    (ffn.second,) = gate(ffn.second)
    final = hidden_one + ffn.result()
    error = final - target
    squares = jnp.sum(valid * jnp.sum(error * error, axis=1))
    grad_final = valid[:, None] * error * (total_tokens / count)
    grad_ffn_own = grad_final.astype(BF16)

    def reduce(left, right):
        whole = mm_tn(left, right).astype(BF16)
        size = whole.shape[0] // nb

        def part(slot):
            return lax.dynamic_slice_in_dim(whole, ring.owner(slot) * size, size)

        return ReduceRun(ring, order, part)

    (grad_ffn_own,) = gate(grad_ffn_own)
    near_ffn = Near(grad_ffn_own)
    d_gateup_all = jnp.zeros((length, 2 * WF), BF16)

    def ffn_back(whole, grad, k):
        d_hidden = mm_nt(grad, w_down)
        gate_k, up_k = gates[k][:, :WF], gates[k][:, WF:]
        d_gate = (d_hidden * up_k * silu_slope(gate_k)).astype(BF16)
        d_up = (d_hidden * jax.nn.silu(gate_k)).astype(BF16)
        whole = lax.dynamic_update_slice(whole, d_gate, (k * own, 0))
        return lax.dynamic_update_slice(whole, d_up, (k * own, WF))

    d_gateup_all = ffn_back(d_gateup_all, near_ffn.own, 0)
    d_gateup_all = ffn_back(d_gateup_all, near_ffn.next, 1)
    near_ffn.far, near_ffn.next, near_ffn.own, d_gateup_all = gate(
        near_ffn.far, near_ffn.next, near_ffn.own, d_gateup_all
    )
    near_ffn.cross()
    d_gateup_all = ffn_back(d_gateup_all, near_ffn.far, 2)
    d_gateup_all, near_ffn.last = gate(d_gateup_all, near_ffn.last)
    grad_ffn_all = stacked(near_ffn.blocks())
    r_down = reduce(hidden_all, grad_ffn_all)
    d_gateup_all = ffn_back(d_gateup_all, near_ffn.last, 3)
    (d_gateup_all,) = gate(d_gateup_all)

    d_gateup_all = turn(r_down, d_gateup_all)
    held = [d_gateup_all]
    two = NearSum(lambda far: in_two(mm_nt(near_rows(held[0], far), w_gu)), 0, True)
    two.third, d_gateup_all = gate(two.third, d_gateup_all)
    held = [d_gateup_all]
    two.go()
    two.stay()
    two.first, two.near = turn(r_down, two.first, two.near)
    two.near, two.second = gate(two.near, two.second)
    grad_normed_two = two.result()
    w_two = norm_back(grad_normed_two, hidden_one, r_h, norm_second)
    g_norm_second = jnp.sum(grad_normed_two * hidden_one * r_h, axis=0)
    grad_hidden_one = grad_final + w_two
    branch_own = grad_hidden_one.astype(BF16)
    branch_own, grad_hidden_one, g_norm_second = gate(branch_own, grad_hidden_one, g_norm_second)
    near_branch = Near(branch_own)
    near_branch.next, d_gateup_all = turn(r_down, near_branch.next, d_gateup_all)
    r_gu = reduce(normed_two_all, d_gateup_all)
    near_branch.far = finish(r_down, near_branch.far)
    near_branch.cross()
    (near_branch.last,) = gate(near_branch.last)
    branch = absolute(near_branch.blocks(), j).reshape(length, MODEL_WIDTH)
    d_acts = mm_nt(branch, w_out)
    grad_attended = d_acts[:, WX:].astype(BF16)
    grad_gated = d_acts[:, :WX]
    grad_ssm_y = grad_gated * silu_z
    d_z = (grad_gated * ssm_y * silu_slope(gate_z)).astype(BF16)
    grad_attended, grad_ssm_y, d_z, branch = gate(grad_attended, grad_ssm_y, d_z, branch)

    out_whole = mm_tn(acts, branch).astype(BF16)

    def out_part(slot):
        b = home(ring.owner(slot))
        return jnp.concatenate(
            [
                lax.dynamic_slice_in_dim(out_whole, b * rows_out, rows_out),
                lax.dynamic_slice_in_dim(out_whole, WX + b * rows_attn, rows_attn),
            ],
            axis=0,
        )

    r_out = ReduceRun(ring, order, out_part)
    grad_attended = turn(r_gu, grad_attended)

    dq, dk, dv = attention_backward(queries, keys, values, segc, segr, grad_attended)
    sent = jnp.where(core == 0, dv, dk)
    d_kv_other = core_swap(sent)
    dq, dk, dv, d_kv_other = turn(r_out, dq, dk, dv, d_kv_other)
    d_query = turned(dq, cosine, -sine).astype(BF16)
    d_kv = jnp.where(core == 0, dk, dv) + d_kv_other
    d_kv = jnp.where(core == 0, turned(d_kv, cosine, -sine), d_kv).astype(BF16)
    d_second = jnp.concatenate([d_query, d_kv, d_z], axis=1)
    r_second = reduce(normed, d_second)

    def collected(run):
        return Collect(run.result.astype(BF16).reshape(NC, rows, run.result.shape[1]), j)

    grad_ssm_y, d_second = turn(r_gu, grad_ssm_y, d_second)
    d_early = mm_nt(d_second, w_second)
    operands = (grad_ssm_y, conv_x, saved, rest_ssd)
    d_in_x, dbc, d_raw, sums_a, tsums_a = ssd_backward(0, *operands)
    d_in_x, dbc, d_raw = turn(r_out, d_in_x, dbc, d_raw)
    d_in_x, dbc, d_raw = turn(r_second, d_in_x, dbc, d_raw)
    d_in_x, dbc, d_raw = turn(r_gu, d_in_x, dbc, d_raw)
    d_in_x, dbc, d_raw, sums_b, tsums_b = ssd_backward(1, *operands, (dbc, d_raw, d_in_x))
    d_in_x, dbc, d_raw = turn(r_second, d_in_x, dbc, d_raw)
    d_in_x, dbc, d_raw = turn(r_out, d_in_x, dbc, d_raw)
    d_bc = dbc.reshape(2, 2, length, WB)
    b_sum = NearSum(lambda far: d_bc[1 - upper if far else upper], core)
    b_sum.near = finish(r_gu, b_sum.near)
    col_gu = collected(r_gu)
    sums = sums_a + sums_b
    tsums = jnp.concatenate([tsums_a, tsums_b], axis=1)
    g_bias, g_log = sums[0, :HEADS], sums[1, :HEADS]
    g_taps_x = tsums[:TAPS]
    g_skip = jnp.sum(tsums[TAPS].reshape(HEADS, P_SIZE), axis=1)

    def conv_back(d_conv, value, taps):
        d_in = taps[0][None] * d_conv
        g_taps = [jnp.sum(d_conv * value, axis=0)]
        for lag in range(1, TAPS):
            masked = d_conv * keeps[lag]
            d_in = d_in + taps[lag][None] * shifted(masked, -lag)
            g_taps.append(jnp.sum(masked * shifted(value, lag), axis=0))
        return d_in.astype(BF16), jnp.stack(g_taps)

    b_sum.second, b_sum.near, b_sum.first, conv_b_own, taps_b_own, col_gu.got = turn(
        r_second, b_sum.second, b_sum.near, b_sum.first, conv_b_own, taps_b_own, col_gu.got
    )
    col_gu.cross()
    conv_b_wide = conv_b_own.astype(F32)
    conv_out_b = convolve(conv_b_wide, taps_b_own, keeps)
    d_in_b, g_taps_b = conv_back(b_sum.result() * silu_slope(conv_out_b), conv_b_wide, taps_b_own)
    d_first = jnp.concatenate(
        [d_in_x, d_in_b, d_raw.astype(BF16)], axis=1
    )
    r_first = reduce(normed, d_first)
    d_first = finish(r_out, d_first)
    d_first, col_gu.far = finish(r_second, d_first, col_gu.far)
    col_second = collected(r_second)
    d_first, col_second.got, out_kept = turn(
        r_first, d_first, col_second.got, r_out.result.astype(BF16)
    )
    col_second.cross()
    out_home = lax.ppermute(out_kept, ("batch", "ctx"), back)

    held = [d_first]
    gain_parts = []

    def normed_part(far):
        addends = in_two(mm_nt(upper_rows(held[0], far), w_first) + upper_rows(d_early, far))
        scaled = upper_rows(normed, far).astype(F32).reshape(addends.shape)
        gain_parts.append(jnp.sum(addends * scaled, axis=(0, 1)))
        return addends

    back_sum = NearSum(normed_part, core, True)
    back_sum.third, d_first = gate(back_sum.third, d_first)
    held = [d_first]
    back_sum.go()
    back_sum.stay()
    g_norm_first = (gain_parts[0] + gain_parts[1]) / norm_first
    back_sum.near, g_norm_first, col_second.far, out_home = turn(
        r_first, back_sum.near, g_norm_first, col_second.far, out_home
    )
    taps_all = jnp.zeros((TAPS, DI + 2 * N), F32)
    taps_all = lax.dynamic_update_slice(taps_all, g_taps_x, (0, j * WX))
    taps_all = lax.dynamic_update_slice(taps_all, g_taps_b, (0, DI + j * WB))
    per_head = lax.dynamic_update_slice(
        jnp.zeros((3, 128), F32), jnp.stack([g_log, g_skip, g_bias]), (0, heads_at)
    )
    small = jnp.concatenate(
        [
            g_norm_first.reshape(-1, 128),
            g_norm_second.reshape(-1, 128),
            taps_all.reshape(-1, 128),
            per_head,
            jnp.broadcast_to(squares, (1, 128)),
        ]
    )
    moves = [("batch", nb, 1 << q) for q in range(nb.bit_length() - 1)]
    moves += [("ctx", NC, 1), ("ctx", NC, 2)]
    for axis, size, bit in moves:
        small = small + lax.ppermute(small, axis, [(q, q ^ bit) for q in range(size)])
    back_sum.first = turn(r_first, back_sum.first)
    back_sum.second, back_sum.first = gate(back_sum.second, back_sum.first)
    grad_normed = back_sum.result()
    grad_tokens = grad_hidden_one + norm_back(grad_normed, x, r_x, norm_first)
    grad_tokens = finish(r_first, grad_tokens)
    col_first = collected(r_first)
    col_first.got, small, grad_tokens = gate(col_first.got, small, grad_tokens)
    lines = MODEL_WIDTH // 128
    g_norm_first = small[:lines].reshape(MODEL_WIDTH)
    g_norm_second = small[lines : 2 * lines].reshape(MODEL_WIDTH)
    taps_all = small[2 * lines : -4].reshape(TAPS, DI + 2 * N)
    per_head = small[-4:-1, :H_M]
    loss_value = small[-1, 0] / (MODEL_WIDTH * count) + order.token[0, 0]
    col_first.cross()

    got_gu = col_gu.result()
    grad_gate_up = (
        got_gu.reshape(NC, rows, 2, nb, unit).transpose(1, 2, 3, 0, 4).reshape(rows, 2 * FF)
    )
    got_second = col_second.result()
    got_first = col_first.result()

    def columns(got, begin, size):
        return got[:, :, begin : begin + size].transpose(1, 0, 2).reshape(rows, NC * size)

    grad_query = columns(got_second, 0, WQ)
    grad_keyval = (
        got_second[:, :, WQ : WQ + HEAD_SIZE]
        .reshape(2, 2, rows, HEAD_SIZE)
        .transpose(2, 1, 0, 3)
        .reshape(rows, 4 * HEAD_SIZE)
    )
    grad_mixer_in = jnp.concatenate(
        [
            columns(got_second, WQ + HEAD_SIZE, WX),
            columns(got_first, 0, WX),
            columns(got_first, WX, WB),
            columns(got_first, WX + WB, HEADS),
        ],
        axis=1,
    )
    output = final.astype(BF16).reshape(tokens.shape)
    return (
        output,
        loss_value,
        grad_tokens.reshape(tokens.shape),
        grad_mixer_in,
        out_home[:rows_out].astype(F32),
        grad_query,
        grad_keyval,
        out_home[rows_out:].astype(F32),
        grad_gate_up,
        r_down.result,
        g_norm_first,
        g_norm_second,
        taps_all,
        per_head[0],
        per_head[1],
        per_head[2],
    )


def solution(mesh):
    split_rows = P(("batch", "ctx"), None)
    by_token = P("batch", "ctx", None)
    return jax.shard_map(
        body,
        mesh=mesh,
        in_specs=(by_token, P("batch", "ctx"), P("batch", "ctx"), by_token)
        + (split_rows,) * 7
        + (P(),) * 6,
        out_specs=(by_token, P(), by_token) + (split_rows,) * 7 + (P(),) * 6,
        check_vma=False,
    )
```

time: 1010 us -> 904 us (0.90)
  waiting for transfers between devices: 333 us -> 254 us
  matrix products: 202 us -> 157 us
  Pallas kernels: 60.2 us -> 77.6 us
    ppermute x44 -> x40, waiting for transfers between devices: 194 us -> 95.2 us  [down(): return lax.ppermute(value, 'batch', self.down_pairs)]
    dot_general x40 -> x5, matrix products: 95.5 us -> 38.6 us  [mm_tn(): lax.dot_general(left, right, (((0,), (0,)), ((), ())), preferred_element_...]
    convert_element_type x4 -> x21, other arithmetic: 2.58 us -> 34.1 us  [the longest x10 18.8 us: turn(): b = (b.astype(F32) + down).astype(BF16)]
    mul x6 -> x0, other arithmetic: 11.8 us -> none  [the longest x1 5.33 us: body(): xs = jax.nn.silu(conv_out_x)]
    pallas_call x2, Pallas kernels: 31.3 us -> 42.8 us  [ssd_backward(): pl.pallas_call(functools.partial(ssd_backward_kernel, part * PAIRS // 2),...]
    ppermute x44 -> x40, waiting for transfers between devices: 52.8 us -> 63.5 us  [up(): return lax.ppermute(value, 'batch', self.up_pairs)]
    ppermute x19 -> x17, starting transfers between devices: 16.2 us -> 26.4 us  [y_swap(): return lax.ppermute(value, 'ctx', [(i, i ^ 2) for i in range(NC)])]
    dynamic_update_slice x54 -> x45, local copies, waits for them, and re-layouts: 32.4 us -> 40.9 us  [put(): self.whole = lax.dynamic_update_slice(self.whole, part, (at, 0))]
  transfers between devices with their start and end apart: 146 -> 133, of which waited for: 65 -> 56; matrix products, arithmetic and copies ran while one was open for 38% -> 34% of each run, Pallas kernels for 6% -> 7%
where the time goes in v2:
time: 904 us; the launch traced here: 894 us
  waiting for transfers between devices  254 us (28%)
  local copies, waits for them, and re-layouts  160 us (18%)
  matrix products  157 us (17%)
  starting transfers between devices  138 us (15%)
  other arithmetic  96.9 us (11%)
  Pallas kernels  77.6 us (9%)
  between operations  10.7 us (1%)
    ppermute x40, waiting for transfers between devices, down(): return lax.ppermute(value, 'batch', self.down_pairs)  95.2 us
    ppermute x17, waiting for transfers between devices, y_swap(): return lax.ppermute(value, 'ctx', [(i, i ^ 2) for i in range(NC)])  73.7 us
    dot_general x10, matrix products, mm_nt(): lax.dot_general(left, right, (((1,), (1,)), ((), ())), preferred_element_...  66.1 us
    ppermute x40, waiting for transfers between devices, up(): return lax.ppermute(value, 'batch', self.up_pairs)  63.5 us
    ppermute x40, starting transfers between devices, up(): return lax.ppermute(value, 'batch', self.up_pairs)  53 us
    dot_general x12, matrix products, mm(): return jnp.dot(left, right, preferred_element_type=F32)  52.1 us
    ppermute x40, starting transfers between devices, down(): return lax.ppermute(value, 'batch', self.down_pairs)  43.7 us
    pallas_call x2, Pallas kernels, ssd_backward(): pl.pallas_call(functools.partial(ssd_backward_kernel, part * PAIRS // 2),...  42.8 us
  transfers between devices with their start and end apart: 133, of which 56 were waited for; matrix products, arithmetic and copies ran while one was open for 34% of the time, Pallas kernels for 7%

profile of v2, /device:TPU:0, one launch (start us, length us, event | category | flops | bytes accessed | tf_op | source)
XLA Modules:
  0.0 893.9 jit_solution(1221861879457246736)
XLA Ops:
  20.7 5.4 collective-permute-start.8
  52.8 5.1 collective-permute-done.9
  81.0 7.8 collective-permute-done.16
  133.7 4.9 collective-permute-done.29
  148.4 6.6 fusion.14.x_ref.refs_1_.refs_2_
  170.9 8.7 collective-permute-done.33
  183.7 16.4 %ssd_forward.1 = (f32[1024,768]{1,0:T(8,128)S(1)}, bf16[8,768,256]{2,1,0:T(8,128)(2,1)S(1)}, f32[1024,768]{1,0:T(8,128)}, bf16[1024,512]{1,0:T(8,128)(2,1)S(1)},...) custom-call(bf16[1024,768]{1,0:T(8,128)(2,1)S(1)} %fusion.14.x_ref.r, ...), custom_call_target="tpu_custom_call" | custom-call | tf_op jit(solution)/shard_map/ssd_forward/pallas_call | solution.py:499
  205.0 8.7 fusion.109
  217.8 11.6 %collective-permute-done.41 = bf16[128,2048]{1,0:T(8,128)(2,1)S(1)} collective-permute-done((bf16[128,2048]{1,0:T(8,128)(2,1)S(1)}, bf16[128,2048]{1,0:T(8,128)(2,1)S(1)}, u32[]{:S(2)}, u32[]{:S(2)}) %collective-permute-start.41) | collective-permute-done | bytes 524320 | tf_op jit(solution)/shard_map/ppermute | solution.py:76
  233.1 7.3 attention_forward.1
  260.4 4.9 fusion.19
  277.9 5.9 collective-permute-done.44
  286.2 10.8 %collective-permute-done.52 = bf16[256,2048]{1,0:T(8,128)(2,1)} collective-permute-done((bf16[256,2048]{1,0:T(8,128)(2,1)}, bf16[256,2048]{1,0:T(8,128)(2,1)}, u32[]{:S(2)}, u32[]{:S(2)}) %collective-permute-start.52) | collective-permute-done | bytes 1048608 | tf_op jit(solution)/shard_map/ppermute | solution.py:59
  319.3 16.6 %collective-permute-done.58 = bf16[256,2048]{1,0:T(8,128)(2,1)S(1)} collective-permute-done((bf16[256,2048]{1,0:T(8,128)(2,1)S(1)}, bf16[256,2048]{1,0:T(8,128)(2,1)S(1)}, u32[]{:S(2)}, u32[]{:S(2)}) %collective-permute-start.58) | collective-permute-done | bytes 1048608 | tf_op jit(solution)/shard_map/ppermute | solution.py:59
  341.6 11.8 %collective-permute-done.59 = bf16[128,2048]{1,0:T(8,128)(2,1)S(1)} collective-permute-done((bf16[128,2048]{1,0:T(8,128)(2,1)S(1)}, bf16[128,2048]{1,0:T(8,128)(2,1)S(1)}, u32[]{:S(2)}, u32[]{:S(2)}) %collective-permute-start.59) | collective-permute-done | bytes 524320 | tf_op jit(solution)/shard_map/ppermute | solution.py:76
  356.3 4.5 fusion.112
  367.3 5.3 fusion.24
  378.1 4.9 fusion.26
  389.2 13.1 %collective-permute-done.64 = bf16[256,2048]{1,0:T(8,128)(2,1)} collective-permute-done((bf16[256,2048]{1,0:T(8,128)(2,1)}, bf16[256,2048]{1,0:T(8,128)(2,1)}, u32[]{:S(2)}, u32[]{:S(2)}) %collective-permute-start.64) | collective-permute-done | bytes 1048608 | tf_op jit(solution)/shard_map/ppermute | solution.py:59
  417.5 14.4 %collective-permute-done.65 = bf16[256,2048]{1,0:T(8,128)(2,1)S(1)} collective-permute-done((bf16[256,2048]{1,0:T(8,128)(2,1)S(1)}, bf16[256,2048]{1,0:T(8,128)(2,1)S(1)}, u32[]{:S(2)}, u32[]{:S(2)}) %collective-permute-start.65) | collective-permute-done | bytes 1048608 | tf_op jit(solution)/shard_map/ppermute | solution.py:59
  440.8 4.9 convolution_convert_fusion.4
  451.5 4.4 collective-permute-done.68
  457.2 6.3 fusion.11
  469.5 9.5 %fusion.9 = f32[512,2048]{1,0:T(8,128)} fusion(bf16[2048,2048]{1,0:T(8,128)(2,1)} %copy-done.37, bf16[1024,2048]{1,0:T(8,128)(2,1)S(1)} %copy-done.58), kind=kOutput, calls=%fused_computation.52 | convolution fusion | flops 4294967296 | bytes 14680064 | tf_op jit(solution)/shard_map/dot_general | solution.py:47
  488.5 9.9 %collective-permute-done.70 = bf16[128,2048]{1,0:T(8,128)(2,1)S(1)} collective-permute-done((bf16[128,2048]{1,0:T(8,128)(2,1)S(1)}, bf16[128,2048]{1,0:T(8,128)(2,1)S(1)}, u32[]{:S(2)}, u32[]{:S(2)}) %collective-permute-start.70) | collective-permute-done | bytes 524320 | tf_op jit(solution)/shard_map/ppermute | solution.py:73
  500.5 8.8 collective-permute-done.74
  517.7 10.4 %collective-permute-done.75 = bf16[128,2048]{1,0:T(8,128)(2,1)S(1)} collective-permute-done((bf16[128,2048]{1,0:T(8,128)(2,1)S(1)}, bf16[128,2048]{1,0:T(8,128)(2,1)S(1)}, u32[]{:S(2)}, u32[]{:S(2)}) %collective-permute-start.75) | collective-permute-done | bytes 524320 | tf_op jit(solution)/shard_map/ppermute | solution.py:73
  532.3 10.9 %convolution_convert_fusion.1 = bf16[2048,2048]{1,0:T(8,128)(2,1)S(1)} fusion(bf16[1024,2048]{1,0:T(8,128)(2,1)} %copy-done.64, bf16[1024,2048]{1,0:T(8,128)(2,1)S(1)} %copy-done.59), kind=kOutput, calls=%fused_computation.1 | convolution fusion | flops 8594128896 | bytes 16777216 | tf_op jit(solution)/shard_map/dot_general | solution.py:43
  550.9 8.1 fusion.17
  560.9 8.1 convolution_convert_fusion.3
  571.6 11.1 %attention_backward.1 = (f32[1024,256]{1,0:T(8,128)S(1)}, f32[1024,128]{1,0:T(8,128)S(1)}, f32[1024,128]{1,0:T(8,128)S(1)}) custom-call(bf16[1024,256]{1,0:T(8,128)(2,1)S(1)} %copy-done.9, bf16[1024,128]{1,0:T(8,128)(2,1)S(1)} %copy-done.13, bf16[1024,128]{1,0:T(8,128)(2,1)S(1)} %copy-done.11, s32[1024,1]{1,0:T(8,128)S(1)} %bitcast.255, ...), custom_call_target="tpu_custom_call" | custom-call | tf_op jit(solution)/shard_map/attention_backward/pallas_call | solution.py:628
  595.4 7.5 convolution_convert_fusion
  610.0 4.6 collective-permute-done.89
  620.2 20.9 %ssd_backward.2 = (bf16[1024,768]{1,0:T(8,128)(2,1)S(1)}, f32[4,1024,128]{2,1,0:T(8,128)S(1)}, f32[1024,128]{1,0:T(8,128)S(1)}, f32[8,128]{1,0:T(8,128)S(1)}, f32[8,384]{1,0:T(8,128)S(1)}) custom-call(f32[1024,768]{1,0:T(8,128)S(1)} %get-tuple-element.526.refs_0_, bf16[1024,768]{1,0:T(8,128)(2,1)S(1)} %copy-done.1, bf16[1024,768]{1,0:T(8,128)(2,1)S(1)} %copy-done.1, ...), custom_call_target="tpu_custom_call" | custom-call | tf_op jit(solution)/shard_map/ssd_backward/pallas_call | solution.py:535
  649.3 10.1 %fusion.114 = f32[1024,2048]{1,0:T(8,128)} fusion(bf16[1024,1152]{1,0:T(8,128)(2,1)S(1)} %pad_maximum_fusion.1, bf16[2048,1152]{1,0:T(8,128)(2,1)} %constant_dynamic-update-slice_fusion.35), kind=kOutput, calls=%fused_computation.465 | convolution fusion | flops 4831838208 | bytes 15466496 | tf_op jit(solution)/shard_map/dot_general | solution.py:47
  660.8 6.5 collective-permute-done.98
  672.5 21.9 %ssd_backward.3 = (bf16[1024,768]{1,0:T(8,128)(2,1)S(1)}, f32[4,1024,128]{2,1,0:T(8,128)}, f32[1024,128]{1,0:T(8,128)S(1)}, f32[8,128]{1,0:T(8,128)S(1)}, f32[8,384]{1,0:T(8,128)S(1)}) custom-call(f32[1024,768]{1,0:T(8,128)} %copy-done.2, bf16[1024,768]{1,0:T(8,128)(2,1)S(1)} %copy-done.1, ...), custom_call_target="tpu_custom_call", output_to_operand_aliasing={{0}: (22, {})} | custom-call | tf_op jit(solution)/shard_map/ssd_backward/pallas_call | solution.py:535
  709.1 12.5 %collective-permute-done.104 = bf16[256,2048]{1,0:T(8,128)(2,1)} collective-permute-done((bf16[256,2048]{1,0:T(8,128)(2,1)}, bf16[256,2048]{1,0:T(8,128)(2,1)}, u32[]{:S(2)}, u32[]{:S(2)}) %collective-permute-start.104) | collective-permute-done | bytes 1048608 | tf_op jit(solution)/shard_map/ppermute | solution.py:76
  729.4 6.6 collective-permute-done.102
  741.5 7.2 convolution_convert_fusion.2
  764.4 7.0 collective-permute-done.109
  776.1 7.9 dynamic-slice_add_fusion.1
  799.5 9.1 %multiply_reduce_fusion = (f32[2048]{0:T(1024)S(1)}, f32[2048]{0:T(1024)S(1)}, f32[512,2048]{1,0:T(8,128)S(1)}) fusion(bf16[1024,2048]{1,0:T(8,128)(2,1)} %bitcast.32, s32[]{:T(128)S(6)} %select_n.920, f32[512,2048]{1,0:T(8,128)} %dynamic-slice_add_fusion.1, s32[]{:T(128)S(6)} %select_n.964, f32[1024,2048]{1,0:T(8,128)} %fusion.114, ...), kind=kOutput, calls=%fused_computation.3 | convolution fusion | flops 2154819584 | bytes 22038016 | tf_op jit(solution)/shard_map/dot_general | solution.py:47
  815.8 9.9 %collective-permute-start.125 = (bf16[256,2048]{1,0:T(8,128)(2,1)S(1)}, bf16[256,2048]{1,0:T(8,128)(2,1)S(1)}, u32[]{:S(2)}, u32[]{:S(2)}) collective-permute-start(bf16[256,2048]{1,0:T(8,128)(2,1)S(1)} %fusion.7), channel_id=1, source_target_pairs={{0,2},{1,3},{2,0},{3,1},{4,6},{5,7},{6,4},{7,5},{8,10},{9,11},{10,... | collective-permute-start | bytes 3145736 | tf_op jit(solution)/shard_map/ppermute | solution.py:59
  827.3 12.7 %collective-permute-start.120 = (bf16[256,1024]{1,0:T(8,128)(2,1)S(1)}, bf16[256,1024]{1,0:T(8,128)(2,1)S(1)}, u32[]{:S(2)}, u32[]{:S(2)}) collective-permute-start(bf16[256,1024]{1,0:T(8,128)(2,1)S(1)} %get-tuple-element.695), channel_id=1, source_target_pairs={{0,8},{8,16},{16,24},{24,28},{28,20},{20,12},{12,4},{4,0},{1,9},{9... | collective-permute-start | bytes 1572872 | tf_op jit(solution)/shard_map/ppermute | solution.py:73
  843.4 11.9 %collective-permute-done.128 = f32[148,128]{1,0:T(8,128)S(1)} collective-permute-done((f32[148,128]{1,0:T(8,128)S(1)}, f32[148,128]{1,0:T(8,128)S(1)}, u32[]{:S(2)}, u32[]{:S(2)}) %collective-permute-start.128) | collective-permute-done | bytes 75808 | tf_op jit(solution)/shard_map/ppermute | solution.py:1106
  856.2 5.0 collective-permute-done.129
  866.9 9.9 %collective-permute-done.123 = bf16[256,1024]{1,0:T(8,128)(2,1)S(1)} collective-permute-done((bf16[256,1024]{1,0:T(8,128)(2,1)S(1)}, bf16[256,1024]{1,0:T(8,128)(2,1)S(1)}, u32[]{:S(2)}, u32[]{:S(2)}) %collective-permute-start.123) | collective-permute-done | bytes 524320 | tf_op jit(solution)/shard_map/ppermute | solution.py:73
  (930 shorter events, 444.7 us)
Async XLA Ops:
  3.6 22.5 %collective-permute-start = (bf16[128,2048]{1,0:T(8,128)(2,1)}, bf16[128,2048]{1,0:T(8,128)(2,1)}, u32[]{:S(2)}, u32[]{:S(2)}) collective-permute-start(bf16[128,2048]{1,0:T(8,128)(2,1)} %param.27), channel_id=1, source_target_pairs={{8,0},{16,8},{24,16},{28,24},{20,28},{12,20},{4,12},{0,4},{9,1},{1... | collective-permute-start | bytes 1572872 | tf_op jit(solution)/shard_map/ppermute | solution.py:76
  20.7 39.0 %collective-permute-start.8 = (bf16[128,2048]{1,0:T(8,128)(2,1)}, bf16[128,2048]{1,0:T(8,128)(2,1)}, u32[]{:S(2)}, u32[]{:S(2)}) collective-permute-start(bf16[128,2048]{1,0:T(8,128)(2,1)} %pad_maximum_fusion.12), channel_id=1, source_target_pairs={{0,0},{1,16},{2,8},{3,24},{4,4},{5,20},{6,12},{7,28},{8,1},{9,17},... | collective-permute-start | bytes 1572872 | tf_op jit(solution)/shard_map/ppermute | solution.py:741
  34.1 23.8 %collective-permute-start.9 = (bf16[128,2048]{1,0:T(8,128)(2,1)}, bf16[128,2048]{1,0:T(8,128)(2,1)}, u32[]{:S(2)}, u32[]{:S(2)}) collective-permute-start(bf16[128,2048]{1,0:T(8,128)(2,1)} %collective-permute-done), channel_id=1, source_target_pairs={{8,0},{16,8},{24,16},{28,24},{20,28},{12,20},{4,12},{0,4},{9,1},{1... | collective-permute-start | bytes 1572872 | tf_op jit(solution)/shard_map/ppermute | solution.py:76
  57.9 23.1 %collective-permute-start.18 = (bf16[256,2048]{1,0:T(8,128)(2,1)}, bf16[256,2048]{1,0:T(8,128)(2,1)}, u32[]{:S(2)}, u32[]{:S(2)}) collective-permute-start(bf16[256,2048]{1,0:T(8,128)(2,1)} %get-tuple-element.662), channel_id=1, source_target_pairs={{0,2},{1,3},{2,0},{3,1},{4,6},{5,7},{6,4},{7,5},{8,10},{9,11},{10,... | collective-permute-start | bytes 3145736 | tf_op jit(solution)/shard_map/ppermute | solution.py:59
  66.7 22.1 %collective-permute-start.16 = (bf16[256,1024]{1,0:T(8,128)(2,1)}, bf16[256,1024]{1,0:T(8,128)(2,1)}, u32[]{:S(2)}, u32[]{:S(2)}) collective-permute-start(bf16[256,1024]{1,0:T(8,128)(2,1)} %collective-permute-done.6), channel_id=1, source_target_pairs={{8,0},{16,8},{24,16},{28,24},{20,28},{12,20},{4,12},{0,4},{9,1},{1... | collective-permute-start | bytes 1572872 | tf_op jit(solution)/shard_map/ppermute | solution.py:76
  81.0 38.4 %collective-permute-start.24 = (bf16[2,64,2048]{2,1,0:T(8,128)(2,1)}, bf16[2,64,2048]{2,1,0:T(8,128)(2,1)}, u32[]{:S(2)}, u32[]{:S(2)}) collective-permute-start(bf16[2,64,2048]{2,1,0:T(8,128)(2,1)} %pad_maximum_fusion.13), channel_id=1, source_target_pairs={{0,2},{1,3},{2,0},{3,1},{4,6},{5,7},{6,4},{7,5},{8,10},{9,11},{10,... | collective-permute-start | bytes 1572872 | tf_op jit(solution)/shard_map/ppermute | solution.py:59
  97.6 21.8 %collective-permute-start.22 = (bf16[256,1024]{1,0:T(8,128)(2,1)}, bf16[256,1024]{1,0:T(8,128)(2,1)S(1)}, u32[]{:S(2)}, u32[]{:S(2)}) collective-permute-start(bf16[256,1024]{1,0:T(8,128)(2,1)} %collective-permute-done.16), channel_id=1, source_target_pairs={{8,0},{16,8},{24,16},{28,24},{20,28},{12,20},{4,12},{0,4},{9,1},{1... | collective-permute-start | bytes 1572872 | tf_op jit(solution)/shard_map/ppermute | solution.py:76
  113.1 33.3 %collective-permute-start.20 = (bf16[256,1152]{1,0:T(8,128)(2,1)}, bf16[256,1152]{1,0:T(8,128)(2,1)}, u32[]{:S(2)}, u32[]{:S(2)}) collective-permute-start(bf16[256,1152]{1,0:T(8,128)(2,1)} %bitcast.14), channel_id=1, source_target_pairs={{8,0},{16,8},{24,16},{28,24},{20,28},{12,20},{4,12},{0,4},{9,1},{1... | collective-permute-start | bytes 1769480 | tf_op jit(solution)/shard_map/ppermute | solution.py:76
  118.2 28.1 %collective-permute-start.21 = (bf16[256,1152]{1,0:T(8,128)(2,1)}, bf16[256,1152]{1,0:T(8,128)(2,1)}, u32[]{:S(2)}, u32[]{:S(2)}) collective-permute-start(bf16[256,1152]{1,0:T(8,128)(2,1)} %bitcast.14), channel_id=1, source_target_pairs={{0,8},{8,16},{16,24},{24,28},{28,20},{20,12},{12,4},{4,0},{1,9},{9... | collective-permute-start | bytes 1769480 | tf_op jit(solution)/shard_map/ppermute | solution.py:73
  125.9 75.2 %collective-permute-start.38 = (bf16[2,64,2048]{2,1,0:T(8,128)(2,1)S(1)}, bf16[2,64,2048]{2,1,0:T(8,128)(2,1)S(1)}, u32[]{:S(2)}, u32[]{:S(2)}) collective-permute-start(bf16[2,64,2048]{2,1,0:T(8,128)(2,1)S(1)} %pad_maximum_fusion.17), channel_id=1, source_target_pairs={{0,1},{1,0},{2,3},{3,2},{4,5},{5,4},{6,7},{7,6},{8,9},{9,8},{10,11... | collective-permute-start | bytes 1572872 | tf_op jit(solution)/shard_map/ppermute | solution.py:55
  165.4 36.9 %collective-permute-start.39 = (bf16[128,2048]{1,0:T(8,128)(2,1)}, bf16[128,2048]{1,0:T(8,128)(2,1)S(1)}, u32[]{:S(2)}, u32[]{:S(2)}) collective-permute-start(bf16[128,2048]{1,0:T(8,128)(2,1)} %collective-permute-done.8), channel_id=1, source_target_pairs={{8,0},{16,8},{24,16},{28,24},{20,28},{12,20},{4,12},{0,4},{9,1},{1... | collective-permute-start | bytes 1572872 | tf_op jit(solution)/shard_map/ppermute | solution.py:76
  169.0 33.4 %collective-permute-start.40 = (bf16[128,2048]{1,0:T(8,128)(2,1)}, bf16[128,2048]{1,0:T(8,128)(2,1)S(1)}, u32[]{:S(2)}, u32[]{:S(2)}) collective-permute-start(bf16[128,2048]{1,0:T(8,128)(2,1)} %collective-permute-done.8), channel_id=1, source_target_pairs={{0,8},{8,16},{16,24},{24,28},{28,20},{20,12},{12,4},{4,0},{1,9},{9... | collective-permute-start | bytes 1572872 | tf_op jit(solution)/shard_map/ppermute | solution.py:73
  258.1 25.7 %collective-permute-start.44 = (bf16[256,2048]{1,0:T(8,128)(2,1)S(1)}, bf16[256,2048]{1,0:T(8,128)(2,1)}, u32[]{:S(2)}, u32[]{:S(2)}) collective-permute-start(bf16[256,2048]{1,0:T(8,128)(2,1)S(1)} %bitcast.270), channel_id=1, source_target_pairs={{8,0},{16,8},{24,16},{28,24},{20,28},{12,20},{4,12},{0,4},{9,1},{1... | collective-permute-start | bytes 3145736 | tf_op jit(solution)/shard_map/ppermute | solution.py:76
  258.6 25.5 %collective-permute-start.45 = (bf16[256,2048]{1,0:T(8,128)(2,1)S(1)}, bf16[256,2048]{1,0:T(8,128)(2,1)}, u32[]{:S(2)}, u32[]{:S(2)}) collective-permute-start(bf16[256,2048]{1,0:T(8,128)(2,1)S(1)} %bitcast.271), channel_id=1, source_target_pairs={{0,8},{8,16},{16,24},{24,28},{28,20},{20,12},{12,4},{4,0},{1,9},{9... | collective-permute-start | bytes 3145736 | tf_op jit(solution)/shard_map/ppermute | solution.py:73
  270.9 26.1 %collective-permute-start.52 = (bf16[256,2048]{1,0:T(8,128)(2,1)}, bf16[256,2048]{1,0:T(8,128)(2,1)}, u32[]{:S(2)}, u32[]{:S(2)}) collective-permute-start(bf16[256,2048]{1,0:T(8,128)(2,1)} %fusion.8), channel_id=1, source_target_pairs={{0,2},{1,3},{2,0},{3,1},{4,6},{5,7},{6,4},{7,5},{8,10},{9,11},{10,... | collective-permute-start | bytes 3145736 | tf_op jit(solution)/shard_map/ppermute | solution.py:59
  284.1 28.3 %collective-permute-start.53 = (bf16[256,2048]{1,0:T(8,128)(2,1)}, bf16[256,2048]{1,0:T(8,128)(2,1)S(1)}, u32[]{:S(2)}, u32[]{:S(2)}) collective-permute-start(bf16[256,2048]{1,0:T(8,128)(2,1)} %collective-permute-done.44), channel_id=1, source_target_pairs={{8,0},{16,8},{24,16},{28,24},{20,28},{12,20},{4,12},{0,4},{9,1},{1... | collective-permute-start | bytes 3145736 | tf_op jit(solution)/shard_map/ppermute | solution.py:76
  285.8 26.6 %collective-permute-start.54 = (bf16[256,2048]{1,0:T(8,128)(2,1)}, bf16[256,2048]{1,0:T(8,128)(2,1)S(1)}, u32[]{:S(2)}, u32[]{:S(2)}) collective-permute-start(bf16[256,2048]{1,0:T(8,128)(2,1)} %collective-permute-done.45), channel_id=1, source_target_pairs={{0,8},{8,16},{16,24},{24,28},{28,20},{20,12},{12,4},{4,0},{1,9},{9... | collective-permute-start | bytes 3145736 | tf_op jit(solution)/shard_map/ppermute | solution.py:73
  310.7 25.2 %collective-permute-start.58 = (bf16[256,2048]{1,0:T(8,128)(2,1)S(1)}, bf16[256,2048]{1,0:T(8,128)(2,1)S(1)}, u32[]{:S(2)}, u32[]{:S(2)}) collective-permute-start(bf16[256,2048]{1,0:T(8,128)(2,1)S(1)} %multiply_convert_fusion.2), channel_id=1, source_target_pairs={{0,2},{1,3},{2,0},{3,1},{4,6},{5,7},{6,4},{7,5},{8,10},{9,11},{10,... | collective-permute-start | bytes 3145736 | tf_op jit(solution)/shard_map/ppermute | solution.py:59
  312.4 25.0 %collective-permute-start.56 = (bf16[256,2048]{1,0:T(8,128)(2,1)S(1)}, bf16[256,2048]{1,0:T(8,128)(2,1)S(1)}, u32[]{:S(2)}, u32[]{:S(2)}) collective-permute-start(bf16[256,2048]{1,0:T(8,128)(2,1)S(1)} %collective-permute-done.53), channel_id=1, source_target_pairs={{8,0},{16,8},{24,16},{28,24},{20,28},{12,20},{4,12},{0,4},{9,1},{1... | collective-permute-start | bytes 3145736 | tf_op jit(solution)/shard_map/ppermute | solution.py:76
  312.9 24.6 %collective-permute-start.57 = (bf16[256,2048]{1,0:T(8,128)(2,1)S(1)}, bf16[256,2048]{1,0:T(8,128)(2,1)S(1)}, u32[]{:S(2)}, u32[]{:S(2)}) collective-permute-start(bf16[256,2048]{1,0:T(8,128)(2,1)S(1)} %collective-permute-done.54), channel_id=1, source_target_pairs={{0,8},{8,16},{16,24},{24,28},{28,20},{20,12},{12,4},{4,0},{1,9},{9... | collective-permute-start | bytes 3145736 | tf_op jit(solution)/shard_map/ppermute | solution.py:73
  376.8 25.5 %collective-permute-start.64 = (bf16[256,2048]{1,0:T(8,128)(2,1)}, bf16[256,2048]{1,0:T(8,128)(2,1)}, u32[]{:S(2)}, u32[]{:S(2)}) collective-permute-start(bf16[256,2048]{1,0:T(8,128)(2,1)} %fusion.4), channel_id=1, source_target_pairs={{0,2},{1,3},{2,0},{3,1},{4,6},{5,7},{6,4},{7,5},{8,10},{9,11},{10,... | collective-permute-start | bytes 3145736 | tf_op jit(solution)/shard_map/ppermute | solution.py:59
  406.3 25.6 %collective-permute-start.65 = (bf16[256,2048]{1,0:T(8,128)(2,1)S(1)}, bf16[256,2048]{1,0:T(8,128)(2,1)S(1)}, u32[]{:S(2)}, u32[]{:S(2)}) collective-permute-start(bf16[256,2048]{1,0:T(8,128)(2,1)S(1)} %fusion.13), channel_id=1, source_target_pairs={{0,2},{1,3},{2,0},{3,1},{4,6},{5,7},{6,4},{7,5},{8,10},{9,11},{10,... | collective-permute-start | bytes 3145736 | tf_op jit(solution)/shard_map/ppermute | solution.py:59
  484.2 25.2 %collective-permute-start.74 = (bf16[256,2048]{1,0:T(8,128)(2,1)S(1)}, bf16[256,2048]{1,0:T(8,128)(2,1)S(1)}, u32[]{:S(2)}, u32[]{:S(2)}) collective-permute-start(bf16[256,2048]{1,0:T(8,128)(2,1)S(1)} %fusion.3), channel_id=1, source_target_pairs={{0,2},{1,3},{2,0},{3,1},{4,6},{5,7},{6,4},{7,5},{8,10},{9,11},{10,... | collective-permute-start | bytes 3145736 | tf_op jit(solution)/shard_map/ppermute | solution.py:59
  516.8 31.2 %collective-permute-start.80 = (bf16[256,2048]{1,0:T(8,128)(2,1)S(1)}, bf16[256,2048]{1,0:T(8,128)(2,1)S(1)}, u32[]{:S(2)}, u32[]{:S(2)}) collective-permute-start(bf16[256,2048]{1,0:T(8,128)(2,1)S(1)} %get-tuple-element.489), channel_id=1, source_target_pairs={{0,2},{1,3},{2,0},{3,1},{4,6},{5,7},{6,4},{7,5},{8,10},{9,11},{10,... | collective-permute-start | bytes 3145736 | tf_op jit(solution)/shard_map/ppermute | solution.py:59
  546.0 25.2 %collective-permute-start.84 = (bf16[128,2048]{1,0:T(8,128)(2,1)}, bf16[128,2048]{1,0:T(8,128)(2,1)}, u32[]{:S(2)}, u32[]{:S(2)}) collective-permute-start(bf16[128,2048]{1,0:T(8,128)(2,1)} %get-tuple-element.741), channel_id=1, source_target_pairs={{0,8},{8,16},{16,24},{24,28},{28,20},{20,12},{12,4},{4,0},{1,9},{9... | collective-permute-start | bytes 1572872 | tf_op jit(solution)/shard_map/ppermute | solution.py:73
  547.4 23.9 %collective-permute-start.85 = (bf16[128,2048]{1,0:T(8,128)(2,1)}, bf16[128,2048]{1,0:T(8,128)(2,1)}, u32[]{:S(2)}, u32[]{:S(2)}) collective-permute-start(bf16[128,2048]{1,0:T(8,128)(2,1)} %get-tuple-element.740), channel_id=1, source_target_pairs={{8,0},{16,8},{24,16},{28,24},{20,28},{12,20},{4,12},{0,4},{9,1},{1... | collective-permute-start | bytes 1572872 | tf_op jit(solution)/shard_map/ppermute | solution.py:76
  586.8 27.9 %collective-permute-start.89 = (bf16[256,2048]{1,0:T(8,128)(2,1)S(1)}, bf16[256,2048]{1,0:T(8,128)(2,1)S(1)}, u32[]{:S(2)}, u32[]{:S(2)}) collective-permute-start(bf16[256,2048]{1,0:T(8,128)(2,1)S(1)} %get-tuple-element.668), channel_id=1, source_target_pairs={{0,8},{8,16},{16,24},{24,28},{28,20},{20,12},{12,4},{4,0},{1,9},{9... | collective-permute-start | bytes 3145736 | tf_op jit(solution)/shard_map/ppermute | solution.py:73
  588.2 28.0 %collective-permute-start.90 = (bf16[256,2048]{1,0:T(8,128)(2,1)S(1)}, bf16[256,2048]{1,0:T(8,128)(2,1)}, u32[]{:S(2)}, u32[]{:S(2)}) collective-permute-start(bf16[256,2048]{1,0:T(8,128)(2,1)S(1)} %get-tuple-element.667), channel_id=1, source_target_pairs={{8,0},{16,8},{24,16},{28,24},{20,28},{12,20},{4,12},{0,4},{9,1},{1... | collective-permute-start | bytes 3145736 | tf_op jit(solution)/shard_map/ppermute | solution.py:76
  605.6 35.4 %collective-permute-start.88 = (bf16[128,2048]{1,0:T(8,128)(2,1)}, bf16[128,2048]{1,0:T(8,128)(2,1)}, u32[]{:S(2)}, u32[]{:S(2)}) collective-permute-start(bf16[128,2048]{1,0:T(8,128)(2,1)} %fusion.71), channel_id=1, source_target_pairs={{8,0},{16,8},{24,16},{28,24},{20,28},{12,20},{4,12},{0,4},{9,1},{1... | collective-permute-start | bytes 1572872 | tf_op jit(solution)/shard_map/ppermute | solution.py:76
  607.1 35.6 %collective-permute-start.87 = (bf16[128,2048]{1,0:T(8,128)(2,1)}, bf16[128,2048]{1,0:T(8,128)(2,1)}, u32[]{:S(2)}, u32[]{:S(2)}) collective-permute-start(bf16[128,2048]{1,0:T(8,128)(2,1)} %fusion.70), channel_id=1, source_target_pairs={{0,8},{8,16},{16,24},{24,28},{28,20},{20,12},{12,4},{4,0},{1,9},{9... | collective-permute-start | bytes 1572872 | tf_op jit(solution)/shard_map/ppermute | solution.py:73
  609.3 33.3 %collective-permute-start.93 = (bf16[128,1152]{1,0:T(8,128)(2,1)}, bf16[128,1152]{1,0:T(8,128)(2,1)}, u32[]{:S(2)}, u32[]{:S(2)}) collective-permute-start(bf16[128,1152]{1,0:T(8,128)(2,1)} %get-tuple-element.755), channel_id=1, source_target_pairs={{0,8},{8,16},{16,24},{24,28},{28,20},{20,12},{12,4},{4,0},{1,9},{9... | collective-permute-start | bytes 884744 | tf_op jit(solution)/shard_map/ppermute | solution.py:73
  614.7 28.0 %collective-permute-start.94 = (bf16[128,1152]{1,0:T(8,128)(2,1)}, bf16[128,1152]{1,0:T(8,128)(2,1)}, u32[]{:S(2)}, u32[]{:S(2)}) collective-permute-start(bf16[128,1152]{1,0:T(8,128)(2,1)} %get-tuple-element.754), channel_id=1, source_target_pairs={{8,0},{16,8},{24,16},{28,24},{20,28},{12,20},{4,12},{0,4},{9,1},{1... | collective-permute-start | bytes 884744 | tf_op jit(solution)/shard_map/ppermute | solution.py:76
  619.6 39.9 %collective-permute-start.97 = (bf16[256,2048]{1,0:T(8,128)(2,1)}, bf16[256,2048]{1,0:T(8,128)(2,1)S(1)}, u32[]{:S(2)}, u32[]{:S(2)}) collective-permute-start(bf16[256,2048]{1,0:T(8,128)(2,1)} %get-tuple-element.666), channel_id=1, source_target_pairs={{0,8},{8,16},{16,24},{24,28},{28,20},{20,12},{12,4},{4,0},{1,9},{9... | collective-permute-start | bytes 3145736 | tf_op jit(solution)/shard_map/ppermute | solution.py:73
  641.1 26.2 %collective-permute-start.98 = (bf16[256,2048]{1,0:T(8,128)(2,1)S(1)}, bf16[256,2048]{1,0:T(8,128)(2,1)S(1)}, u32[]{:S(2)}, u32[]{:S(2)}) collective-permute-start(bf16[256,2048]{1,0:T(8,128)(2,1)S(1)} %copy-done.101), channel_id=1, source_target_pairs={{8,0},{16,8},{24,16},{28,24},{20,28},{12,20},{4,12},{0,4},{9,1},{1... | collective-permute-start | bytes 3145736 | tf_op jit(solution)/shard_map/ppermute | solution.py:76
  644.1 51.0 %collective-permute-start.95 = (bf16[256,1152]{1,0:T(8,128)(2,1)S(1)}, bf16[256,1152]{1,0:T(8,128)(2,1)S(1)}, u32[]{:S(2)}, u32[]{:S(2)}) collective-permute-start(bf16[256,1152]{1,0:T(8,128)(2,1)S(1)} %get-tuple-element.682), channel_id=1, source_target_pairs={{0,8},{8,16},{16,24},{24,28},{28,20},{20,12},{12,4},{4,0},{1,9},{9... | collective-permute-start | bytes 1769480 | tf_op jit(solution)/shard_map/ppermute | solution.py:73
  644.7 51.2 %collective-permute-start.96 = (bf16[256,1152]{1,0:T(8,128)(2,1)S(1)}, bf16[256,1152]{1,0:T(8,128)(2,1)S(1)}, u32[]{:S(2)}, u32[]{:S(2)}) collective-permute-start(bf16[256,1152]{1,0:T(8,128)(2,1)S(1)} %get-tuple-element.681), channel_id=1, source_target_pairs={{8,0},{16,8},{24,16},{28,24},{20,28},{12,20},{4,12},{0,4},{9,1},{1... | collective-permute-start | bytes 1769480 | tf_op jit(solution)/shard_map/ppermute | solution.py:76
  647.4 48.5 %collective-permute-start.92 = (bf16[128,2048]{1,0:T(8,128)(2,1)S(1)}, bf16[128,2048]{1,0:T(8,128)(2,1)S(1)}, u32[]{:S(2)}, u32[]{:S(2)}) collective-permute-start(bf16[128,2048]{1,0:T(8,128)(2,1)S(1)} %add_convert_fusion.18), channel_id=1, source_target_pairs={{8,0},{16,8},{24,16},{28,24},{20,28},{12,20},{4,12},{0,4},{9,1},{1... | collective-permute-start | bytes 1572872 | tf_op jit(solution)/shard_map/ppermute | solution.py:76
  659.4 36.5 %collective-permute-start.91 = (bf16[128,2048]{1,0:T(8,128)(2,1)S(1)}, bf16[128,2048]{1,0:T(8,128)(2,1)S(1)}, u32[]{:S(2)}, u32[]{:S(2)}) collective-permute-start(bf16[128,2048]{1,0:T(8,128)(2,1)S(1)} %add_convert_fusion.19), channel_id=1, source_target_pairs={{0,8},{8,16},{16,24},{24,28},{28,20},{20,12},{12,4},{4,0},{1,9},{9... | collective-permute-start | bytes 1572872 | tf_op jit(solution)/shard_map/ppermute | solution.py:73
  670.9 38.1 %collective-permute-start.103 = (bf16[256,2048]{1,0:T(8,128)(2,1)}, bf16[256,2048]{1,0:T(8,128)(2,1)}, u32[]{:S(2)}, u32[]{:S(2)}) collective-permute-start(bf16[256,2048]{1,0:T(8,128)(2,1)} %get-tuple-element.664), channel_id=1, source_target_pairs={{0,8},{8,16},{16,24},{24,28},{28,20},{20,12},{12,4},{4,0},{1,9},{9... | collective-permute-start | bytes 3145736 | tf_op jit(solution)/shard_map/ppermute | solution.py:73
  695.2 26.5 %collective-permute-start.104 = (bf16[256,2048]{1,0:T(8,128)(2,1)}, bf16[256,2048]{1,0:T(8,128)(2,1)}, u32[]{:S(2)}, u32[]{:S(2)}) collective-permute-start(bf16[256,2048]{1,0:T(8,128)(2,1)} %get-tuple-element.663), channel_id=1, source_target_pairs={{8,0},{16,8},{24,16},{28,24},{20,28},{12,20},{4,12},{0,4},{9,1},{1... | collective-permute-start | bytes 3145736 | tf_op jit(solution)/shard_map/ppermute | solution.py:76
  698.3 26.8 %collective-permute-start.101 = (bf16[1024,128]{1,0:T(8,128)(2,1)}, bf16[1024,128]{1,0:T(8,128)(2,1)}, u32[]{:S(2)}, u32[]{:S(2)}) collective-permute-start(bf16[1024,128]{1,0:T(8,128)(2,1)} %get-tuple-element.727), channel_id=1, source_target_pairs={{0,1},{1,0},{2,3},{3,2},{4,5},{5,4},{6,7},{7,6},{8,9},{9,8},{10,11... | collective-permute-start | bytes 786440 | tf_op jit(solution)/shard_map/ppermute | solution.py:55
  700.9 35.5 %collective-permute-start.100 = (bf16[256,1152]{1,0:T(8,128)(2,1)}, bf16[256,1152]{1,0:T(8,128)(2,1)}, u32[]{:S(2)}, u32[]{:S(2)}) collective-permute-start(bf16[256,1152]{1,0:T(8,128)(2,1)} %get-tuple-element.679), channel_id=1, source_target_pairs={{8,0},{16,8},{24,16},{28,24},{20,28},{12,20},{4,12},{0,4},{9,1},{1... | collective-permute-start | bytes 1769480 | tf_op jit(solution)/shard_map/ppermute | solution.py:76
  702.4 34.0 %collective-permute-start.99 = (bf16[256,1152]{1,0:T(8,128)(2,1)}, bf16[256,1152]{1,0:T(8,128)(2,1)}, u32[]{:S(2)}, u32[]{:S(2)}) collective-permute-start(bf16[256,1152]{1,0:T(8,128)(2,1)} %get-tuple-element.680), channel_id=1, source_target_pairs={{0,8},{8,16},{16,24},{24,28},{28,20},{20,12},{12,4},{4,0},{1,9},{9... | collective-permute-start | bytes 1769480 | tf_op jit(solution)/shard_map/ppermute | solution.py:73
  728.7 22.8 %collective-permute-start.112 = (bf16[128,2048]{1,0:T(8,128)(2,1)}, bf16[128,2048]{1,0:T(8,128)(2,1)S(1)}, u32[]{:S(2)}, u32[]{:S(2)}) collective-permute-start(bf16[128,2048]{1,0:T(8,128)(2,1)} %add_convert_fusion.16), channel_id=1, source_target_pairs={{8,0},{16,8},{24,16},{28,24},{20,28},{12,20},{4,12},{0,4},{9,1},{1... | collective-permute-start | bytes 1572872 | tf_op jit(solution)/shard_map/ppermute | solution.py:76
  738.5 26.0 %collective-permute-start.113 = (bf16[2,64,2048]{2,1,0:T(8,128)(2,1)}, bf16[2,64,2048]{2,1,0:T(8,128)(2,1)}, u32[]{:S(2)}, u32[]{:S(2)}) collective-permute-start(bf16[2,64,2048]{2,1,0:T(8,128)(2,1)} %pad_maximum_fusion.22), channel_id=1, source_target_pairs={{0,2},{1,3},{2,0},{3,1},{4,6},{5,7},{6,4},{7,5},{8,10},{9,11},{10,... | collective-permute-start | bytes 1572872 | tf_op jit(solution)/shard_map/ppermute | solution.py:59
  811.8 30.4 %collective-permute-start.127 = (f32[148,128]{1,0:T(8,128)S(1)}, f32[148,128]{1,0:T(8,128)S(1)}, u32[]{:S(2)}, u32[]{:S(2)}) collective-permute-start(f32[148,128]{1,0:T(8,128)S(1)} %concatenate.193), channel_id=1, source_target_pairs={{0,4},{4,0},{8,12},{12,8},{16,20},{20,16},{24,28},{28,24},{1,5},{5... | collective-permute-start | bytes 227336 | tf_op jit(solution)/shard_map/ppermute | solution.py:1106
  815.8 45.6 %collective-permute-start.125 = (bf16[256,2048]{1,0:T(8,128)(2,1)S(1)}, bf16[256,2048]{1,0:T(8,128)(2,1)S(1)}, u32[]{:S(2)}, u32[]{:S(2)}) collective-permute-start(bf16[256,2048]{1,0:T(8,128)(2,1)S(1)} %fusion.7), channel_id=1, source_target_pairs={{0,2},{1,3},{2,0},{3,1},{4,6},{5,7},{6,4},{7,5},{8,10},{9,11},{10,... | collective-permute-start | bytes 3145736 | tf_op jit(solution)/shard_map/ppermute | solution.py:59
  827.3 34.0 %collective-permute-start.120 = (bf16[256,1024]{1,0:T(8,128)(2,1)S(1)}, bf16[256,1024]{1,0:T(8,128)(2,1)S(1)}, u32[]{:S(2)}, u32[]{:S(2)}) collective-permute-start(bf16[256,1024]{1,0:T(8,128)(2,1)S(1)} %get-tuple-element.695), channel_id=1, source_target_pairs={{0,8},{8,16},{16,24},{24,28},{28,20},{20,12},{12,4},{4,0},{1,9},{9... | collective-permute-start | bytes 1572872 | tf_op jit(solution)/shard_map/ppermute | solution.py:73
  (245 other events, 3150.5 us)

commit v3 on v2

--- a/solution.py
+++ b/solution.py
@@ -302,34 +302,43 @@
     inner = mm_nt(c, b)
     lanes = lax.broadcasted_iota(jnp.int32, (CHUNK, PAIR), 1)
     subs = lax.broadcasted_iota(jnp.int32, (PAIR, N), 0)
-    for p in range(PAIRS):
-        span = slice(PAIR * p, PAIR * (p + 1))
-        h = 2 * p
-
-        def pick(value):
-            return halves(value[:, h : h + 1], value[:, h + 1 : h + 2], lanes)
-
+    spans = [slice(PAIR * p, PAIR * (p + 1)) for p in range(PAIRS)]
+
+    def picked(value):
+        return [
+            halves(value[:, 2 * p : 2 * p + 1], value[:, 2 * p + 1 : 2 * p + 2], lanes)
+            for p in range(PAIRS)
+        ]
+
+    held = [state[span, :] for span in spans]
+    low = [v.astype(BF16) for v in held]
+    carried = [mm_nt(c, v) for v in low]
+    x = []
+    for span in spans:
         conv = taps_ref[0:1, span] * buf[EDGE : EDGE + CHUNK, span]
         for lag in range(1, TAPS):
             moved = buf[EDGE - lag : EDGE - lag + CHUNK, span]
             conv = conv + taps_ref[lag : lag + 1, span] * moved * marks[:, 2 + lag : 3 + lag]
         conv_ref[:, span] = conv
-        x = conv * jax.nn.sigmoid(conv)
-        scaled = (x * pick(step)).astype(BF16)
-        local = []
-        for q in (h, h + 1):
-            spread = cum[:, q : q + 1] - cum_rows[q : q + 1, :]
-            mixing = jnp.exp(jnp.where(allowed, spread, -1e30)) * inner
-            local.append(mm(mixing.astype(BF16), scaled))
-        held = state[span, :]
-        hb = held.astype(BF16)
-        st_ref[0, span, :] = hb
+        x.append(conv * jax.nn.sigmoid(conv))
+    scaled = [(v * w).astype(BF16) for v, w in zip(x, picked(step))]
+    weighed = [(v * w).astype(BF16) for v, w in zip(x, picked(weight))]
+    tails = [mm_tn(v, b) for v in weighed]
+    mixing = []
+    for q in range(HEADS):
+        spread = cum[:, q : q + 1] - cum_rows[q : q + 1, :]
+        mixing.append((jnp.exp(jnp.where(allowed, spread, -1e30)) * inner).astype(BF16))
+    local = [mm(mixing[q], scaled[q // 2]) for q in range(HEADS)]
+    reach2 = picked(reach)
+    for p, span in enumerate(spans):
+        st_ref[0, span, :] = low[p]
         y_ref[:, span] = (
-            halves(local[0], local[1], lanes) + pick(reach) * mm_nt(c, hb) + skip_ref[:, span] * x
+            halves(local[2 * p], local[2 * p + 1], lanes)
+            + reach2[p] * carried[p]
+            + skip_ref[:, span] * x[p]
         )
-        tail = mm_tn((pick(weight) * x).astype(BF16), b)
-        kept = jnp.where(subs < P_SIZE, through[:, h : h + 1], through[:, h + 1 : h + 2])
-        state[span, :] = kept * held + tail
+        kept = jnp.where(subs < P_SIZE, through[:, 2 * p : 2 * p + 1], through[:, 2 * p + 1 : 2 * p + 2])
+        state[span, :] = kept * held[p] + tails[p]
 
 
 def ssd_backward_kernel(first, *refs):
@@ -575,8 +584,13 @@
 
 
 def attention_forward_kernel(q_ref, k_ref, v_ref, segc_ref, segr_ref, o_ref):
-    probs = attention_probs(q_ref[...], k_ref[...], segc_ref[...], segr_ref[...], pl.program_id(1))
-    o_ref[...] = mm(probs.astype(BF16), v_ref[...]).astype(BF16)
+    for i in range(k_ref.shape[0] // Q_BLOCK):
+
+        @pl.when(pl.program_id(1) == i)
+        def _():
+            seen = slice(0, (i + 1) * Q_BLOCK)
+            probs = attention_probs(q_ref[...], k_ref[seen, :], segc_ref[...], segr_ref[:, seen], i)
+            o_ref[...] = mm(probs.astype(BF16), v_ref[seen, :]).astype(BF16)
 
 
 def attention_backward_kernel(
@@ -587,14 +601,19 @@
         dk_ref[...] = jnp.zeros_like(dk_ref)
         dv_ref[...] = jnp.zeros_like(dv_ref)
 
-    q, k, g = q_ref[...], k_ref[...], g_ref[...]
-    probs = attention_probs(q, k, segc_ref[...], segr_ref[...], pl.program_id(1))
-    d_probs = mm_nt(g, v_ref[...])
-    inner = jnp.sum(probs * d_probs, axis=-1, keepdims=True)
-    d_scores = (probs * (d_probs - inner)).astype(BF16)
-    dq_ref[...] = mm(d_scores, k) * SCALE
-    dk_ref[...] += mm_tn(d_scores, q) * SCALE
-    dv_ref[...] += mm_tn(probs.astype(BF16), g)
+    for i in range(k_ref.shape[0] // Q_BLOCK):
+
+        @pl.when(pl.program_id(1) == i)
+        def _():
+            seen = slice(0, (i + 1) * Q_BLOCK)
+            q, k, g = q_ref[...], k_ref[seen, :], g_ref[...]
+            probs = attention_probs(q, k, segc_ref[...], segr_ref[:, seen], i)
+            d_probs = mm_nt(g, v_ref[seen, :])
+            inner = jnp.sum(probs * d_probs, axis=-1, keepdims=True)
+            d_scores = (probs * (d_probs - inner)).astype(BF16)
+            dq_ref[...] = mm(d_scores, k) * SCALE
+            dk_ref[seen, :] += mm_tn(d_scores, q) * SCALE
+            dv_ref[seen, :] += mm_tn(probs.astype(BF16), g)
 
 
 def attention_specs(tokens):
@@ -781,12 +800,11 @@
     near_normed.far, near_seg.last = turn(g_first, near_normed.far, near_seg.last)
     near_normed.cross()
     g_second = start(spread_two.block())
-    (near_normed.last,) = gate(near_normed.last)
+    place = jnp.arange(length, dtype=jnp.int32)
+    near_normed.last, conv_taps, decay_log, skip_gain, step_bias, place = finish(
+        g_down, near_normed.last, conv_taps, decay_log, skip_gain, step_bias, place
+    )
     normed = absolute(near_normed.blocks(), j).reshape(length, MODEL_WIDTH)
-    place = jnp.arange(length, dtype=jnp.int32)
-    normed, conv_taps, decay_log, skip_gain, step_bias, place = finish(
-        g_down, normed, conv_taps, decay_log, skip_gain, step_bias, place
-    )
     w_down = g_down.whole
 
     seg = absolute(near_seg.blocks(), j).reshape(length)
@@ -840,7 +858,7 @@
     g_out = start(both_out, lambda b: home(b))
     upper, core = j // 2, j % 2
     mine = (jnp.where(upper == 0, conv_b_own, b_far), jnp.where(upper == 0, b_far, conv_b_own))
-    b_other = turn(g_second, b_other)
+    (b_other,) = gate(b_other)
     theirs = (
         jnp.where(upper == 0, b_other[:, :WB], b_other[:, WB:]),
         jnp.where(upper == 0, b_other[:, WB:], b_other[:, :WB]),
@@ -856,10 +874,12 @@
     )
     rest_ssd = (step_raw, own_bias, own_log, taps_x, taps_b, marks, row, skip_wide)
     ssm_y, saved = ssd_forward(conv_x, conv_b, *rest_ssd)
-    ssm_y, normed, spread_gu.across = finish(g_second, ssm_y, normed, spread_gu.across)
+    ssm_y, normed = turn(g_second, ssm_y, normed)
+    ssm_y, normed = turn(g_out, ssm_y, normed)
+    normed, spread_gu.across = finish(g_second, normed, spread_gu.across)
     w_second = g_second.whole
-    normed = turn(g_out, normed)
     rest = mm(normed, w_second)
+    rest = turn(g_out, rest)
     gate_z = rest[:, WQ + HEAD_SIZE :]
     queries = turned(rest[:, :WQ], cosine, sine).astype(BF16)
     kv_raw = rest[:, WQ : WQ + HEAD_SIZE]
@@ -908,13 +928,9 @@
     normed_two = list(finish(g_gu, *normed_two))
     w_gu = g_gu.whole
 
-    gates = {}
-    hidden_all = jnp.zeros((length, WF), BF16)
-    for k in reversed(range(NC)):
-        gateup = mm(normed_two[k], w_gu)
-        gates[k] = gateup
-        piece = (jax.nn.silu(gateup[:, :WF]) * gateup[:, WF:]).astype(BF16)
-        hidden_all = lax.dynamic_update_slice(hidden_all, piece, (k * own, 0))
+    (normed_two_all,) = gate(normed_two_all)
+    gateup = mm(normed_two_all, w_gu)
+    hidden_all = (jax.nn.silu(gateup[:, :WF]) * gateup[:, WF:]).astype(BF16)
 
     def near_rows(value, far):
         return value[2 * own :] if far else value[: 2 * own]
@@ -940,25 +956,25 @@
     near_ffn = Near(grad_ffn_own)
     d_gateup_all = jnp.zeros((length, 2 * WF), BF16)
 
-    def ffn_back(whole, grad, k):
+    def ffn_back(whole, grad, at):
         d_hidden = mm_nt(grad, w_down)
-        gate_k, up_k = gates[k][:, :WF], gates[k][:, WF:]
+        part = gateup[at : at + grad.shape[0]]
+        gate_k, up_k = part[:, :WF], part[:, WF:]
         d_gate = (d_hidden * up_k * silu_slope(gate_k)).astype(BF16)
         d_up = (d_hidden * jax.nn.silu(gate_k)).astype(BF16)
-        whole = lax.dynamic_update_slice(whole, d_gate, (k * own, 0))
-        return lax.dynamic_update_slice(whole, d_up, (k * own, WF))
+        whole = lax.dynamic_update_slice(whole, d_gate, (at, 0))
+        return lax.dynamic_update_slice(whole, d_up, (at, WF))
 
     d_gateup_all = ffn_back(d_gateup_all, near_ffn.own, 0)
-    d_gateup_all = ffn_back(d_gateup_all, near_ffn.next, 1)
+    d_gateup_all = ffn_back(d_gateup_all, near_ffn.next, own)
     near_ffn.far, near_ffn.next, near_ffn.own, d_gateup_all = gate(
         near_ffn.far, near_ffn.next, near_ffn.own, d_gateup_all
     )
     near_ffn.cross()
-    d_gateup_all = ffn_back(d_gateup_all, near_ffn.far, 2)
-    d_gateup_all, near_ffn.last = gate(d_gateup_all, near_ffn.last)
+    (near_ffn.last,) = gate(near_ffn.last)
     grad_ffn_all = stacked(near_ffn.blocks())
+    d_gateup_all = ffn_back(d_gateup_all, near_rows(grad_ffn_all, True), 2 * own)
     r_down = reduce(hidden_all, grad_ffn_all)
-    d_gateup_all = ffn_back(d_gateup_all, near_ffn.last, 3)
     (d_gateup_all,) = gate(d_gateup_all)
 
     d_gateup_all = turn(r_down, d_gateup_all)
@@ -1077,7 +1093,7 @@
         return addends
 
     back_sum = NearSum(normed_part, core, True)
-    back_sum.third, d_first = gate(back_sum.third, d_first)
+    back_sum.third, d_first = turn(r_first, back_sum.third, d_first)
     held = [d_first]
     back_sum.go()
     back_sum.stay()
@@ -1104,20 +1120,21 @@
     moves += [("ctx", NC, 1), ("ctx", NC, 2)]
     for axis, size, bit in moves:
         small = small + lax.ppermute(small, axis, [(q, q ^ bit) for q in range(size)])
-    back_sum.first = turn(r_first, back_sum.first)
-    back_sum.second, back_sum.first = gate(back_sum.second, back_sum.first)
+    back_sum.first = finish(r_first, back_sum.first)
+    col_first = collected(r_first)
+    back_sum.second, back_sum.first, col_first.got = gate(
+        back_sum.second, back_sum.first, col_first.got
+    )
+    col_first.cross()
     grad_normed = back_sum.result()
     grad_tokens = grad_hidden_one + norm_back(grad_normed, x, r_x, norm_first)
-    grad_tokens = finish(r_first, grad_tokens)
-    col_first = collected(r_first)
-    col_first.got, small, grad_tokens = gate(col_first.got, small, grad_tokens)
+    small, grad_tokens = gate(small, grad_tokens)
     lines = MODEL_WIDTH // 128
     g_norm_first = small[:lines].reshape(MODEL_WIDTH)
     g_norm_second = small[lines : 2 * lines].reshape(MODEL_WIDTH)
     taps_all = small[2 * lines : -4].reshape(TAPS, DI + 2 * N)
     per_head = small[-4:-1, :H_M]
     loss_value = small[-1, 0] / (MODEL_WIDTH * count) + order.token[0, 0]
-    col_first.cross()
 
     got_gu = col_gu.result()
     grad_gate_up = (

time: 904 us -> 881 us (0.975)
  matrix products: 157 us -> 132 us
  other arithmetic: 96.9 us -> 116 us
  starting transfers between devices: 138 us -> 127 us
    ppermute x40, starting transfers between devices: 53 us -> 39.1 us  [up(): return lax.ppermute(value, 'batch', self.up_pairs)]
    dot_general x10 -> x9, matrix products: 66.1 us -> 53.2 us  [mm_nt(): lax.dot_general(left, right, (((1,), (1,)), ((), ())), preferred_element_...]
    ppermute x40, waiting for transfers between devices: 95.2 us -> 84.7 us  [down(): return lax.ppermute(value, 'batch', self.down_pairs)]
    dot_general x12 -> x9, matrix products: 52.1 us -> 43.8 us  [mm(): return jnp.dot(left, right, preferred_element_type=F32)]
    unnamed x328 -> x313, local copies, waits for them, and re-layouts: 19.8 us -> 27.2 us
  transfers between devices with their start and end apart: 133 -> 133, of which waited for: 56 -> 60; matrix products, arithmetic and copies ran while one was open for 34% -> 36% of each run, Pallas kernels for 7% -> 7%
where the time goes in v3:
time: 881 us; the launch traced here: 871 us
  waiting for transfers between devices  247 us (28%)
  local copies, waits for them, and re-layouts  166 us (19%)
  matrix products  132 us (15%)
  starting transfers between devices  127 us (14%)
  other arithmetic  116 us (13%)
  Pallas kernels  72.7 us (8%)
  between operations  10.8 us (1%)
    ppermute x40, waiting for transfers between devices, down(): return lax.ppermute(value, 'batch', self.down_pairs)  84.7 us
    ppermute x17, waiting for transfers between devices, y_swap(): return lax.ppermute(value, 'ctx', [(i, i ^ 2) for i in range(NC)])  70.1 us
    ppermute x40, waiting for transfers between devices, up(): return lax.ppermute(value, 'batch', self.up_pairs)  67.9 us
    dot_general x9, matrix products, mm_nt(): lax.dot_general(left, right, (((1,), (1,)), ((), ())), preferred_element_...  53.2 us
    ppermute x40, starting transfers between devices, down(): return lax.ppermute(value, 'batch', self.down_pairs)  52.7 us
    dot_general x9, matrix products, mm(): return jnp.dot(left, right, preferred_element_type=F32)  43.8 us
    pallas_call x2, Pallas kernels, ssd_backward(): pl.pallas_call(functools.partial(ssd_backward_kernel, part * PAIRS // 2),...  42.3 us
    dynamic_update_slice x45, local copies, waits for them, and re-layouts, put(): self.whole = lax.dynamic_update_slice(self.whole, part, (at, 0))  42.1 us
  transfers between devices with their start and end apart: 133, of which 60 were waited for; matrix products, arithmetic and copies ran while one was open for 36% of the time, Pallas kernels for 7%

profile of v3, /device:TPU:0, one launch (start us, length us, event | category | flops | bytes accessed | tf_op | source)
XLA Modules:
  0.0 871.4 jit_solution(9566206782957863635)
XLA Ops:
  19.2 5.4 collective-permute-start.8
  51.4 5.0 collective-permute-done.9
  79.6 8.0 collective-permute-done.16
  144.6 6.6 fusion.19.x_ref.refs_1_.refs_2_
  151.2 4.1 fusion.48.raw_ref.refs_12_
  167.4 15.8 %ssd_forward.1 = (f32[1024,768]{1,0:T(8,128)S(1)}, bf16[8,768,256]{2,1,0:T(8,128)(2,1)S(1)}, f32[1024,768]{1,0:T(8,128)}, bf16[1024,512]{1,0:T(8,128)(2,1)S(1)},...) custom-call(bf16[1024,768]{1,0:T(8,128)(2,1)S(1)} %fusion.19.x_ref.r, ...), custom_call_target="tpu_custom_call" | custom-call | tf_op jit(solution)/shard_map/ssd_forward/pallas_call | solution.py:508
  197.7 8.8 %fusion.109 = f32[1024,1152]{1,0:T(8,128)S(1)} fusion(bf16[1024,2048]{1,0:T(8,128)(2,1)} %bitcast.32, bf16[2048,1152]{1,0:T(8,128)(2,1)} %constant_dynamic-update-slice_fusion.35), kind=kOutput, calls=%fused_computation.453 | convolution fusion | flops 4831838208 | bytes 13631488 | tf_op jit(solution)/shard_map/dot_general | solution.py:39
  210.4 11.8 %collective-permute-done.43 = bf16[128,2048]{1,0:T(8,128)(2,1)S(1)} collective-permute-done((bf16[128,2048]{1,0:T(8,128)(2,1)S(1)}, bf16[128,2048]{1,0:T(8,128)(2,1)S(1)}, u32[]{:S(2)}, u32[]{:S(2)}) %collective-permute-start.43) | collective-permute-done | bytes 524320 | tf_op jit(solution)/shard_map/ppermute | solution.py:76
  225.6 6.0 attention_forward.1
  240.2 4.9 fusion.24
  256.8 6.9 collective-permute-done.46
  266.0 10.6 %collective-permute-done.52 = bf16[256,2048]{1,0:T(8,128)(2,1)} collective-permute-done((bf16[256,2048]{1,0:T(8,128)(2,1)}, bf16[256,2048]{1,0:T(8,128)(2,1)}, u32[]{:S(2)}, u32[]{:S(2)}) %collective-permute-start.52) | collective-permute-done | bytes 1048608 | tf_op jit(solution)/shard_map/ppermute | solution.py:59
  297.9 11.6 %collective-permute-done.58 = bf16[256,2048]{1,0:T(8,128)(2,1)} collective-permute-done((bf16[256,2048]{1,0:T(8,128)(2,1)S(1)}, bf16[256,2048]{1,0:T(8,128)(2,1)}, u32[]{:S(2)}, u32[]{:S(2)}) %collective-permute-start.58) | collective-permute-done | bytes 1048608 | tf_op jit(solution)/shard_map/ppermute | solution.py:59
  322.7 8.0 collective-permute-done.60
  332.9 8.8 %fusion.110 = f32[1024,2048]{1,0:T(8,128)S(1)} fusion(bf16[1024,2048]{1,0:T(8,128)(2,1)S(1)} %constant_dynamic-update-slice_fusion.23, bf16[2048,2048]{1,0:T(8,128)(2,1)S(1)} %constant_dynamic-update-slice_fusion.14), kind=kOutput, calls=%fused_computation.454 | convolution fusion | flops 8589934592 | bytes 20971520 | tf_op jit(solution)/shard_map/dot_general | solution.py:39
  360.6 16.5 %collective-permute-done.64 = bf16[256,2048]{1,0:T(8,128)(2,1)} collective-permute-done((bf16[256,2048]{1,0:T(8,128)(2,1)}, bf16[256,2048]{1,0:T(8,128)(2,1)}, u32[]{:S(2)}, u32[]{:S(2)}) %collective-permute-start.64) | collective-permute-done | bytes 1048608 | tf_op jit(solution)/shard_map/ppermute | solution.py:59
  377.1 4.2 multiply_reduce_fusion.3
  390.8 16.5 %collective-permute-done.65 = bf16[256,2048]{1,0:T(8,128)(2,1)S(1)} collective-permute-done((bf16[256,2048]{1,0:T(8,128)(2,1)S(1)}, bf16[256,2048]{1,0:T(8,128)(2,1)S(1)}, u32[]{:S(2)}, u32[]{:S(2)}) %collective-permute-start.65) | collective-permute-done | bytes 1048608 | tf_op jit(solution)/shard_map/ppermute | solution.py:59
  412.1 4.9 convolution_convert_fusion.4
  417.0 7.2 fusion.30
  428.3 5.4 collective-permute-done.68
  435.0 4.5 fusion.16
  442.5 4.5 fusion.14
  461.4 8.5 collective-permute-done.70
  471.0 7.9 collective-permute-done.74
  481.4 4.7 fusion.94
  491.5 10.8 %collective-permute-done.75 = bf16[128,2048]{1,0:T(8,128)(2,1)S(1)} collective-permute-done((bf16[128,2048]{1,0:T(8,128)(2,1)S(1)}, bf16[128,2048]{1,0:T(8,128)(2,1)S(1)}, u32[]{:S(2)}, u32[]{:S(2)}) %collective-permute-start.75) | collective-permute-done | bytes 524320 | tf_op jit(solution)/shard_map/ppermute | solution.py:73
  502.4 10.9 %convolution_convert_fusion.1 = bf16[2048,2048]{1,0:T(8,128)(2,1)S(1)} fusion(bf16[1024,2048]{1,0:T(8,128)(2,1)} %copy-done.74, bf16[1024,2048]{1,0:T(8,128)(2,1)S(1)} %copy-done.69), kind=kOutput, calls=%fused_computation.1 | convolution fusion | flops 8594128896 | bytes 16777216 | tf_op jit(solution)/shard_map/dot_general | solution.py:43
  520.3 8.3 collective-permute-done.78
  534.3 6.6 fusion.22
  543.9 4.9 convolution_convert_fusion.3
  551.4 8.7 attention_backward.1
  572.9 7.6 convolution_convert_fusion
  597.1 20.9 %ssd_backward.2 = (bf16[1024,768]{1,0:T(8,128)(2,1)S(1)}, f32[4,1024,128]{2,1,0:T(8,128)S(1)}, f32[1024,128]{1,0:T(8,128)S(1)}, f32[8,128]{1,0:T(8,128)S(1)}, f32[8,384]{1,0:T(8,128)S(1)}) custom-call(f32[1024,768]{1,0:T(8,128)S(1)} %get-tuple-element.520.refs_0_, bf16[1024,768]{1,0:T(8,128)(2,1)S(1)} %copy-done.1, bf16[1024,768]{1,0:T(8,128)(2,1)S(1)} %copy-done.1, ...), custom_call_target="tpu_custom_call" | custom-call | tf_op jit(solution)/shard_map/ssd_backward/pallas_call | solution.py:544
  628.4 10.1 %fusion.111 = f32[1024,2048]{1,0:T(8,128)} fusion(bf16[1024,1152]{1,0:T(8,128)(2,1)S(1)} %copy-done.95, bf16[2048,1152]{1,0:T(8,128)(2,1)} %constant_dynamic-update-slice_fusion.35), kind=kOutput, calls=%fused_computation.455 | convolution fusion | flops 4831838208 | bytes 15466496 | tf_op jit(solution)/shard_map/dot_general | solution.py:47
  639.3 5.1 collective-permute-done.98
  648.8 21.4 %ssd_backward.3 = (bf16[1024,768]{1,0:T(8,128)(2,1)S(1)}, f32[4,1024,128]{2,1,0:T(8,128)S(1)}, f32[1024,128]{1,0:T(8,128)S(1)}, f32[8,128]{1,0:T(8,128)S(1)}, f32[8,384]{1,0:T(8,128)S(1)}) custom-call(f32[1024,768]{1,0:T(8,128)} %copy-done.2, bf16[1024,768]{1,0:T(8,128)(2,1)S(1)} %copy-done.1, ...), custom_call_target="tpu_custom_call", output_to_operand_aliasing={{0}: (22, {})} | custom-call | tf_op jit(solution)/shard_map/ssd_backward/pallas_call | solution.py:544
  684.2 12.4 %collective-permute-done.104 = bf16[256,2048]{1,0:T(8,128)(2,1)} collective-permute-done((bf16[256,2048]{1,0:T(8,128)(2,1)}, bf16[256,2048]{1,0:T(8,128)(2,1)}, u32[]{:S(2)}, u32[]{:S(2)}) %collective-permute-start.104) | collective-permute-done | bytes 1048608 | tf_op jit(solution)/shard_map/ppermute | solution.py:76
  705.8 5.2 collective-permute-done.102
  720.3 7.2 convolution_convert_fusion.2
  743.1 7.3 collective-permute-done.109
  754.3 5.8 dynamic-slice_add_fusion.1
  775.5 8.2 collective-permute-done.115
  783.7 9.1 %multiply_reduce_fusion = (f32[2048]{0:T(1024)S(1)}, f32[2048]{0:T(1024)S(1)}, f32[512,2048]{1,0:T(8,128)S(1)}) fusion(bf16[1024,2048]{1,0:T(8,128)(2,1)} %bitcast.32, s32[]{:T(128)S(6)} %select_n.920, f32[512,2048]{1,0:T(8,128)} %copy-done.50, s32[]{:T(128)S(6)} %select_n.964, f32[1024,2048]{1,0:T(8,128)} %fusion.111, ...), kind=kOutput, calls=%fused_computation.5 | convolution fusion | flops 2154819584 | bytes 22038016 | tf_op jit(solution)/shard_map/dot_general | solution.py:47
  800.1 9.5 %collective-permute-start.127 = (bf16[256,2048]{1,0:T(8,128)(2,1)}, bf16[256,2048]{1,0:T(8,128)(2,1)}, u32[]{:S(2)}, u32[]{:S(2)}) collective-permute-start(bf16[256,2048]{1,0:T(8,128)(2,1)} %fusion.12), channel_id=1, source_target_pairs={{0,2},{1,3},{2,0},{3,1},{4,6},{5,7},{6,4},{7,5},{8,10},{9,11},{10,... | collective-permute-start | bytes 3145736 | tf_op jit(solution)/shard_map/ppermute | solution.py:59
  814.2 5.4 collective-permute-start.128
  824.0 8.4 collective-permute-done.122
  832.6 4.3 collective-permute-done.123
  (907 shorter events, 455.7 us)
Async XLA Ops:
  19.2 39.0 %collective-permute-start.8 = (bf16[128,2048]{1,0:T(8,128)(2,1)}, bf16[128,2048]{1,0:T(8,128)(2,1)}, u32[]{:S(2)}, u32[]{:S(2)}) collective-permute-start(bf16[128,2048]{1,0:T(8,128)(2,1)} %pad_maximum_fusion.11), channel_id=1, source_target_pairs={{0,0},{1,16},{2,8},{3,24},{4,4},{5,20},{6,12},{7,28},{8,1},{9,17},... | collective-permute-start | bytes 1572872 | tf_op jit(solution)/shard_map/ppermute | solution.py:760
  32.6 23.8 %collective-permute-start.9 = (bf16[128,2048]{1,0:T(8,128)(2,1)}, bf16[128,2048]{1,0:T(8,128)(2,1)}, u32[]{:S(2)}, u32[]{:S(2)}) collective-permute-start(bf16[128,2048]{1,0:T(8,128)(2,1)} %collective-permute-done), channel_id=1, source_target_pairs={{8,0},{16,8},{24,16},{28,24},{20,28},{12,20},{4,12},{0,4},{9,1},{1... | collective-permute-start | bytes 1572872 | tf_op jit(solution)/shard_map/ppermute | solution.py:76
  56.4 23.2 %collective-permute-start.18 = (bf16[256,2048]{1,0:T(8,128)(2,1)}, bf16[256,2048]{1,0:T(8,128)(2,1)}, u32[]{:S(2)}, u32[]{:S(2)}) collective-permute-start(bf16[256,2048]{1,0:T(8,128)(2,1)} %get-tuple-element.654), channel_id=1, source_target_pairs={{0,2},{1,3},{2,0},{3,1},{4,6},{5,7},{6,4},{7,5},{8,10},{9,11},{10,... | collective-permute-start | bytes 3145736 | tf_op jit(solution)/shard_map/ppermute | solution.py:59
  79.6 35.8 %collective-permute-start.24 = (bf16[2,64,2048]{2,1,0:T(8,128)(2,1)}, bf16[2,64,2048]{2,1,0:T(8,128)(2,1)S(1)}, u32[]{:S(2)}, u32[]{:S(2)}) collective-permute-start(bf16[2,64,2048]{2,1,0:T(8,128)(2,1)} %pad_maximum_fusion.12), channel_id=1, source_target_pairs={{0,2},{1,3},{2,0},{3,1},{4,6},{5,7},{6,4},{7,5},{8,10},{9,11},{10,... | collective-permute-start | bytes 1572872 | tf_op jit(solution)/shard_map/ppermute | solution.py:59
  88.4 26.7 %collective-permute-start.27 = (bf16[256,2048]{1,0:T(8,128)(2,1)}, bf16[256,2048]{1,0:T(8,128)(2,1)}, u32[]{:S(2)}, u32[]{:S(2)}) collective-permute-start(bf16[256,2048]{1,0:T(8,128)(2,1)} %collective-permute-done.18), channel_id=1, source_target_pairs={{0,1},{1,0},{2,3},{3,2},{4,5},{5,4},{6,7},{7,6},{8,9},{9,8},{10,11... | collective-permute-start | bytes 3145736 | tf_op jit(solution)/shard_map/ppermute | solution.py:55
  113.3 29.2 %collective-permute-start.20 = (bf16[256,1152]{1,0:T(8,128)(2,1)}, bf16[256,1152]{1,0:T(8,128)(2,1)}, u32[]{:S(2)}, u32[]{:S(2)}) collective-permute-start(bf16[256,1152]{1,0:T(8,128)(2,1)} %bitcast.14), channel_id=1, source_target_pairs={{8,0},{16,8},{24,16},{28,24},{20,28},{12,20},{4,12},{0,4},{9,1},{1... | collective-permute-start | bytes 1769480 | tf_op jit(solution)/shard_map/ppermute | solution.py:76
  115.1 27.5 %collective-permute-start.21 = (bf16[256,1152]{1,0:T(8,128)(2,1)}, bf16[256,1152]{1,0:T(8,128)(2,1)}, u32[]{:S(2)}, u32[]{:S(2)}) collective-permute-start(bf16[256,1152]{1,0:T(8,128)(2,1)} %bitcast.14), channel_id=1, source_target_pairs={{0,8},{8,16},{16,24},{24,28},{28,20},{20,12},{12,4},{4,0},{1,9},{9... | collective-permute-start | bytes 1769480 | tf_op jit(solution)/shard_map/ppermute | solution.py:73
  159.4 27.2 %collective-permute-start.38 = (bf16[128,2048]{1,0:T(8,128)(2,1)}, bf16[128,2048]{1,0:T(8,128)(2,1)}, u32[]{:S(2)}, u32[]{:S(2)}) collective-permute-start(bf16[128,2048]{1,0:T(8,128)(2,1)} %collective-permute-done.8), channel_id=1, source_target_pairs={{8,0},{16,8},{24,16},{28,24},{20,28},{12,20},{4,12},{0,4},{9,1},{1... | collective-permute-start | bytes 1572872 | tf_op jit(solution)/shard_map/ppermute | solution.py:76
  161.1 25.5 %collective-permute-start.39 = (bf16[128,2048]{1,0:T(8,128)(2,1)}, bf16[128,2048]{1,0:T(8,128)(2,1)}, u32[]{:S(2)}, u32[]{:S(2)}) collective-permute-start(bf16[128,2048]{1,0:T(8,128)(2,1)} %collective-permute-done.8), channel_id=1, source_target_pairs={{0,8},{8,16},{16,24},{24,28},{28,20},{20,12},{12,4},{4,0},{1,9},{9... | collective-permute-start | bytes 1572872 | tf_op jit(solution)/shard_map/ppermute | solution.py:73
  167.0 25.7 %collective-permute-start.40 = (bf16[2,64,2048]{2,1,0:T(8,128)(2,1)S(1)}, bf16[2,64,2048]{2,1,0:T(8,128)(2,1)S(1)}, u32[]{:S(2)}, u32[]{:S(2)}) collective-permute-start(bf16[2,64,2048]{2,1,0:T(8,128)(2,1)S(1)} %pad_maximum_fusion.16), channel_id=1, source_target_pairs={{0,1},{1,0},{2,3},{3,2},{4,5},{5,4},{6,7},{7,6},{8,9},{9,8},{10,11... | collective-permute-start | bytes 1572872 | tf_op jit(solution)/shard_map/ppermute | solution.py:55
  238.1 25.7 %collective-permute-start.46 = (bf16[256,2048]{1,0:T(8,128)(2,1)S(1)}, bf16[256,2048]{1,0:T(8,128)(2,1)}, u32[]{:S(2)}, u32[]{:S(2)}) collective-permute-start(bf16[256,2048]{1,0:T(8,128)(2,1)S(1)} %bitcast.268), channel_id=1, source_target_pairs={{8,0},{16,8},{24,16},{28,24},{20,28},{12,20},{4,12},{0,4},{9,1},{1... | collective-permute-start | bytes 3145736 | tf_op jit(solution)/shard_map/ppermute | solution.py:76
  238.6 25.3 %collective-permute-start.47 = (bf16[256,2048]{1,0:T(8,128)(2,1)S(1)}, bf16[256,2048]{1,0:T(8,128)(2,1)}, u32[]{:S(2)}, u32[]{:S(2)}) collective-permute-start(bf16[256,2048]{1,0:T(8,128)(2,1)S(1)} %bitcast.269), channel_id=1, source_target_pairs={{0,8},{8,16},{16,24},{24,28},{28,20},{20,12},{12,4},{4,0},{1,9},{9... | collective-permute-start | bytes 3145736 | tf_op jit(solution)/shard_map/ppermute | solution.py:73
  250.7 25.9 %collective-permute-start.52 = (bf16[256,2048]{1,0:T(8,128)(2,1)}, bf16[256,2048]{1,0:T(8,128)(2,1)}, u32[]{:S(2)}, u32[]{:S(2)}) collective-permute-start(bf16[256,2048]{1,0:T(8,128)(2,1)} %fusion.13), channel_id=1, source_target_pairs={{0,2},{1,3},{2,0},{3,1},{4,6},{5,7},{6,4},{7,5},{8,10},{9,11},{10,... | collective-permute-start | bytes 3145736 | tf_op jit(solution)/shard_map/ppermute | solution.py:59
  264.0 24.8 %collective-permute-start.53 = (bf16[256,2048]{1,0:T(8,128)(2,1)}, bf16[256,2048]{1,0:T(8,128)(2,1)}, u32[]{:S(2)}, u32[]{:S(2)}) collective-permute-start(bf16[256,2048]{1,0:T(8,128)(2,1)} %collective-permute-done.46), channel_id=1, source_target_pairs={{8,0},{16,8},{24,16},{28,24},{20,28},{12,20},{4,12},{0,4},{9,1},{1... | collective-permute-start | bytes 3145736 | tf_op jit(solution)/shard_map/ppermute | solution.py:76
  265.5 24.5 %collective-permute-start.54 = (bf16[256,2048]{1,0:T(8,128)(2,1)}, bf16[256,2048]{1,0:T(8,128)(2,1)}, u32[]{:S(2)}, u32[]{:S(2)}) collective-permute-start(bf16[256,2048]{1,0:T(8,128)(2,1)} %collective-permute-done.47), channel_id=1, source_target_pairs={{0,8},{8,16},{16,24},{24,28},{28,20},{20,12},{12,4},{4,0},{1,9},{9... | collective-permute-start | bytes 3145736 | tf_op jit(solution)/shard_map/ppermute | solution.py:73
  283.7 25.7 %collective-permute-start.58 = (bf16[256,2048]{1,0:T(8,128)(2,1)S(1)}, bf16[256,2048]{1,0:T(8,128)(2,1)}, u32[]{:S(2)}, u32[]{:S(2)}) collective-permute-start(bf16[256,2048]{1,0:T(8,128)(2,1)S(1)} %multiply_convert_fusion.3), channel_id=1, source_target_pairs={{0,2},{1,3},{2,0},{3,1},{4,6},{5,7},{6,4},{7,5},{8,10},{9,11},{10,... | collective-permute-start | bytes 3145736 | tf_op jit(solution)/shard_map/ppermute | solution.py:59
  289.9 23.4 %collective-permute-start.56 = (bf16[256,2048]{1,0:T(8,128)(2,1)}, bf16[256,2048]{1,0:T(8,128)(2,1)S(1)}, u32[]{:S(2)}, u32[]{:S(2)}) collective-permute-start(bf16[256,2048]{1,0:T(8,128)(2,1)} %collective-permute-done.53), channel_id=1, source_target_pairs={{8,0},{16,8},{24,16},{28,24},{20,28},{12,20},{4,12},{0,4},{9,1},{1... | collective-permute-start | bytes 3145736 | tf_op jit(solution)/shard_map/ppermute | solution.py:76
  291.6 23.3 %collective-permute-start.57 = (bf16[256,2048]{1,0:T(8,128)(2,1)}, bf16[256,2048]{1,0:T(8,128)(2,1)}, u32[]{:S(2)}, u32[]{:S(2)}) collective-permute-start(bf16[256,2048]{1,0:T(8,128)(2,1)} %collective-permute-done.54), channel_id=1, source_target_pairs={{0,8},{8,16},{16,24},{24,28},{28,20},{20,12},{12,4},{4,0},{1,9},{9... | collective-permute-start | bytes 3145736 | tf_op jit(solution)/shard_map/ppermute | solution.py:73
  351.5 25.5 %collective-permute-start.64 = (bf16[256,2048]{1,0:T(8,128)(2,1)}, bf16[256,2048]{1,0:T(8,128)(2,1)}, u32[]{:S(2)}, u32[]{:S(2)}) collective-permute-start(bf16[256,2048]{1,0:T(8,128)(2,1)} %fusion.9), channel_id=1, source_target_pairs={{0,2},{1,3},{2,0},{3,1},{4,6},{5,7},{6,4},{7,5},{8,10},{9,11},{10,... | collective-permute-start | bytes 3145736 | tf_op jit(solution)/shard_map/ppermute | solution.py:59
  381.7 25.6 %collective-permute-start.65 = (bf16[256,2048]{1,0:T(8,128)(2,1)S(1)}, bf16[256,2048]{1,0:T(8,128)(2,1)S(1)}, u32[]{:S(2)}, u32[]{:S(2)}) collective-permute-start(bf16[256,2048]{1,0:T(8,128)(2,1)S(1)} %fusion.18), channel_id=1, source_target_pairs={{0,2},{1,3},{2,0},{3,1},{4,6},{5,7},{6,4},{7,5},{8,10},{9,11},{10,... | collective-permute-start | bytes 3145736 | tf_op jit(solution)/shard_map/ppermute | solution.py:59
  453.2 25.7 %collective-permute-start.74 = (bf16[256,2048]{1,0:T(8,128)(2,1)}, bf16[256,2048]{1,0:T(8,128)(2,1)}, u32[]{:S(2)}, u32[]{:S(2)}) collective-permute-start(bf16[256,2048]{1,0:T(8,128)(2,1)} %fusion.4), channel_id=1, source_target_pairs={{0,2},{1,3},{2,0},{3,1},{4,6},{5,7},{6,4},{7,5},{8,10},{9,11},{10,... | collective-permute-start | bytes 3145736 | tf_op jit(solution)/shard_map/ppermute | solution.py:59
  490.5 29.8 %collective-permute-start.80 = (bf16[256,2048]{1,0:T(8,128)(2,1)S(1)}, bf16[256,2048]{1,0:T(8,128)(2,1)S(1)}, u32[]{:S(2)}, u32[]{:S(2)}) collective-permute-start(bf16[256,2048]{1,0:T(8,128)(2,1)S(1)} %get-tuple-element.483), channel_id=1, source_target_pairs={{0,2},{1,3},{2,0},{3,1},{4,6},{5,7},{6,4},{7,5},{8,10},{9,11},{10,... | collective-permute-start | bytes 3145736 | tf_op jit(solution)/shard_map/ppermute | solution.py:59
  518.1 32.8 %collective-permute-start.84 = (bf16[128,2048]{1,0:T(8,128)(2,1)}, bf16[128,2048]{1,0:T(8,128)(2,1)}, u32[]{:S(2)}, u32[]{:S(2)}) collective-permute-start(bf16[128,2048]{1,0:T(8,128)(2,1)} %get-tuple-element.733), channel_id=1, source_target_pairs={{0,8},{8,16},{16,24},{24,28},{28,20},{20,12},{12,4},{4,0},{1,9},{9... | collective-permute-start | bytes 1572872 | tf_op jit(solution)/shard_map/ppermute | solution.py:73
  519.1 31.8 %collective-permute-start.85 = (bf16[128,2048]{1,0:T(8,128)(2,1)}, bf16[128,2048]{1,0:T(8,128)(2,1)}, u32[]{:S(2)}, u32[]{:S(2)}) collective-permute-start(bf16[128,2048]{1,0:T(8,128)(2,1)} %get-tuple-element.732), channel_id=1, source_target_pairs={{8,0},{16,8},{24,16},{28,24},{20,28},{12,20},{4,12},{0,4},{9,1},{1... | collective-permute-start | bytes 1572872 | tf_op jit(solution)/shard_map/ppermute | solution.py:76
  564.0 28.0 %collective-permute-start.89 = (bf16[256,2048]{1,0:T(8,128)(2,1)S(1)}, bf16[256,2048]{1,0:T(8,128)(2,1)S(1)}, u32[]{:S(2)}, u32[]{:S(2)}) collective-permute-start(bf16[256,2048]{1,0:T(8,128)(2,1)S(1)} %get-tuple-element.660), channel_id=1, source_target_pairs={{0,8},{8,16},{16,24},{24,28},{28,20},{20,12},{12,4},{4,0},{1,9},{9... | collective-permute-start | bytes 3145736 | tf_op jit(solution)/shard_map/ppermute | solution.py:73
  565.5 28.0 %collective-permute-start.90 = (bf16[256,2048]{1,0:T(8,128)(2,1)S(1)}, bf16[256,2048]{1,0:T(8,128)(2,1)S(1)}, u32[]{:S(2)}, u32[]{:S(2)}) collective-permute-start(bf16[256,2048]{1,0:T(8,128)(2,1)S(1)} %get-tuple-element.659), channel_id=1, source_target_pairs={{8,0},{16,8},{24,16},{28,24},{20,28},{12,20},{4,12},{0,4},{9,1},{1... | collective-permute-start | bytes 3145736 | tf_op jit(solution)/shard_map/ppermute | solution.py:76
  583.0 34.9 %collective-permute-start.88 = (bf16[128,2048]{1,0:T(8,128)(2,1)}, bf16[128,2048]{1,0:T(8,128)(2,1)}, u32[]{:S(2)}, u32[]{:S(2)}) collective-permute-start(bf16[128,2048]{1,0:T(8,128)(2,1)} %fusion.71), channel_id=1, source_target_pairs={{8,0},{16,8},{24,16},{28,24},{20,28},{12,20},{4,12},{0,4},{9,1},{1... | collective-permute-start | bytes 1572872 | tf_op jit(solution)/shard_map/ppermute | solution.py:76
  584.4 34.4 %collective-permute-start.87 = (bf16[128,2048]{1,0:T(8,128)(2,1)}, bf16[128,2048]{1,0:T(8,128)(2,1)}, u32[]{:S(2)}, u32[]{:S(2)}) collective-permute-start(bf16[128,2048]{1,0:T(8,128)(2,1)} %fusion.70), channel_id=1, source_target_pairs={{0,8},{8,16},{16,24},{24,28},{28,20},{20,12},{12,4},{4,0},{1,9},{9... | collective-permute-start | bytes 1572872 | tf_op jit(solution)/shard_map/ppermute | solution.py:73
  586.7 32.1 %collective-permute-start.93 = (bf16[128,1152]{1,0:T(8,128)(2,1)}, bf16[128,1152]{1,0:T(8,128)(2,1)}, u32[]{:S(2)}, u32[]{:S(2)}) collective-permute-start(bf16[128,1152]{1,0:T(8,128)(2,1)} %get-tuple-element.747), channel_id=1, source_target_pairs={{0,8},{8,16},{16,24},{24,28},{28,20},{20,12},{12,4},{4,0},{1,9},{9... | collective-permute-start | bytes 884744 | tf_op jit(solution)/shard_map/ppermute | solution.py:73
  592.0 26.7 %collective-permute-start.94 = (bf16[128,1152]{1,0:T(8,128)(2,1)}, bf16[128,1152]{1,0:T(8,128)(2,1)}, u32[]{:S(2)}, u32[]{:S(2)}) collective-permute-start(bf16[128,1152]{1,0:T(8,128)(2,1)} %get-tuple-element.746), channel_id=1, source_target_pairs={{8,0},{16,8},{24,16},{28,24},{20,28},{12,20},{4,12},{0,4},{9,1},{1... | collective-permute-start | bytes 884744 | tf_op jit(solution)/shard_map/ppermute | solution.py:76
  595.6 42.9 %collective-permute-start.97 = (bf16[256,2048]{1,0:T(8,128)(2,1)}, bf16[256,2048]{1,0:T(8,128)(2,1)}, u32[]{:S(2)}, u32[]{:S(2)}) collective-permute-start(bf16[256,2048]{1,0:T(8,128)(2,1)} %get-tuple-element.658), channel_id=1, source_target_pairs={{0,8},{8,16},{16,24},{24,28},{28,20},{20,12},{12,4},{4,0},{1,9},{9... | collective-permute-start | bytes 3145736 | tf_op jit(solution)/shard_map/ppermute | solution.py:73
  618.0 26.4 %collective-permute-start.98 = (bf16[256,2048]{1,0:T(8,128)(2,1)}, bf16[256,2048]{1,0:T(8,128)(2,1)S(1)}, u32[]{:S(2)}, u32[]{:S(2)}) collective-permute-start(bf16[256,2048]{1,0:T(8,128)(2,1)} %get-tuple-element.657), channel_id=1, source_target_pairs={{8,0},{16,8},{24,16},{28,24},{20,28},{12,20},{4,12},{0,4},{9,1},{1... | collective-permute-start | bytes 3145736 | tf_op jit(solution)/shard_map/ppermute | solution.py:76
  621.0 49.2 %collective-permute-start.95 = (bf16[256,1152]{1,0:T(8,128)(2,1)}, bf16[256,1152]{1,0:T(8,128)(2,1)}, u32[]{:S(2)}, u32[]{:S(2)}) collective-permute-start(bf16[256,1152]{1,0:T(8,128)(2,1)} %get-tuple-element.674), channel_id=1, source_target_pairs={{0,8},{8,16},{16,24},{24,28},{28,20},{20,12},{12,4},{4,0},{1,9},{9... | collective-permute-start | bytes 1769480 | tf_op jit(solution)/shard_map/ppermute | solution.py:73
  622.3 49.3 %collective-permute-start.96 = (bf16[256,1152]{1,0:T(8,128)(2,1)}, bf16[256,1152]{1,0:T(8,128)(2,1)}, u32[]{:S(2)}, u32[]{:S(2)}) collective-permute-start(bf16[256,1152]{1,0:T(8,128)(2,1)} %get-tuple-element.673), channel_id=1, source_target_pairs={{8,0},{16,8},{24,16},{28,24},{20,28},{12,20},{4,12},{0,4},{9,1},{1... | collective-permute-start | bytes 1769480 | tf_op jit(solution)/shard_map/ppermute | solution.py:76
  625.1 46.5 %collective-permute-start.92 = (bf16[128,2048]{1,0:T(8,128)(2,1)}, bf16[128,2048]{1,0:T(8,128)(2,1)}, u32[]{:S(2)}, u32[]{:S(2)}) collective-permute-start(bf16[128,2048]{1,0:T(8,128)(2,1)} %add_convert_fusion.18), channel_id=1, source_target_pairs={{8,0},{16,8},{24,16},{28,24},{20,28},{12,20},{4,12},{0,4},{9,1},{1... | collective-permute-start | bytes 1572872 | tf_op jit(solution)/shard_map/ppermute | solution.py:76
  638.6 33.0 %collective-permute-start.91 = (bf16[128,2048]{1,0:T(8,128)(2,1)}, bf16[128,2048]{1,0:T(8,128)(2,1)S(1)}, u32[]{:S(2)}, u32[]{:S(2)}) collective-permute-start(bf16[128,2048]{1,0:T(8,128)(2,1)} %add_convert_fusion.19), channel_id=1, source_target_pairs={{0,8},{8,16},{16,24},{24,28},{28,20},{20,12},{12,4},{4,0},{1,9},{9... | collective-permute-start | bytes 1572872 | tf_op jit(solution)/shard_map/ppermute | solution.py:73
  647.7 36.5 %collective-permute-start.103 = (bf16[256,2048]{1,0:T(8,128)(2,1)}, bf16[256,2048]{1,0:T(8,128)(2,1)}, u32[]{:S(2)}, u32[]{:S(2)}) collective-permute-start(bf16[256,2048]{1,0:T(8,128)(2,1)} %get-tuple-element.656), channel_id=1, source_target_pairs={{0,8},{8,16},{16,24},{24,28},{28,20},{20,12},{12,4},{4,0},{1,9},{9... | collective-permute-start | bytes 3145736 | tf_op jit(solution)/shard_map/ppermute | solution.py:73
  670.2 26.5 %collective-permute-start.104 = (bf16[256,2048]{1,0:T(8,128)(2,1)}, bf16[256,2048]{1,0:T(8,128)(2,1)}, u32[]{:S(2)}, u32[]{:S(2)}) collective-permute-start(bf16[256,2048]{1,0:T(8,128)(2,1)} %get-tuple-element.655), channel_id=1, source_target_pairs={{8,0},{16,8},{24,16},{28,24},{20,28},{12,20},{4,12},{0,4},{9,1},{1... | collective-permute-start | bytes 3145736 | tf_op jit(solution)/shard_map/ppermute | solution.py:76
  672.5 27.7 %collective-permute-start.101 = (bf16[1024,128]{1,0:T(8,128)(2,1)}, bf16[1024,128]{1,0:T(8,128)(2,1)S(1)}, u32[]{:S(2)}, u32[]{:S(2)}) collective-permute-start(bf16[1024,128]{1,0:T(8,128)(2,1)} %get-tuple-element.719), channel_id=1, source_target_pairs={{0,1},{1,0},{2,3},{3,2},{4,5},{5,4},{6,7},{7,6},{8,9},{9,8},{10,11... | collective-permute-start | bytes 786440 | tf_op jit(solution)/shard_map/ppermute | solution.py:55
  675.4 36.9 %collective-permute-start.100 = (bf16[256,1152]{1,0:T(8,128)(2,1)}, bf16[256,1152]{1,0:T(8,128)(2,1)}, u32[]{:S(2)}, u32[]{:S(2)}) collective-permute-start(bf16[256,1152]{1,0:T(8,128)(2,1)} %get-tuple-element.671), channel_id=1, source_target_pairs={{8,0},{16,8},{24,16},{28,24},{20,28},{12,20},{4,12},{0,4},{9,1},{1... | collective-permute-start | bytes 1769480 | tf_op jit(solution)/shard_map/ppermute | solution.py:76
  676.5 35.8 %collective-permute-start.99 = (bf16[256,1152]{1,0:T(8,128)(2,1)}, bf16[256,1152]{1,0:T(8,128)(2,1)}, u32[]{:S(2)}, u32[]{:S(2)}) collective-permute-start(bf16[256,1152]{1,0:T(8,128)(2,1)} %get-tuple-element.672), channel_id=1, source_target_pairs={{0,8},{8,16},{16,24},{24,28},{28,20},{20,12},{12,4},{4,0},{1,9},{9... | collective-permute-start | bytes 1769480 | tf_op jit(solution)/shard_map/ppermute | solution.py:73
  705.2 25.3 %collective-permute-start.112 = (bf16[128,2048]{1,0:T(8,128)(2,1)}, bf16[128,2048]{1,0:T(8,128)(2,1)S(1)}, u32[]{:S(2)}, u32[]{:S(2)}) collective-permute-start(bf16[128,2048]{1,0:T(8,128)(2,1)} %add_convert_fusion.16), channel_id=1, source_target_pairs={{8,0},{16,8},{24,16},{28,24},{20,28},{12,20},{4,12},{0,4},{9,1},{1... | collective-permute-start | bytes 1572872 | tf_op jit(solution)/shard_map/ppermute | solution.py:76
  715.9 27.2 %collective-permute-start.113 = (bf16[2,64,2048]{2,1,0:T(8,128)(2,1)}, bf16[2,64,2048]{2,1,0:T(8,128)(2,1)}, u32[]{:S(2)}, u32[]{:S(2)}) collective-permute-start(bf16[2,64,2048]{2,1,0:T(8,128)(2,1)} %pad_maximum_fusion.21), channel_id=1, source_target_pairs={{0,2},{1,3},{2,0},{3,1},{4,6},{5,7},{6,4},{7,5},{8,10},{9,11},{10,... | collective-permute-start | bytes 1572872 | tf_op jit(solution)/shard_map/ppermute | solution.py:59
  773.2 26.9 %collective-permute-start.120 = (bf16[2,64,1152]{2,1,0:T(8,128)(2,1)S(1)}, bf16[2,64,1152]{2,1,0:T(8,128)(2,1)S(1)}, u32[]{:S(2)}, u32[]{:S(2)}) collective-permute-start(bf16[2,64,1152]{2,1,0:T(8,128)(2,1)S(1)} %pad_maximum_fusion.25), channel_id=1, source_target_pairs={{0,2},{1,3},{2,0},{3,1},{4,6},{5,7},{6,4},{7,5},{8,10},{9,11},{10,... | collective-permute-start | bytes 884744 | tf_op jit(solution)/shard_map/ppermute | solution.py:59
  773.6 36.0 %collective-permute-start.121 = (bf16[128,2048]{1,0:T(8,128)(2,1)}, bf16[128,2048]{1,0:T(8,128)(2,1)S(1)}, u32[]{:S(2)}, u32[]{:S(2)}) collective-permute-start(bf16[128,2048]{1,0:T(8,128)(2,1)} %add_convert_fusion.15), channel_id=1, source_target_pairs={{0,0},{16,1},{8,2},{24,3},{4,4},{20,5},{12,6},{28,7},{1,8},{17,9},... | collective-permute-start | bytes 1572872 | tf_op jit(solution)/shard_map/ppermute | solution.py:1084
  795.9 46.8 %collective-permute-start.130 = (bf16[256,2048]{1,0:T(8,128)(2,1)S(1)}, bf16[256,2048]{1,0:T(8,128)(2,1)S(1)}, u32[]{:S(2)}, u32[]{:S(2)}) collective-permute-start(bf16[256,2048]{1,0:T(8,128)(2,1)S(1)} %fusion.29), channel_id=1, source_target_pairs={{0,1},{1,0},{2,3},{3,2},{4,5},{5,4},{6,7},{7,6},{8,9},{9,8},{10,11... | collective-permute-start | bytes 3145736 | tf_op jit(solution)/shard_map/ppermute | solution.py:55
  800.1 51.5 %collective-permute-start.127 = (bf16[256,2048]{1,0:T(8,128)(2,1)}, bf16[256,2048]{1,0:T(8,128)(2,1)}, u32[]{:S(2)}, u32[]{:S(2)}) collective-permute-start(bf16[256,2048]{1,0:T(8,128)(2,1)} %fusion.12), channel_id=1, source_target_pairs={{0,2},{1,3},{2,0},{3,1},{4,6},{5,7},{6,4},{7,5},{8,10},{9,11},{10,... | collective-permute-start | bytes 3145736 | tf_op jit(solution)/shard_map/ppermute | solution.py:59
  814.2 28.5 %collective-permute-start.128 = (bf16[256,1024]{1,0:T(8,128)(2,1)}, bf16[256,1024]{1,0:T(8,128)(2,1)}, u32[]{:S(2)}, u32[]{:S(2)}) collective-permute-start(bf16[256,1024]{1,0:T(8,128)(2,1)} %get-tuple-element.685), channel_id=1, source_target_pairs={{0,8},{8,16},{16,24},{24,28},{28,20},{20,12},{12,4},{4,0},{1,9},{9... | collective-permute-start | bytes 1572872 | tf_op jit(solution)/shard_map/ppermute | solution.py:73
  (237 other events, 3270.8 us)
